TPU v7x, 128 devices: a whole 4x4x4 slice. The times are simulated.
128 devices in a mesh: row: 16 (over y_hi, z, core), col: 8 (over x, y_lo).
Axes of the slice: x: 4, y: 4 (y_hi: 2, y_lo: 2; y = y_hi * 2 + y_lo), z: 4, core: 2. Of those that a mesh axis runs over, the one named last changes fastest.
Arguments:
- amplitudes: float32 [16, 16, 160, 160], P('row', 'col'), may hold values from -8 to 8, as said below
- vvvv: float32 [160, 160, 160, 160], P('row', None, 'col'), may hold values from -0.0390625 to 0.0390625
- hole_ints: float32 [16, 16, 16, 16], replicated, may hold values from -0.375 to 0.375
- exchange_ints: float32 [16, 16, 160, 160], P('row', None, 'col'), may hold values from -0.0024414062 to 0.0024414062
- fock_occ: float32 [16, 16], replicated, may hold values from -1.5 to 1.5
- fock_vir: float32 [160, 160], replicated, may hold values from -0.5 to 0.5
- eps_occ: float32 [16], replicated, may hold values from -2 to -0.5
- eps_vir: float32 [160], replicated, may hold values from 0.3 to 3
Outputs:
- update: float32 [16, 16, 160, 160], P('row', 'col')
Inputs may be any that keep to these rules, and one draw needn't show every extreme that they name: amplitudes[i, j, a, b] equals amplitudes[j, i, b, a].
All inputs are finite; a program needn't handle non-finite values.
Results may differ from a plain program's by a relative error of at most 0.000064.
Values sent between devices are 32-bit elements; how exact they have to be, the bound alone decides.
No kernel may reach another device: no remote copies, remote signals or barrier semaphores. Data moves between devices by JAX's collectives and lax.ppermute only.
A program may use at most 128 MiB of HBM per device.

v0:
```python
import functools

import jax
import jax.numpy as jnp
from jax import lax
from jax.experimental import pallas as pl
from jax.experimental.pallas import tpu as pltpu
from jax.sharding import PartitionSpec as P

NO = 16
NV = 160
ROWS = 16
COLS = 8
AB = NV // ROWS
CB = NV // COLS
KT = 25
VROWS = AB * NV
EROWS = AB * 4
MROWS = VROWS + NO + EROWS
NT = (((1,), (1,)), ((), ()))


def row_perm(dy, dz, dc):
    def source(r):
        return ((r // 8 + dy) % 2) * 8 + ((r // 2 + dz) % 4) * 2 + ((r % 2) ^ dc)

    return [(source(r), r) for r in range(ROWS)]


def pack_kernel(t_ref, o_ref, tail):
    tail[:, :, 0:32] = t_ref[:, :, 128:NV]
    for c in range(COLS):
        for j in range(2):
            o_ref[c, j, 0:CB, :] = t_ref[j, c * CB : (c + 1) * CB, 0:128]
            tails = [
                tail[j, pl.ds(c * CB + cc, CB // 4, stride=4), :][:, 0:32] for cc in range(4)
            ]
            o_ref[c, j, CB:KT, :] = jnp.concatenate(tails, axis=1)


def pack(t):
    return pl.pallas_call(
        pack_kernel,
        out_shape=jax.ShapeDtypeStruct((COLS, 2, KT, 128), jnp.float32),
        scratch_shapes=[pltpu.VMEM((2, NV, 128), jnp.float32)],
        cost_estimate=pl.CostEstimate(flops=0, bytes_accessed=600000, transcendentals=0),
    )(t)


def split(x):
    hi = x.astype(jnp.bfloat16)
    lo = (x - hi.astype(jnp.float32)).astype(jnp.bfloat16)
    return hi, lo


def ladder_kernel(
    tbl_ref, s_ref, q_ref, v_ref, k_ref, e_ref, l_ref, chi_ref, p_ref, hi, lo, ghi, glo, acc, pacc
):
    step = pl.program_id(0)
    for rel in range(ROWS):
        ref = s_ref if rel < 8 else q_ref
        start = pl.multiple_of(tbl_ref[rel] * NO, NO)
        for kt in range(5):
            index = step * 4 + kt if kt < 4 else CB + step
            ph, plo = split(ref[rel % 8, index])
            ghi[pl.ds(start, NO), kt * 128 : (kt + 1) * 128] = ph
            glo[pl.ds(start, NO), kt * 128 : (kt + 1) * 128] = plo
    for a in range(AB + 1):
        rows = NV if a < AB else NO
        base = a * NV

        def get(cc, lanes, a=a):
            return v_ref[a, cc, :, lanes] if a < AB else k_ref[cc, :, lanes]

        for kt in range(5):
            if kt < 4:
                x = get(kt, slice(0, 128))
            else:
                x = jnp.concatenate([get(cc, slice(128, NV)) for cc in range(4)], axis=1)
            xh, xl = split(x)
            hi[base : base + rows, kt * 128 : (kt + 1) * 128] = xh
            lo[base : base + rows, kt * 128 : (kt + 1) * 128] = xl

    dot = functools.partial(
        lax.dot_general, dimension_numbers=NT, preferred_element_type=jnp.float32
    )
    part = dot(hi[...], ghi[...]) + dot(hi[...], glo[...]) + dot(lo[...], ghi[...])

    @pl.when(step == 0)
    def _():
        acc[...] = part

    @pl.when(step > 0)
    def _():
        acc[...] += part

    pacc[step] = dot(e_ref[...], ghi[...]) + dot(e_ref[...], glo[...])

    @pl.when(step == pl.num_programs(0) - 1)
    def _():
        for a in range(AB):
            for c in range(COLS):
                first = a * NV + c * CB
                l_ref[c, a * CB : (a + 1) * CB, :] = acc[first : first + CB, :]
            for g in range(5):
                p_ref[a * CB + g * 4 : a * CB + g * 4 + 4, :] = pacc[g, a * 4 : a * 4 + 4, :]
        chi_ref[...] = acc[VROWS : VROWS + NO, :]


def ladder(tbl, s, q, v, k, e):
    whole = lambda shape: pl.BlockSpec(shape, lambda g, t: (0,) * len(shape))
    return pl.pallas_call(
        ladder_kernel,
        out_shape=(
            jax.ShapeDtypeStruct((COLS, AB * CB, NO * NO), jnp.float32),
            jax.ShapeDtypeStruct((NO, NO * NO), jnp.float32),
            jax.ShapeDtypeStruct((AB * CB, NO * NO), jnp.float32),
        ),
        grid_spec=pltpu.PrefetchScalarGridSpec(
            num_scalar_prefetch=1,
            grid=(5,),
            in_specs=[
                whole((8, KT, NO, 128)),
                whole((8, KT, NO, 128)),
                pl.BlockSpec((AB, 4, NV, NV), lambda g, t: (0, g, 0, 0)),
                pl.BlockSpec((4, NO, NV), lambda g, t: (g, 0, 0)),
                whole((EROWS, 640)),
            ],
            out_specs=(
                whole((COLS, AB * CB, NO * NO)),
                whole((NO, NO * NO)),
                whole((AB * CB, NO * NO)),
            ),
            scratch_shapes=[
                pltpu.VMEM((VROWS + NO, 640), jnp.bfloat16),
                pltpu.VMEM((VROWS + NO, 640), jnp.bfloat16),
                pltpu.VMEM((NO * NO, 640), jnp.bfloat16),
                pltpu.VMEM((NO * NO, 640), jnp.bfloat16),
                pltpu.VMEM((VROWS + NO, NO * NO), jnp.float32),
                pltpu.VMEM((5, EROWS, NO * NO), jnp.float32),
            ],
        ),
        compiler_params=pltpu.CompilerParams(vmem_limit_bytes=48 << 20),
        cost_estimate=pl.CostEstimate(
            flops=3 * 2 * 1680 * 3200 * 256, bytes_accessed=38 << 20, transcendentals=0
        ),
    )(tbl, s, q, v, k, e)


def final_kernel(e_ref, x_ref, tf_ref, vrow_ref, vcol_ref, o_ref, left, right):
    for o in range(2):
        for s in range(2):
            for a in range(AB):
                pieces = [x_ref[o, s, c, :, a * CB : (a + 1) * CB] for c in range(COLS)]
                line = jnp.concatenate(pieces, axis=1)
                left[o, s, pl.ds(a, ROWS, stride=AB), :] = line[:, 0:128]
                right[o, s, pl.ds(a, ROWS, stride=AB), 0:32] = line[:, 128:NV]
    for s in range(2):
        full = [
            jnp.concatenate([left[o, s], right[o, s, :, 0:32]], axis=1) for o in range(2)
        ]
        total = full[0] + full[1].T + tf_ref[s]
        den = (e_ref[s] - vcol_ref[...]) - vrow_ref[...]
        o_ref[s] = total / den


def finish(e, x, tf, eps_vir):
    return pl.pallas_call(
        final_kernel,
        out_shape=jax.ShapeDtypeStruct((2, NV, NV), jnp.float32),
        in_specs=[pl.BlockSpec(memory_space=pltpu.SMEM)]
        + [pl.BlockSpec(memory_space=pltpu.VMEM)] * 4,
        out_specs=pl.BlockSpec(memory_space=pltpu.VMEM),
        scratch_shapes=[pltpu.VMEM((2, 2, NV, 128), jnp.float32)] * 2,
        cost_estimate=pl.CostEstimate(flops=0, bytes_accessed=2 << 20, transcendentals=0),
    )(e, x, tf, eps_vir.reshape(1, NV), eps_vir.reshape(NV, 1))


def on_device(amplitudes, vvvv, hole_ints, exchange_ints, fock_occ, fock_vir, eps_occ, eps_vir):
    high = lax.Precision.HIGHEST
    row = lax.axis_index("row")
    col = lax.axis_index("col")
    t = amplitudes[0]
    packed = pack(t)
    arrived = lax.all_to_all(packed, "col", split_axis=0, concat_axis=0, tiled=True)
    x = arrived.reshape(NO, KT, 128).transpose(1, 0, 2)

    pair = jnp.stack([x, lax.ppermute(x, "row", row_perm(1, 0, 0))])
    rings = [pair] + [lax.ppermute(pair, "row", row_perm(0, dz, 0)) for dz in (1, 2, 3)]
    own = jnp.stack(rings)
    other = lax.ppermute(own, "row", row_perm(0, 0, 1))
    own = own.reshape(8, KT, NO, 128)
    other = other.reshape(8, KT, NO, 128)

    rel = jnp.arange(ROWS, dtype=jnp.int32)
    dc, dz, dy = rel // 8, (rel // 2) % 4, rel % 2
    table = ((row // 8 + dy) % 2) * 8 + ((row // 2 + dz) % 4) * 2 + ((row % 2) ^ dc)

    e_row = jnp.arange(EROWS, dtype=jnp.int32)[:, None]
    e_col = jnp.arange(640, dtype=jnp.int32)[None, :]
    want = row * AB + e_row // 4
    cc = e_row % 4
    place = jnp.where(want < 128, cc * 128 + want, 512 + cc * 32 + want - 128)
    onehot = (e_col == place).astype(jnp.bfloat16)

    lad, chi_part, block = ladder(
        table,
        own,
        other,
        vvvv.transpose(0, 2, 1, 3),
        exchange_ints[0].transpose(1, 0, 2),
        onehot,
    )
    scattered = lax.all_to_all(lad, "col", split_axis=0, concat_axis=0, tiled=True)
    summed = jnp.sum(scattered, axis=0)

    chi_cols = jnp.sum(lax.all_gather(chi_part, "col", axis=0), axis=0)
    chi_rows = lax.all_gather(chi_cols, "row", axis=0)
    eye = jnp.eye(NO, dtype=jnp.float32)
    fixed = hole_ints - eye[:, None, :, None] * fock_occ[None, :, None, :]
    chi = fixed + chi_rows.reshape(NO, NO, NO, NO)
    chi = chi.transpose(1, 0, 2, 3).reshape(NO * NO, NO * NO)
    raw = summed + jnp.dot(block, chi, precision=high)
    raw = jnp.pad(raw.T, ((0, 0), (0, 256 - AB * CB))).reshape(NO, NO, 256)
    sending = jnp.stack([raw, raw.transpose(1, 0, 2)])
    sending = sending.reshape(2, NO, COLS, 2, 256).transpose(1, 2, 0, 3, 4)
    sending = sending.reshape(ROWS * COLS, 4, 256)
    back = lax.all_to_all(sending, ("row", "col"), split_axis=0, concat_axis=0, tiled=True)
    back = back.reshape(ROWS, COLS, 2, 2, 256).transpose(2, 3, 1, 0, 4)

    tf = jnp.einsum("jac,cb->jab", t, fock_vir, precision=high)
    tf = tf + jnp.einsum("ac,jcb->jab", fock_vir, t, precision=high)
    first = lax.dynamic_slice_in_dim(eps_occ, row, 1)
    second = lax.dynamic_slice_in_dim(eps_occ, col * 2, 2)
    return finish(first + second, back, tf, eps_vir)[None]


def solution(mesh):
    in_specs = (
        P("row", "col", None, None),
        P("row", None, "col", None),
        P(),
        P("row", None, "col", None),
        P(),
        P(),
        P(),
        P(),
    )
    return jax.shard_map(
        on_device,
        mesh=mesh,
        in_specs=in_specs,
        out_specs=P("row", "col", None, None),
        check_vma=False,
    )
```

profile of v0, /device:TPU:0, one launch (start us, length us, event | category | flops | bytes accessed | tf_op | source)
XLA Modules:
  0.0 174.2 jit_solution(4370841607111515386)
XLA Ops:
  0.0 1.8 %shard_map.82 = f32[8,2,25,128]{3,2,1,0:T(8,128)} custom-call(f32[2,160,160]{2,1,0:T(8,128)} %bitcast.60), custom_call_target="tpu_custom_call" | custom-call | bytes 600000 | tf_op jit(solution)/shard_map/pallas_call | solution.py:42
  1.8 1.1 copy.35
  3.0 11.9 %all_to_all.15 = f32[8,2,25,128]{3,1,2,0:T(2,128)S(1)} all-to-all(f32[8,2,25,128]{3,1,2,0:T(2,128)S(1)} %copy.35), channel_id=1, replica_groups=mesh['row'=16,'col'=8] {'col'}, dimensions={0} | all-to-all | bytes 409600 | tf_op jit(solution)/shard_map/all_to_all | solution.py:185
  14.8 0.1 copy.36
  14.9 3.0 %collective-permute-start = (f32[25,16,128]{2,1,0:T(8,128)S(1)}, f32[25,16,128]{2,1,0:T(8,128)S(1)}, u32[]{:S(2)}, u32[]{:S(2)}) collective-permute-start(f32[25,16,128]{2,1,0:T(8,128)S(1)} %bitcast.65), channel_id=1, source_target_pairs={{64,0},{72,8},{80,16},{88,24},{96,32},{104,40},{112,48},{120,56},{... | collective-permute-start | bytes 614408 | tf_op jit(solution)/shard_map/ppermute | solution.py:188
  17.9 4.4 %collective-permute-done = f32[25,16,128]{2,1,0:T(8,128)S(1)} collective-permute-done((f32[25,16,128]{2,1,0:T(8,128)S(1)}, f32[25,16,128]{2,1,0:T(8,128)S(1)}, u32[]{:S(2)}, u32[]{:S(2)}) %collective-permute-start) | collective-permute-done | bytes 204832 | tf_op jit(solution)/shard_map/ppermute | solution.py:188
  22.3 0.1 fusion.19
  22.3 4.0 %collective-permute-start.2 = (f32[2,25,16,128]{3,2,1,0:T(8,128)S(1)}, f32[2,25,16,128]{3,2,1,0:T(8,128)S(1)}, u32[]{:S(2)}, u32[]{:S(2)}) collective-permute-start(f32[2,25,16,128]{3,2,1,0:T(8,128)S(1)} %get-tuple-element.12), channel_id=1, source_target_pairs={{32,0},{40,8},{48,16},{56,24},{0,32},{8,40},{16,48},{24,56},{96,64... | collective-permute-start | bytes 1228808 | tf_op jit(solution)/shard_map/ppermute | solution.py:189
  26.3 0.7 collective-permute-start.1
  27.0 1.3 collective-permute-start.3
  28.3 8.4 %collective-permute-done.2 = f32[2,25,16,128]{3,2,1,0:T(8,128)S(1)} collective-permute-done((f32[2,25,16,128]{3,2,1,0:T(8,128)S(1)}, f32[2,25,16,128]{3,2,1,0:T(8,128)S(1)}, u32[]{:S(2)}, u32[]{:S(2)}) %collective-permute-start.2) | collective-permute-done | bytes 409632 | tf_op jit(solution)/shard_map/ppermute | solution.py:189
  36.7 6.1 %collective-permute-done.1 = f32[2,25,16,128]{3,2,1,0:T(8,128)S(1)} collective-permute-done((f32[2,25,16,128]{3,2,1,0:T(8,128)S(1)}, f32[2,25,16,128]{3,2,1,0:T(8,128)S(1)}, u32[]{:S(2)}, u32[]{:S(2)}) %collective-permute-start.1) | collective-permute-done | bytes 409632 | tf_op jit(solution)/shard_map/ppermute | solution.py:189
  42.8 0.0 collective-permute-done.3
  42.8 0.1 pad_maximum_fusion
  42.9 0.1 collective-permute-start.4
  43.1 0.1 fusion.4.e_ref
  43.2 3.3 %collective-permute-done.4 = f32[4,2,25,16,128]{4,3,2,1,0:T(8,128)S(1)} collective-permute-done((f32[4,2,25,16,128]{4,3,2,1,0:T(8,128)S(1)}, f32[4,2,25,16,128]{4,3,2,1,0:T(8,128)S(1)}, u32[]{:S(2)}, u32[]{:S(2)}) %collective-permute-start.4) | collective-permute-done | bytes 1638432 | tf_op jit(solution)/shard_map/ppermute | solution.py:191
  46.5 1.0 copy-done.1
  47.5 21.6 %shard_map.83 = (f32[8,200,256]{2,1,0:T(8,128)}, f32[16,256]{1,0:T(8,128)S(1)}, f32[200,256]{1,0:T(8,128)S(1)}) custom-call(s32[16]{0:T(128)S(1)} %fusion.7.tbl_ref, f32[8,25,16,128]{3,2,1,0:T(8,128)S(1)} %bitcast.56, f32[8,25,16,128]{3,2,1,0:T(8,128)S(1)} %bitcast.57, f32[10,20,160,160]{3,2,1,0:T(8,128)} %bitcast.59, f32[20,16,160]{2,1,0:T(8,128)S(1)} %bitcast.58, ...), custom_call_target="tpu_custom_call" | custom-call | flops 8257536000 | bytes 39845888 | tf_op jit(solution)/shard_map/pallas_call | solution.py:112
  69.1 0.7 copy-done.2
  69.7 4.4 %all-to-all-start.1 = ((f32[8,200,256]{2,1,0:T(8,128)}), f32[8,200,256]{2,1,0:T(8,128)}, u32[]{:S(2)}, u32[]{:S(2)}) async-start(f32[8,200,256]{2,1,0:T(8,128)} %get-tuple-element.8), calls=%async_computation.1 | async-start | bytes 3276800 | tf_op jit(solution)/shard_map/all_to_all | solution.py:214
  74.2 0.0 copy-start.5
  74.2 0.7 dynamic_slice.6
  74.9 45.0 %all-gather = f32[128,256]{1,0:T(8,128)S(1)} all-gather(f32[16,256]{1,0:T(8,128)S(1)} %get-tuple-element.9), channel_id=2, replica_groups=mesh['row'=16,'col'=8] {'col'}, dimensions={0}, use_global_device_ids=true | all-gather | bytes 147456 | tf_op jit(solution)/shard_map/all_gather | solution.py:217
  119.9 24.6 %all-gather.1 = f32[256,256]{1,0:T(8,128)S(1)} all-gather(f32[16,256]{1,0:T(8,128)S(1)} %reduce_sum.22), channel_id=3, replica_groups=mesh['row'=16,'col'=8] {'row'}, dimensions={0}, use_global_device_ids=true | all-gather | bytes 278528 | tf_op jit(solution)/shard_map/all_gather | solution.py:218
  144.4 0.6 reshape.116
  145.1 1.9 %add_bitcast_fusion = f32[16,16,16,16]{3,2,0,1:T(8,128)S(1)} fusion(f32[16,16,16,16]{3,2,1,0:T(8,128)S(1)} %reshape.116, f32[16,16,16,16]{3,2,1,0:T(8,128)} %param.10, f32[16,16]{1,0:T(8,128)S(1)} %copy-done.5, f32[16,16]{1,0:T(8,128)S(1)} %fusion.5), kind=kLoop, calls=%fused_computation | loop fusion | flops 196608 | bytes 788480 | tf_op jit(solution)/shard_map/transpose | solution.py:222
  147.0 0.2 copy.37
  147.3 0.0 copy-start.3
  147.3 0.9 reshape.117
  148.2 1.6 reduce_sum.20
  149.8 0.3 convolution_add_fusion
  150.1 0.1 copy.51
  150.3 0.1 stack.40
  150.5 0.2 copy.50
  150.7 0.0 copy-start.6
  150.7 0.0 copy-start.4
  150.7 0.2 maximum_bitcast_fusion
  151.0 1.1 copy.42
  152.1 4.6 %all-to-all-start.2 = ((f32[128,4,256]{2,1,0:T(4,128)}), f32[128,4,256]{2,1,0:T(4,128)S(1)}, u32[]{:S(2)}, u32[]{:S(2)}) async-start(f32[128,4,256]{2,1,0:T(4,128)} %copy.42), calls=%async_computation.2 | async-start | bytes 1048576 | tf_op jit(solution)/shard_map/all_to_all | solution.py:228
  156.7 1.2 dynamic-slice_add_fusion.e_ref
  158.0 0.7 copy.47.vcol_ref
  158.7 0.4 fusion.2
  159.2 1.2 fusion.tf_ref
  160.3 9.9 %all-to-all-done.2 = f32[128,4,256]{2,1,0:T(4,128)S(1)} async-done(((f32[128,4,256]{2,1,0:T(4,128)}), f32[128,4,256]{2,1,0:T(4,128)S(1)}, u32[]{:S(2)}, u32[]{:S(2)}) %all-to-all-start.2) | async-done | bytes 524320 | tf_op jit(solution)/shard_map/all_to_all | solution.py:228
  170.3 0.1 copy.43
  170.4 1.0 copy.53
  171.3 2.9 %shard_map.84 = f32[2,160,160]{2,1,0:T(8,128)} custom-call(f32[2]{0:T(128)} %dynamic-slice_add_fusion.e_ref, f32[2,2,8,16,256]{4,3,2,1,0:T(8,128)} %bitcast.64, f32[2,160,160]{2,1,0:T(8,128)} %fusion.tf_ref, f32[1,160]{1,0:T(1,128)} %bitcast.72, f32[160,1]{1,0:T(8,128)} %copy.47.vcol_ref), custom_call_target="tpu_custom_call" | custom-call | bytes 2097152 | tf_op jit(solution)/shard_map/pallas_call | solution.py:168
  (17 shorter events, 0.1 us)
Async XLA Ops:
  0.0 158.7 %copy-start = (f32[160,160]{1,0:T(8,128)S(1)}, f32[160,160]{1,0:T(8,128)}, u32[]{:S(2)}) copy-start(f32[160,160]{1,0:T(8,128)} %param.13) | copy-start | bytes 307204
  14.9 7.3 %collective-permute-start = (f32[25,16,128]{2,1,0:T(8,128)S(1)}, f32[25,16,128]{2,1,0:T(8,128)S(1)}, u32[]{:S(2)}, u32[]{:S(2)}) collective-permute-start(f32[25,16,128]{2,1,0:T(8,128)S(1)} %bitcast.65), channel_id=1, source_target_pairs={{64,0},{72,8},{80,16},{88,24},{96,32},{104,40},{112,48},{120,56},{... | collective-permute-start | bytes 614408 | tf_op jit(solution)/shard_map/ppermute | solution.py:188
  22.3 14.4 %collective-permute-start.2 = (f32[2,25,16,128]{3,2,1,0:T(8,128)S(1)}, f32[2,25,16,128]{3,2,1,0:T(8,128)S(1)}, u32[]{:S(2)}, u32[]{:S(2)}) collective-permute-start(f32[2,25,16,128]{3,2,1,0:T(8,128)S(1)} %get-tuple-element.12), channel_id=1, source_target_pairs={{32,0},{40,8},{48,16},{56,24},{0,32},{8,40},{16,48},{24,56},{96,64... | collective-permute-start | bytes 1228808 | tf_op jit(solution)/shard_map/ppermute | solution.py:189
  26.3 16.5 %collective-permute-start.1 = (f32[2,25,16,128]{3,2,1,0:T(8,128)S(1)}, f32[2,25,16,128]{3,2,1,0:T(8,128)S(1)}, u32[]{:S(2)}, u32[]{:S(2)}) collective-permute-start(f32[2,25,16,128]{3,2,1,0:T(8,128)S(1)} %get-tuple-element.12), channel_id=1, source_target_pairs={{16,0},{24,8},{32,16},{40,24},{48,32},{56,40},{0,48},{8,56},{80,64... | collective-permute-start | bytes 1228808 | tf_op jit(solution)/shard_map/ppermute | solution.py:189
  27.0 15.8 %collective-permute-start.3 = (f32[2,25,16,128]{3,2,1,0:T(8,128)S(1)}, f32[2,25,16,128]{3,2,1,0:T(8,128)S(1)}, u32[]{:S(2)}, u32[]{:S(2)}) collective-permute-start(f32[2,25,16,128]{3,2,1,0:T(8,128)S(1)} %get-tuple-element.12), channel_id=1, source_target_pairs={{48,0},{56,8},{0,16},{8,24},{16,32},{24,40},{32,48},{40,56},{112,6... | collective-permute-start | bytes 1228808 | tf_op jit(solution)/shard_map/ppermute | solution.py:189
  42.9 3.6 %collective-permute-start.4 = (f32[4,2,25,16,128]{4,3,2,1,0:T(8,128)S(1)}, f32[4,2,25,16,128]{4,3,2,1,0:T(8,128)S(1)}, u32[]{:S(2)}, u32[]{:S(2)}) collective-permute-start(f32[4,2,25,16,128]{4,3,2,1,0:T(8,128)S(1)} %pad_maximum_fusion), channel_id=1, source_target_pairs={{8,0},{0,8},{24,16},{16,24},{40,32},{32,40},{56,48},{48,56},{72,64... | collective-permute-start | bytes 4915208 | tf_op jit(solution)/shard_map/ppermute | solution.py:191
  46.5 1.0 copy-start.1
  69.1 0.7 copy-start.2
  69.7 4.5 %copy-start.7 = (f32[16]{0:T(128)S(1)}, f32[16]{0:T(128)}, u32[]{:S(2)}) copy-start(f32[16]{0:T(128)} %param.14) | copy-start | bytes 196
  69.7 78.5 %all-to-all-start.1 = ((f32[8,200,256]{2,1,0:T(8,128)}), f32[8,200,256]{2,1,0:T(8,128)}, u32[]{:S(2)}, u32[]{:S(2)}) async-start(f32[8,200,256]{2,1,0:T(8,128)} %get-tuple-element.8), calls=%async_computation.1 | async-start | bytes 3276800 | tf_op jit(solution)/shard_map/all_to_all | solution.py:214
  74.2 70.9 %copy-start.5 = (f32[16,16]{1,0:T(8,128)S(1)}, f32[16,16]{1,0:T(8,128)}, u32[]{:S(2)}) copy-start(f32[16,16]{1,0:T(8,128)} %param.12) | copy-start | bytes 3076
  147.3 2.5 %copy-start.3 = (f32[200,256]{1,0:T(8,128)S(1)}, f32[200,256]{1,0:T(8,128)}, u32[]{:S(2)}) copy-start(f32[200,256]{1,0:T(8,128)} %copy-done.2) | copy-start | bytes 614404
  150.7 7.3 %copy-start.6 = (f32[160]{0:T(256)S(1)}, f32[160]{0:T(256)}, u32[]{:S(2)}) copy-start(f32[160]{0:T(256)} %param.15) | copy-start | bytes 1924
  150.7 8.1 %copy-start.4 = (f32[1,2,160,160]{3,2,1,0:T(8,128)S(1)}, f32[1,2,160,160]{3,2,1,0:T(8,128)}, u32[]{:S(2)}) copy-start(f32[1,2,160,160]{3,2,1,0:T(8,128)} %param.8) | copy-start | bytes 614404
  152.1 18.1 %all-to-all-start.2 = ((f32[128,4,256]{2,1,0:T(4,128)}), f32[128,4,256]{2,1,0:T(4,128)S(1)}, u32[]{:S(2)}, u32[]{:S(2)}) async-start(f32[128,4,256]{2,1,0:T(4,128)} %copy.42), calls=%async_computation.2 | async-start | bytes 1048576 | tf_op jit(solution)/shard_map/all_to_all | solution.py:228
where the time goes:
time: 175 us; the launch traced here: 174 us
  blocking collectives  81.4 us (47%)
  waiting for transfers between devices  32.1 us (18%)
  Pallas kernels  26.3 us (15%)
  starting transfers between devices  18.1 us (10%)
  local copies, waits for them, and re-layouts  8.78 us (5%)
  other arithmetic  5.29 us (3%)
  matrix products  1.95 us (1%)
    all_gather x1, blocking collectives, on_device(): chi_cols = jnp.sum(lax.all_gather(chi_part, 'col', axis=0), axis=0)  45 us
    all_gather x1, blocking collectives, on_device(): chi_rows = lax.all_gather(chi_cols, 'row', axis=0)  24.6 us
    pallas_call x1, Pallas kernels, ladder(): pl.pallas_call(ladder_kernel, out_shape=(jax.ShapeDtypeStruct((COLS, AB *...  21.6 us
    ppermute x3, waiting for transfers between devices, on_device(): lax.ppermute(pair, 'row', row_perm(0, dz, 0))  14.5 us
    all_to_all x1, blocking collectives, on_device(): lax.all_to_all(packed, 'col', split_axis=0, concat_axis=0, tiled=True)  11.9 us
    all_to_all x1, waiting for transfers between devices, on_device(): lax.all_to_all(sending, ('row', 'col'), split_axis=0, concat_axis=0, tile...  9.91 us
    ppermute x3, starting transfers between devices, on_device(): lax.ppermute(pair, 'row', row_perm(0, dz, 0))  5.98 us
    all_to_all x1, starting transfers between devices, on_device(): lax.all_to_all(sending, ('row', 'col'), split_axis=0, concat_axis=0, tile...  4.61 us
  transfers between devices with their start and end apart: 7, of which 5 were waited for; matrix products, arithmetic and copies ran while one was open for 5% of the time, Pallas kernels for 0%

commit v1 on v0

v1 whole, which is shorter than its diff:
```python
import functools

import jax
import jax.numpy as jnp
from jax import lax
from jax.experimental import pallas as pl
from jax.experimental.pallas import tpu as pltpu
from jax.sharding import PartitionSpec as P

NO = 16
NV = 160
ROWS = 16
COLS = 8
AB = NV // ROWS
CB = NV // COLS
KT = 25
VROWS = AB * NV
EROWS = AB * 4
HALF = VROWS // 2
NT = (((1,), (1,)), ((), ()))
VMEM = pl.BlockSpec(memory_space=pltpu.VMEM)


def row_perm(dy, dz, dc):
    def source(r):
        return ((r // 8 + dy) % 2) * 8 + ((r // 2 + dz) % 4) * 2 + ((r % 2) ^ dc)

    return [(source(r), r) for r in range(ROWS)]


def pack_kernel(t_ref, o_ref, tail):
    tail[:, :, 0:32] = t_ref[:, :, 128:NV]
    for c in range(COLS):
        for j in range(2):
            o_ref[c, j, 0:CB, :] = t_ref[j, c * CB : (c + 1) * CB, 0:128]
            tails = [
                tail[j, pl.ds(c * CB + cc, CB // 4, stride=4), :][:, 0:32] for cc in range(4)
            ]
            o_ref[c, j, CB:KT, :] = jnp.concatenate(tails, axis=1)


def pack(t):
    return pl.pallas_call(
        pack_kernel,
        out_shape=jax.ShapeDtypeStruct((COLS, 2, KT, 128), jnp.float32),
        scratch_shapes=[pltpu.VMEM((2, NV, 128), jnp.float32)],
        cost_estimate=pl.CostEstimate(flops=0, bytes_accessed=600000, transcendentals=0),
    )(t)


def split(x):
    hi = x.astype(jnp.bfloat16)
    lo = (x - hi.astype(jnp.float32)).astype(jnp.bfloat16)
    return hi, lo


def prepare_kernel(tbl_ref, s_ref, q_ref, k_ref, ghi, glo, chi_ref):
    for rel in range(ROWS):
        ref = s_ref if rel < 8 else q_ref
        start = pl.multiple_of(tbl_ref[rel] * NO, NO)
        for kt in range(KT):
            g, place = (kt // 4, kt % 4) if kt < CB else (kt - CB, 4)
            hi, lo = split(ref[rel % 8, kt])
            ghi[g, pl.ds(start, NO), place * 128 : (place + 1) * 128] = hi
            ghi[g, pl.ds(start, NO), 640 + place * 128 : 640 + (place + 1) * 128] = hi
            glo[g, pl.ds(start, NO), place * 128 : (place + 1) * 128] = lo
    chi = jnp.zeros((NO * NO, NO), jnp.float32)
    for g in range(5):
        parts = [k_ref[g * 4 + cc, :, 0:128] for cc in range(4)]
        parts.append(
            jnp.concatenate([k_ref[g * 4 + cc, :, 128:NV] for cc in range(4)], axis=1)
        )
        hi, lo = split(jnp.concatenate(parts, axis=1))
        chi = chi + dot_nt(ghi[g, :, 0:640], hi) + dot_nt(ghi[g, :, 0:640], lo)
        chi = chi + dot_nt(glo[g], hi)
    chi_ref[...] = chi.T


def dot_nt(x, y):
    return lax.dot_general(x, y, NT, preferred_element_type=jnp.float32)


def prepare(tbl, s, q, k):
    return pl.pallas_call(
        prepare_kernel,
        out_shape=(
            pltpu.VMEM((5, NO * NO, 1280), jnp.bfloat16),
            pltpu.VMEM((5, NO * NO, 640), jnp.bfloat16),
            jax.ShapeDtypeStruct((NO, NO * NO), jnp.float32),
        ),
        in_specs=[pl.BlockSpec(memory_space=pltpu.SMEM)] + [VMEM] * 3,
        out_specs=(VMEM, VMEM, VMEM),
        compiler_params=pltpu.CompilerParams(vmem_limit_bytes=7 << 20),
        cost_estimate=pl.CostEstimate(flops=0, bytes_accessed=8 << 20, transcendentals=0),
    )(tbl, s, q, k)


def ladder_kernel(groups, ghi, glo, v_hbm, *refs):
    first, last = groups[0] == 0, groups[-1] == 4
    refs = list(refs)
    before = None if first else refs.pop(0)
    e_ref = refs.pop(0) if last else None
    out = refs.pop(0)
    p_ref = refs.pop(0) if last else None
    buf, hi, lo, sem = refs
    blocks = [(g, half) for g in groups for half in range(2)]
    copies = []
    for n, (g, half) in enumerate(blocks):
        source = v_hbm.at[pl.ds(half * (AB // 2), AB // 2), pl.ds(g * 4, 4)]
        copies.append(pltpu.make_async_copy(source, buf.at[n], sem.at[n]))
        copies[-1].start()
    if last:
        for g in range(5):
            block = dot_nt(e_ref[...], ghi[g, :, 0:640]) + dot_nt(e_ref[...], glo[g])
            for a in range(AB):
                row = a * CB + g * 4
                p_ref[row : row + 4, :] = block[a * 4 : a * 4 + 4, :]

    def convert(n):
        copies[n].wait()
        for a in range(AB // 2):
            rows = slice(a * NV, (a + 1) * NV)
            for kt in range(5):
                if kt < 4:
                    x = buf[n, a, kt, :, 0:128]
                else:
                    tails = [buf[n, a, cc, :, 128:NV] for cc in range(4)]
                    x = jnp.concatenate(tails, axis=1)
                xh, xl = split(x)
                hi[n, rows, kt * 128 : (kt + 1) * 128] = xh
                lo[n, rows, kt * 128 : (kt + 1) * 128] = xl

    totals = [None, None]
    if not first:
        totals = [before[0:HALF, :], before[HALF:VROWS, :]]
    for n, (g, half) in enumerate(blocks):
        convert(n)
        part = dot_nt(hi[n], ghi[g, :, 0:640]) + dot_nt(hi[n], glo[g])
        part = part + dot_nt(lo[n], ghi[g, :, 0:640])
        totals[half] = part if totals[half] is None else totals[half] + part
    for half in range(2):
        total = totals[half]
        if not last:
            out[half * HALF : (half + 1) * HALF, :] = total
            continue
        for a in range(AB // 2):
            row = (half * (AB // 2) + a) * CB
            for c in range(COLS):
                start = a * NV + c * CB
                out[c, row : row + CB, :] = total[start : start + CB, :]


def ladder(ghi, glo, v, groups, before=None, onehot=None):
    operands = [ghi, glo, v]
    in_specs = [VMEM, VMEM, pl.BlockSpec(memory_space=pltpu.HBM)]
    for extra in (before, onehot):
        if extra is not None:
            operands.append(extra)
            in_specs.append(VMEM)
    if onehot is not None:
        out_shape = (
            jax.ShapeDtypeStruct((COLS, AB * CB, NO * NO), jnp.float32),
            jax.ShapeDtypeStruct((AB * CB, NO * NO), jnp.float32),
        )
        out_specs = (VMEM, VMEM)
    else:
        out_shape = pltpu.VMEM((VROWS, NO * NO), jnp.float32)
        out_specs = VMEM
    count = 2 * len(groups)
    return pl.pallas_call(
        functools.partial(ladder_kernel, groups),
        out_shape=out_shape,
        in_specs=in_specs,
        out_specs=out_specs,
        scratch_shapes=[
            pltpu.VMEM((count, AB // 2, 4, NV, NV), jnp.float32),
            pltpu.VMEM((count, HALF, 640), jnp.bfloat16),
            pltpu.VMEM((count, HALF, 640), jnp.bfloat16),
            pltpu.SemaphoreType.DMA((count,)),
        ],
        compiler_params=pltpu.CompilerParams(vmem_limit_bytes=(6 + 13 * len(groups)) << 20),
        cost_estimate=pl.CostEstimate(
            flops=len(groups) * 3 * 2 * 1600 * 640 * 256,
            bytes_accessed=len(groups) * (8 << 20),
            transcendentals=0,
        ),
    )(*operands)


def post_kernel(tbl_ref, x_ref, chi_ref, w_ref, f_ref, p_ref, o_ref, c0, c1, r0, r1, m1):
    owner = lax.broadcasted_iota(jnp.int32, (NO, NO * NO), 1) // NO
    for rel in range(ROWS):
        k = tbl_ref[rel]
        piece = chi_ref[rel] + w_ref[pl.ds(pl.multiple_of(k * NO, NO), NO), :]
        piece = piece - jnp.where(owner == k, f_ref[...], 0.0)
        c0[pl.ds(k, NO, stride=NO), :] = piece[:, 0:128]
        c1[pl.ds(k, NO, stride=NO), :] = piece[:, 128:256]
    chi = jnp.concatenate([c0[...], c1[...]], axis=1)
    total = x_ref[0]
    for c in range(1, COLS):
        total = total + x_ref[c]
    total = total + jnp.dot(
        p_ref[...], chi, precision=lax.Precision.HIGHEST, preferred_element_type=jnp.float32
    )
    total = jnp.concatenate([total, jnp.zeros((256 - AB * CB, NO * NO), jnp.float32)], axis=0)
    raw = total.T
    r0[...] = raw[:, 0:128]
    r1[...] = raw[:, 128:256]
    for i in range(NO):
        m1[i * NO : (i + 1) * NO, 0:128] = r0[pl.ds(i, NO, stride=NO), :]
        m1[i * NO : (i + 1) * NO, 128:256] = r1[pl.ds(i, NO, stride=NO), :]
    flipped = m1[...]
    for d in range(ROWS * COLS):
        o_ref[d, 0:2, :] = raw[2 * d : 2 * d + 2, :]
        o_ref[d, 2:4, :] = flipped[2 * d : 2 * d + 2, :]


def post(tbl, scattered, chi, bare, fock, block):
    return pl.pallas_call(
        post_kernel,
        out_shape=jax.ShapeDtypeStruct((ROWS * COLS, 4, 256), jnp.float32),
        in_specs=[pl.BlockSpec(memory_space=pltpu.SMEM)] + [VMEM] * 5,
        out_specs=VMEM,
        scratch_shapes=[pltpu.VMEM((NO * NO, 128), jnp.float32)] * 4
        + [pltpu.VMEM((NO * NO, 256), jnp.float32)],
        compiler_params=pltpu.CompilerParams(vmem_limit_bytes=12 << 20),
        cost_estimate=pl.CostEstimate(
            flops=6 * 2 * 200 * 65536, bytes_accessed=3 << 20, transcendentals=0
        ),
    )(tbl, scattered, chi, bare, fock, block)


def final_kernel(e_ref, x_ref, tf_ref, vrow_ref, vcol_ref, o_ref, left, right):
    for o in range(2):
        for s in range(2):
            for a in range(AB):
                pieces = [x_ref[o, s, c, :, a * CB : (a + 1) * CB] for c in range(COLS)]
                line = jnp.concatenate(pieces, axis=1)
                left[o, s, pl.ds(a, ROWS, stride=AB), :] = line[:, 0:128]
                right[o, s, pl.ds(a, ROWS, stride=AB), 0:32] = line[:, 128:NV]
    for s in range(2):
        full = [
            jnp.concatenate([left[o, s], right[o, s, :, 0:32]], axis=1) for o in range(2)
        ]
        total = full[0] + full[1].T + tf_ref[s]
        den = (e_ref[s] - vcol_ref[...]) - vrow_ref[...]
        o_ref[s] = total / den


def finish(e, x, tf, eps_vir):
    return pl.pallas_call(
        final_kernel,
        out_shape=jax.ShapeDtypeStruct((2, NV, NV), jnp.float32),
        in_specs=[pl.BlockSpec(memory_space=pltpu.SMEM)]
        + [pl.BlockSpec(memory_space=pltpu.VMEM)] * 4,
        out_specs=pl.BlockSpec(memory_space=pltpu.VMEM),
        scratch_shapes=[pltpu.VMEM((2, 2, NV, 128), jnp.float32)] * 2,
        cost_estimate=pl.CostEstimate(flops=0, bytes_accessed=2 << 20, transcendentals=0),
    )(e, x, tf, eps_vir.reshape(1, NV), eps_vir.reshape(NV, 1))


def on_device(amplitudes, vvvv, hole_ints, exchange_ints, fock_occ, fock_vir, eps_occ, eps_vir):
    high = lax.Precision.HIGHEST
    row = lax.axis_index("row")
    col = lax.axis_index("col")
    t = amplitudes[0]
    packed = pack(t)
    arrived = lax.all_to_all(packed, "col", split_axis=0, concat_axis=0, tiled=True)
    x = arrived.reshape(NO, KT, 128).transpose(1, 0, 2)

    def hop(value, dy, dz, dc):
        return lax.ppermute(value, "row", row_perm(dy, dz, dc))

    v4 = pltpu.with_memory_space_constraint(vvvv.transpose(0, 2, 1, 3), pltpu.HBM)
    k4 = exchange_ints[0].transpose(1, 0, 2)
    bare = hole_ints.reshape(NO * NO, NO * NO)
    fock = jnp.tile(fock_occ, (1, NO))
    pair = jnp.stack([x, hop(x, 1, 0, 0)])
    pair, bare, fock = lax.optimization_barrier((pair, bare, fock))
    ahead = hop(pair, 0, 1, 0)
    behind = hop(pair, 0, 3, 0)
    far = jnp.stack([hop(ahead[0], 0, 1, 0), hop(behind[1], 0, 3, 0)])
    own = jnp.stack([pair, ahead, far, behind])
    other = hop(own, 0, 0, 1)
    own = own.reshape(8, KT, NO, 128)
    other = other.reshape(8, KT, NO, 128)

    rel = jnp.arange(ROWS, dtype=jnp.int32)
    dc, dz, dy = rel // 8, (rel // 2) % 4, rel % 2
    table = ((row // 8 + dy) % 2) * 8 + ((row // 2 + dz) % 4) * 2 + ((row % 2) ^ dc)

    e_row = jnp.arange(EROWS, dtype=jnp.int32)[:, None]
    e_col = jnp.arange(640, dtype=jnp.int32)[None, :]
    want = row * AB + e_row // 4
    cc = e_row % 4
    place = jnp.where(want < 128, cc * 128 + want, 512 + cc * 32 + want - 128)
    onehot = (e_col == place).astype(jnp.bfloat16)

    ghi, glo, chi = prepare(table, own, other, k4)

    def fold(value, flip):
        return value + lax.ppermute(value, "col", [(c, c ^ flip) for c in range(COLS)])

    chi = fold(chi, 1)
    lad = ladder(ghi, glo, v4, (0, 1))
    chi = fold(chi, 2)
    lad = ladder(ghi, glo, v4, (2,), before=lad)
    chi = fold(chi, 4)
    lad = ladder(ghi, glo, v4, (3,), before=lad)
    chi = jnp.stack([chi, hop(chi, 1, 0, 0)])
    lad, block = ladder(ghi, glo, v4, (4,), before=lad, onehot=onehot)
    lad, chi = lax.optimization_barrier((lad, chi))
    scattered = lax.all_to_all(lad, "col", split_axis=0, concat_axis=0, tiled=True)

    chi = jnp.stack([chi] + [hop(chi, 0, dz, 0) for dz in (1, 2, 3)])
    chi = jnp.stack([chi, hop(chi, 0, 0, 1)]).reshape(ROWS, NO, NO * NO)
    sending = post(table, scattered, chi, bare, fock, block)
    back = lax.all_to_all(sending, ("row", "col"), split_axis=0, concat_axis=0, tiled=True)
    back = back.reshape(ROWS, COLS, 2, 2, 256).transpose(2, 3, 1, 0, 4)

    tf = jnp.einsum("jac,cb->jab", t, fock_vir, precision=high)
    tf = tf + jnp.einsum("ac,jcb->jab", fock_vir, t, precision=high)
    first = lax.dynamic_slice_in_dim(eps_occ, row, 1)
    second = lax.dynamic_slice_in_dim(eps_occ, col * 2, 2)
    return finish(first + second, back, tf, eps_vir)[None]


def solution(mesh):
    in_specs = (
        P("row", "col", None, None),
        P("row", None, "col", None),
        P(),
        P("row", None, "col", None),
        P(),
        P(),
        P(),
        P(),
    )
    return jax.shard_map(
        on_device,
        mesh=mesh,
        in_specs=in_specs,
        out_specs=P("row", "col", None, None),
        check_vma=False,
    )
```

time: 175 us -> 139 us (0.79)
  blocking collectives: 81.4 us -> 11.9 us
  starting transfers between devices: 18.1 us -> 32.8 us
  Pallas kernels: 26.3 us -> 40.1 us
  waiting for transfers between devices: 32.1 us -> 42 us
  other arithmetic: 5.29 us -> 1.64 us
    all_gather x2 -> x0, blocking collectives: 69.5 us -> none  [the longest x1 45 us: on_device(): chi_cols = jnp.sum(lax.all_gather(chi_part, 'col', axis=0), axis=0)]
    ppermute x5 -> x14, starting transfers between devices: 9.05 us -> 23.7 us  [the longest x11 19.5 us: hop(): return lax.ppermute(value, 'row', row_perm(dy, dz, dc))]
    pallas_call x1 -> x6, Pallas kernels: 21.6 us -> 35.4 us  [the longest x4 30.7 us: ladder(): pl.pallas_call(functools.partial(ladder_kernel, groups), out_shape=out_sh...]
    all_to_all x1, waiting for transfers between devices: 0.01 us -> 13.2 us  [on_device(): lax.all_to_all(lad, 'col', split_axis=0, concat_axis=0, tiled=True)]
    ppermute x5 -> x14, waiting for transfers between devices: 22.2 us -> 19 us  [the longest x11 18.9 us: hop(): return lax.ppermute(value, 'row', row_perm(dy, dz, dc))]
    transpose x2 -> x0, other arithmetic: 2.18 us -> none  [the longest x1 1.94 us: on_device(): chi = chi.transpose(1, 0, 2, 3).reshape(NO * NO, NO * NO)]
  transfers between devices with their start and end apart: 7 -> 16, of which waited for: 5 -> 9; matrix products, arithmetic and copies ran while one was open for 5% -> 5% of each run, Pallas kernels for 0% -> 22%
where the time goes in v1:
time: 139 us; the launch traced here: 138 us
  waiting for transfers between devices  42 us (30%)
  Pallas kernels  40.1 us (29%)
  starting transfers between devices  32.8 us (24%)
  blocking collectives  11.9 us (9%)
  local copies, waits for them, and re-layouts  7.81 us (6%)
  other arithmetic  1.64 us (1%)
  matrix products  1.62 us (1%)
    pallas_call x4, Pallas kernels, ladder(): pl.pallas_call(functools.partial(ladder_kernel, groups), out_shape=out_sh...  30.7 us
    ppermute x11, starting transfers between devices, hop(): return lax.ppermute(value, 'row', row_perm(dy, dz, dc))  19.5 us
    ppermute x11, waiting for transfers between devices, hop(): return lax.ppermute(value, 'row', row_perm(dy, dz, dc))  18.9 us
    all_to_all x1, waiting for transfers between devices, on_device(): lax.all_to_all(lad, 'col', split_axis=0, concat_axis=0, tiled=True)  13.2 us
    all_to_all x1, blocking collectives, on_device(): lax.all_to_all(packed, 'col', split_axis=0, concat_axis=0, tiled=True)  11.9 us
    all_to_all x1, waiting for transfers between devices, on_device(): lax.all_to_all(sending, ('row', 'col'), split_axis=0, concat_axis=0, tile...  9.86 us
    all_to_all x1, starting transfers between devices, on_device(): lax.all_to_all(sending, ('row', 'col'), split_axis=0, concat_axis=0, tile...  5.44 us
    ppermute x3, starting transfers between devices, fold(): lax.ppermute(value, 'col', [(c, c ^ flip) for c in range(COLS)])  4.18 us
  transfers between devices with their start and end apart: 16, of which 9 were waited for; matrix products, arithmetic and copies ran while one was open for 5% of the time, Pallas kernels for 22%

profile of v1, /device:TPU:0, one launch (start us, length us, event | category | flops | bytes accessed | tf_op | source)
XLA Modules:
  0.0 138.2 jit_solution(10712340723919163613)
XLA Ops:
  0.0 1.8 %shard_map.82 = f32[8,2,25,128]{3,2,1,0:T(8,128)} custom-call(f32[2,160,160]{2,1,0:T(8,128)} %bitcast.65), custom_call_target="tpu_custom_call" | custom-call | bytes 600000 | tf_op jit(solution)/shard_map/pallas_call | solution.py:43
  1.8 1.1 copy.24
  3.0 11.9 %all_to_all.15 = f32[8,2,25,128]{3,1,2,0:T(2,128)S(1)} all-to-all(f32[8,2,25,128]{3,1,2,0:T(2,128)S(1)} %copy.24), channel_id=1, replica_groups=mesh['row'=16,'col'=8] {'col'}, dimensions={0} | all-to-all | bytes 409600 | tf_op jit(solution)/shard_map/all_to_all | solution.py:268
  14.9 0.1 copy.25
  14.9 3.0 %collective-permute-start = (f32[25,16,128]{2,1,0:T(8,128)S(1)}, f32[25,16,128]{2,1,0:T(8,128)S(1)}, u32[]{:S(2)}, u32[]{:S(2)}) collective-permute-start(f32[25,16,128]{2,1,0:T(8,128)S(1)} %bitcast.71), channel_id=1, source_target_pairs={{64,0},{72,8},{80,16},{88,24},{96,32},{104,40},{112,48},{120,56},{... | collective-permute-start | bytes 614408 | tf_op jit(solution)/shard_map/ppermute | solution.py:272
  17.9 3.1 %reshape.98.w_ref = f32[256,256]{1,0:T(8,128)} reshape(f32[16,16,16,16]{3,2,1,0:T(8,128)} %param.10) | data formatting | bytes 524288 | tf_op jit(solution)/shard_map/reshape | solution.py:276
  21.0 0.1 tile.10.f_ref
  21.1 1.2 collective-permute-done
  22.3 2.0 %collective-permute-start.3 = (f32[2,25,16,128]{3,2,1,0:T(8,128)S(1)}, f32[2,25,16,128]{3,2,1,0:T(8,128)S(1)}, u32[]{:S(2)}, u32[]{:S(2)}) collective-permute-start(f32[2,25,16,128]{3,2,1,0:T(8,128)S(1)} %pad_maximum_fusion.1), channel_id=1, source_target_pairs={{48,0},{56,8},{0,16},{8,24},{16,32},{24,40},{32,48},{40,56},{112,6... | collective-permute-start | bytes 1228808 | tf_op jit(solution)/shard_map/ppermute | solution.py:272
  24.3 2.2 %collective-permute-start.1 = (f32[2,25,16,128]{3,2,1,0:T(8,128)S(1)}, f32[2,25,16,128]{3,2,1,0:T(8,128)S(1)}, u32[]{:S(2)}, u32[]{:S(2)}) collective-permute-start(f32[2,25,16,128]{3,2,1,0:T(8,128)S(1)} %pad_maximum_fusion.1), channel_id=1, source_target_pairs={{16,0},{24,8},{32,16},{40,24},{48,32},{56,40},{0,48},{8,56},{80,64... | collective-permute-start | bytes 1228808 | tf_op jit(solution)/shard_map/ppermute | solution.py:272
  26.5 6.9 %collective-permute-done.3 = f32[2,25,16,128]{3,2,1,0:T(8,128)S(1)} collective-permute-done((f32[2,25,16,128]{3,2,1,0:T(8,128)S(1)}, f32[2,25,16,128]{3,2,1,0:T(8,128)S(1)}, u32[]{:S(2)}, u32[]{:S(2)}) %collective-permute-start.3) | collective-permute-done | bytes 409632 | tf_op jit(solution)/shard_map/ppermute | solution.py:272
  33.4 0.1 collective-permute-start.4
  33.5 3.3 %collective-permute-start.2 = (f32[25,16,128]{2,1,0:T(8,128)S(1)}, f32[25,16,128]{2,1,0:T(8,128)S(1)}, u32[]{:S(2)}, u32[]{:S(2)}) collective-permute-start(f32[25,16,128]{2,1,0:T(8,128)S(1)} %slice_bitcast_fusion.1), channel_id=1, source_target_pairs={{16,0},{24,8},{32,16},{40,24},{48,32},{56,40},{0,48},{8,56},{80,64... | collective-permute-start | bytes 614408 | tf_op jit(solution)/shard_map/ppermute | solution.py:272
  36.8 3.6 %collective-permute-done.4 = f32[25,16,128]{2,1,0:T(8,128)S(1)} collective-permute-done((f32[25,16,128]{2,1,0:T(8,128)S(1)}, f32[25,16,128]{2,1,0:T(8,128)S(1)}, u32[]{:S(2)}, u32[]{:S(2)}) %collective-permute-start.4) | collective-permute-done | bytes 204832 | tf_op jit(solution)/shard_map/ppermute | solution.py:272
  40.5 0.1 pad_maximum_fusion
  40.6 0.1 collective-permute-start.5
  40.8 0.1 fusion.4.refs_1_
  40.9 3.3 %collective-permute-done.5 = f32[4,2,25,16,128]{4,3,2,1,0:T(8,128)S(1)} collective-permute-done((f32[4,2,25,16,128]{4,3,2,1,0:T(8,128)S(1)}, f32[4,2,25,16,128]{4,3,2,1,0:T(8,128)S(1)}, u32[]{:S(2)}, u32[]{:S(2)}) %collective-permute-start.5) | collective-permute-done | bytes 1638432 | tf_op jit(solution)/shard_map/ppermute | solution.py:272
  44.2 1.0 copy-done.2
  45.2 2.7 %shard_map.83 = (bf16[5,256,1280]{2,1,0:T(8,128)(2,1)S(1)}, bf16[5,256,640]{2,1,0:T(8,128)(2,1)S(1)}, f32[16,256]{1,0:T(8,128)S(1)}) custom-call(s32[16]{0:T(128)S(1)} %fusion.6.tbl_ref, f32[8,25,16,128]{3,2,1,0:T(8,128)S(1)} %bitcast.57, f32[8,25,16,128]{3,2,1,0:T(8,128)S(1)} %bitcast.58, f32[20,16,160]{2,1,0:T(8,128)S(1)} %bitcast.60), custom_call_target="tpu_custom_call" | custom-call | bytes 8388608 | tf_op jit(solution)/shard_map/pallas_call | solution.py:84
  47.9 1.1 collective-permute-start.6
  49.0 10.2 %shard_map.84.refs_0_ = f32[1600,256]{1,0:T(8,128)S(1)} custom-call(bf16[5,256,1280]{2,1,0:T(8,128)(2,1)S(1)} %get-tuple-element.16.ghi, bf16[5,256,640]{2,1,0:T(8,128)(2,1)S(1)} %get-tuple-element.17.glo, f32[10,20,160,160]{3,2,1,0:T(8,128)} %bitcast.61), custom_call_target="tpu_custom_call" | custom-call | flops 3145728000 | bytes 16777216 | tf_op jit(solution)/shard_map/pallas_call | solution.py:170
  59.3 1.1 collective-permute-start.7
  60.4 6.2 %shard_map.85.refs_0_ = f32[1600,256]{1,0:T(8,128)S(1)} custom-call(bf16[5,256,1280]{2,1,0:T(8,128)(2,1)S(1)} %get-tuple-element.16.ghi, bf16[5,256,640]{2,1,0:T(8,128)(2,1)S(1)} %get-tuple-element.17.glo, f32[10,20,160,160]{3,2,1,0:T(8,128)} %bitcast.62, f32[1600,256]{1,0:T(8,128)S(1)} %shard_map.84.refs_0_), custom_call_target="tpu_custom_call" | custom-call | flops 1572864000 | bytes 8388608 | tf_op jit(solution)/shard_map/pallas_call | solution.py:170
  66.6 1.9 %collective-permute-start.8 = (f32[16,256]{1,0:T(8,128)S(1)}, f32[16,256]{1,0:T(8,128)S(1)}, u32[]{:S(2)}, u32[]{:S(2)}) collective-permute-start(f32[16,256]{1,0:T(8,128)S(1)} %add.159), channel_id=1, source_target_pairs={{0,4},{1,5},{2,6},{3,7},{4,0},{5,1},{6,2},{7,3},{8,12},{9,13},{10,... | collective-permute-start | bytes 49160 | tf_op jit(solution)/shard_map/ppermute | solution.py:302
  68.6 6.2 %shard_map.86.refs_0_ = f32[1600,256]{1,0:T(8,128)S(1)} custom-call(bf16[5,256,1280]{2,1,0:T(8,128)(2,1)S(1)} %get-tuple-element.16.ghi, bf16[5,256,640]{2,1,0:T(8,128)(2,1)S(1)} %get-tuple-element.17.glo, f32[10,20,160,160]{3,2,1,0:T(8,128)} %bitcast.63, f32[1600,256]{1,0:T(8,128)S(1)} %shard_map.85.refs_0_), custom_call_target="tpu_custom_call" | custom-call | flops 1572864000 | bytes 8388608 | tf_op jit(solution)/shard_map/pallas_call | solution.py:170
  74.8 3.0 %collective-permute-start.9 = (f32[16,256]{1,0:T(8,128)S(1)}, f32[16,256]{1,0:T(8,128)S(1)}, u32[]{:S(2)}, u32[]{:S(2)}) collective-permute-start(f32[16,256]{1,0:T(8,128)S(1)} %add.160), channel_id=1, source_target_pairs={{64,0},{72,8},{80,16},{88,24},{96,32},{104,40},{112,48},{120,56},{... | collective-permute-start | bytes 49160 | tf_op jit(solution)/shard_map/ppermute | solution.py:272
  77.8 8.1 %shard_map.87 = (f32[8,200,256]{2,1,0:T(8,128)}, f32[200,256]{1,0:T(8,128)S(1)}) custom-call(bf16[5,256,1280]{2,1,0:T(8,128)(2,1)S(1)} %get-tuple-element.16.ghi, bf16[5,256,640]{2,1,0:T(8,128)(2,1)S(1)} %get-tuple-element.17.glo, f32[10,20,160,160]{3,2,1,0:T(8,128)} %bitcast.64, f32[1600,256]{1,0:T(8,128)S(1)} %shard_map.86.refs_0_, ...), custom_call_target="tpu_custom_call" | custom-call | flops 1572864000 | bytes 8388608 | tf_op jit(solution)/shard_map/pallas_call | solution.py:170
  85.9 3.7 %all-to-all-start.1 = ((f32[8,200,256]{2,1,0:T(8,128)}), f32[8,200,256]{2,1,0:T(8,128)S(1)}, u32[]{:S(2)}, u32[]{:S(2)}) async-start(f32[8,200,256]{2,1,0:T(8,128)} %get-tuple-element.20), calls=%async_computation.1 | async-start | bytes 3276800 | tf_op jit(solution)/shard_map/all_to_all | solution.py:313
  89.7 1.3 collective-permute-start.12
  91.0 3.6 %collective-permute-start.11 = (f32[2,16,256]{2,1,0:T(8,128)S(1)}, f32[2,16,256]{2,1,0:T(8,128)S(1)}, u32[]{:S(2)}, u32[]{:S(2)}) collective-permute-start(f32[2,16,256]{2,1,0:T(8,128)S(1)} %pad_maximum_fusion.4), channel_id=1, source_target_pairs={{32,0},{40,8},{48,16},{56,24},{0,32},{8,40},{16,48},{24,56},{96,64... | collective-permute-start | bytes 98312 | tf_op jit(solution)/shard_map/ppermute | solution.py:272
  94.5 0.7 collective-permute-start.10
  95.3 1.5 %collective-permute-done.11 = f32[2,16,256]{2,1,0:T(8,128)S(1)} collective-permute-done((f32[2,16,256]{2,1,0:T(8,128)S(1)}, f32[2,16,256]{2,1,0:T(8,128)S(1)}, u32[]{:S(2)}, u32[]{:S(2)}) %collective-permute-start.11) | collective-permute-done | bytes 32800 | tf_op jit(solution)/shard_map/ppermute | solution.py:272
  96.8 1.7 %collective-permute-done.10 = f32[2,16,256]{2,1,0:T(8,128)S(1)} collective-permute-done((f32[2,16,256]{2,1,0:T(8,128)S(1)}, f32[2,16,256]{2,1,0:T(8,128)S(1)}, u32[]{:S(2)}, u32[]{:S(2)}) %collective-permute-start.10) | collective-permute-done | bytes 32800 | tf_op jit(solution)/shard_map/ppermute | solution.py:272
  98.5 0.3 collective-permute-start.13
  98.8 0.6 dynamic_slice.6
  99.4 0.7 collective-permute-done.13
  100.1 13.2 %all-to-all-done.1.x_ref = f32[8,200,256]{2,1,0:T(8,128)S(1)} async-done(((f32[8,200,256]{2,1,0:T(8,128)}), f32[8,200,256]{2,1,0:T(8,128)S(1)}, u32[]{:S(2)}, u32[]{:S(2)}) %all-to-all-start.1) | async-done | bytes 1638432 | tf_op jit(solution)/shard_map/all_to_all | solution.py:313
  113.4 2.0 %shard_map.88 = f32[128,4,256]{2,1,0:T(4,128)} custom-call(s32[16]{0:T(128)S(1)} %fusion.6.tbl_ref, f32[8,200,256]{2,1,0:T(8,128)S(1)} %all-to-all-done.1.x_ref, f32[16,16,256]{2,1,0:T(8,128)S(1)} %bitcast.59, f32[256,256]{1,0:T(8,128)S(1)} %copy-done.1, f32[16,256]{1,0:T(8,128)S(1)} %tile.10.f_ref, f32[200,256]{1,0:T(8,128)S(1)} %get-tuple-element.24.p_ref), custom_call_target="tpu_custom_call" | custom-call | flops 157286400 | bytes 3145728 | tf_op jit(solution)/shard_map/pallas_call | solution.py:219
  115.3 5.4 %all-to-all-start.2 = ((f32[128,4,256]{2,1,0:T(4,128)}), f32[128,4,256]{2,1,0:T(4,128)S(1)}, u32[]{:S(2)}, u32[]{:S(2)}) async-start(f32[128,4,256]{2,1,0:T(4,128)} %shard_map.88), calls=%async_computation.2 | async-start | bytes 1048576 | tf_op jit(solution)/shard_map/all_to_all | solution.py:318
  120.8 1.3 dynamic-slice_add_fusion.e_ref
  122.1 0.7 copy.30.vcol_ref
  122.8 0.4 fusion.2
  123.3 1.2 fusion.tf_ref
  124.5 9.9 %all-to-all-done.2 = f32[128,4,256]{2,1,0:T(4,128)S(1)} async-done(((f32[128,4,256]{2,1,0:T(4,128)}), f32[128,4,256]{2,1,0:T(4,128)S(1)}, u32[]{:S(2)}, u32[]{:S(2)}) %all-to-all-start.2) | async-done | bytes 524320 | tf_op jit(solution)/shard_map/all_to_all | solution.py:318
  134.3 0.1 copy.26
  134.4 1.0 copy.34
  135.4 2.9 %shard_map.89 = f32[2,160,160]{2,1,0:T(8,128)} custom-call(f32[2]{0:T(128)} %dynamic-slice_add_fusion.e_ref, f32[2,2,8,16,256]{4,3,2,1,0:T(8,128)} %bitcast.67, f32[2,160,160]{2,1,0:T(8,128)} %fusion.tf_ref, f32[1,160]{1,0:T(1,128)} %bitcast.83, f32[160,1]{1,0:T(8,128)} %copy.30.vcol_ref), custom_call_target="tpu_custom_call" | custom-call | bytes 2097152 | tf_op jit(solution)/shard_map/pallas_call | solution.py:251
  (33 shorter events, 0.3 us)
Async XLA Ops:
  0.0 122.8 %copy-start = (f32[160,160]{1,0:T(8,128)S(1)}, f32[160,160]{1,0:T(8,128)}, u32[]{:S(2)}) copy-start(f32[160,160]{1,0:T(8,128)} %param.13) | copy-start | bytes 307204
  3.0 18.0 %copy-start.4 = (f32[16,16]{1,0:T(8,128)S(1)}, f32[16,16]{1,0:T(8,128)}, u32[]{:S(2)}) copy-start(f32[16,16]{1,0:T(8,128)} %param.12) | copy-start | bytes 3076
  14.9 7.3 %collective-permute-start = (f32[25,16,128]{2,1,0:T(8,128)S(1)}, f32[25,16,128]{2,1,0:T(8,128)S(1)}, u32[]{:S(2)}, u32[]{:S(2)}) collective-permute-start(f32[25,16,128]{2,1,0:T(8,128)S(1)} %bitcast.71), channel_id=1, source_target_pairs={{64,0},{72,8},{80,16},{88,24},{96,32},{104,40},{112,48},{120,56},{... | collective-permute-start | bytes 614408 | tf_op jit(solution)/shard_map/ppermute | solution.py:272
  22.3 11.1 %collective-permute-start.3 = (f32[2,25,16,128]{3,2,1,0:T(8,128)S(1)}, f32[2,25,16,128]{3,2,1,0:T(8,128)S(1)}, u32[]{:S(2)}, u32[]{:S(2)}) collective-permute-start(f32[2,25,16,128]{3,2,1,0:T(8,128)S(1)} %pad_maximum_fusion.1), channel_id=1, source_target_pairs={{48,0},{56,8},{0,16},{8,24},{16,32},{24,40},{32,48},{40,56},{112,6... | collective-permute-start | bytes 1228808 | tf_op jit(solution)/shard_map/ppermute | solution.py:272
  24.3 9.2 %collective-permute-start.1 = (f32[2,25,16,128]{3,2,1,0:T(8,128)S(1)}, f32[2,25,16,128]{3,2,1,0:T(8,128)S(1)}, u32[]{:S(2)}, u32[]{:S(2)}) collective-permute-start(f32[2,25,16,128]{3,2,1,0:T(8,128)S(1)} %pad_maximum_fusion.1), channel_id=1, source_target_pairs={{16,0},{24,8},{32,16},{40,24},{48,32},{56,40},{0,48},{8,56},{80,64... | collective-permute-start | bytes 1228808 | tf_op jit(solution)/shard_map/ppermute | solution.py:272
  33.4 7.0 %collective-permute-start.4 = (f32[25,16,128]{2,1,0:T(8,128)S(1)}, f32[25,16,128]{2,1,0:T(8,128)S(1)}, u32[]{:S(2)}, u32[]{:S(2)}) collective-permute-start(f32[25,16,128]{2,1,0:T(8,128)S(1)} %slice_bitcast_fusion), channel_id=1, source_target_pairs={{48,0},{56,8},{0,16},{8,24},{16,32},{24,40},{32,48},{40,56},{112,6... | collective-permute-start | bytes 614408 | tf_op jit(solution)/shard_map/ppermute | solution.py:272
  33.5 6.9 %collective-permute-start.2 = (f32[25,16,128]{2,1,0:T(8,128)S(1)}, f32[25,16,128]{2,1,0:T(8,128)S(1)}, u32[]{:S(2)}, u32[]{:S(2)}) collective-permute-start(f32[25,16,128]{2,1,0:T(8,128)S(1)} %slice_bitcast_fusion.1), channel_id=1, source_target_pairs={{16,0},{24,8},{32,16},{40,24},{48,32},{56,40},{0,48},{8,56},{80,64... | collective-permute-start | bytes 614408 | tf_op jit(solution)/shard_map/ppermute | solution.py:272
  40.6 3.6 %collective-permute-start.5 = (f32[4,2,25,16,128]{4,3,2,1,0:T(8,128)S(1)}, f32[4,2,25,16,128]{4,3,2,1,0:T(8,128)S(1)}, u32[]{:S(2)}, u32[]{:S(2)}) collective-permute-start(f32[4,2,25,16,128]{4,3,2,1,0:T(8,128)S(1)} %pad_maximum_fusion), channel_id=1, source_target_pairs={{8,0},{0,8},{24,16},{16,24},{40,32},{32,40},{56,48},{48,56},{72,64... | collective-permute-start | bytes 4915208 | tf_op jit(solution)/shard_map/ppermute | solution.py:272
  44.2 1.0 copy-start.2
  47.9 11.3 %collective-permute-start.6 = (f32[16,256]{1,0:T(8,128)S(1)}, f32[16,256]{1,0:T(8,128)S(1)}, u32[]{:S(2)}, u32[]{:S(2)}) collective-permute-start(f32[16,256]{1,0:T(8,128)S(1)} %get-tuple-element.19), channel_id=1, source_target_pairs={{0,1},{1,0},{2,3},{3,2},{4,5},{5,4},{6,7},{7,6},{8,9},{9,8},{10,11... | collective-permute-start | bytes 49160 | tf_op jit(solution)/shard_map/ppermute | solution.py:302
  59.3 7.3 %collective-permute-start.7 = (f32[16,256]{1,0:T(8,128)S(1)}, f32[16,256]{1,0:T(8,128)S(1)}, u32[]{:S(2)}, u32[]{:S(2)}) collective-permute-start(f32[16,256]{1,0:T(8,128)S(1)} %add.158), channel_id=1, source_target_pairs={{0,2},{1,3},{2,0},{3,1},{4,6},{5,7},{6,4},{7,5},{8,10},{9,11},{10,... | collective-permute-start | bytes 49160 | tf_op jit(solution)/shard_map/ppermute | solution.py:302
  66.6 8.2 %collective-permute-start.8 = (f32[16,256]{1,0:T(8,128)S(1)}, f32[16,256]{1,0:T(8,128)S(1)}, u32[]{:S(2)}, u32[]{:S(2)}) collective-permute-start(f32[16,256]{1,0:T(8,128)S(1)} %add.159), channel_id=1, source_target_pairs={{0,4},{1,5},{2,6},{3,7},{4,0},{5,1},{6,2},{7,3},{8,12},{9,13},{10,... | collective-permute-start | bytes 49160 | tf_op jit(solution)/shard_map/ppermute | solution.py:302
  74.8 11.1 %collective-permute-start.9 = (f32[16,256]{1,0:T(8,128)S(1)}, f32[16,256]{1,0:T(8,128)S(1)}, u32[]{:S(2)}, u32[]{:S(2)}) collective-permute-start(f32[16,256]{1,0:T(8,128)S(1)} %add.160), channel_id=1, source_target_pairs={{64,0},{72,8},{80,16},{88,24},{96,32},{104,40},{112,48},{120,56},{... | collective-permute-start | bytes 49160 | tf_op jit(solution)/shard_map/ppermute | solution.py:272
  85.9 12.9 %copy-start.6 = (f32[16]{0:T(128)S(1)}, f32[16]{0:T(128)}, u32[]{:S(2)}) copy-start(f32[16]{0:T(128)} %param.14) | copy-start | bytes 196
  85.9 27.4 %copy-start.1 = (f32[256,256]{1,0:T(8,128)S(1)}, f32[256,256]{1,0:T(8,128)}, u32[]{:S(2)}) copy-start(f32[256,256]{1,0:T(8,128)} %reshape.98.w_ref) | copy-start | bytes 786436
  85.9 27.4 %all-to-all-start.1 = ((f32[8,200,256]{2,1,0:T(8,128)}), f32[8,200,256]{2,1,0:T(8,128)S(1)}, u32[]{:S(2)}, u32[]{:S(2)}) async-start(f32[8,200,256]{2,1,0:T(8,128)} %get-tuple-element.20), calls=%async_computation.1 | async-start | bytes 3276800 | tf_op jit(solution)/shard_map/all_to_all | solution.py:313
  89.7 5.6 %collective-permute-start.12 = (f32[2,16,256]{2,1,0:T(8,128)S(1)}, f32[2,16,256]{2,1,0:T(8,128)S(1)}, u32[]{:S(2)}, u32[]{:S(2)}) collective-permute-start(f32[2,16,256]{2,1,0:T(8,128)S(1)} %pad_maximum_fusion.4), channel_id=1, source_target_pairs={{48,0},{56,8},{0,16},{8,24},{16,32},{24,40},{32,48},{40,56},{112,6... | collective-permute-start | bytes 98312 | tf_op jit(solution)/shard_map/ppermute | solution.py:272
  91.0 5.8 %collective-permute-start.11 = (f32[2,16,256]{2,1,0:T(8,128)S(1)}, f32[2,16,256]{2,1,0:T(8,128)S(1)}, u32[]{:S(2)}, u32[]{:S(2)}) collective-permute-start(f32[2,16,256]{2,1,0:T(8,128)S(1)} %pad_maximum_fusion.4), channel_id=1, source_target_pairs={{32,0},{40,8},{48,16},{56,24},{0,32},{8,40},{16,48},{24,56},{96,64... | collective-permute-start | bytes 98312 | tf_op jit(solution)/shard_map/ppermute | solution.py:272
  94.5 3.9 %collective-permute-start.10 = (f32[2,16,256]{2,1,0:T(8,128)S(1)}, f32[2,16,256]{2,1,0:T(8,128)S(1)}, u32[]{:S(2)}, u32[]{:S(2)}) collective-permute-start(f32[2,16,256]{2,1,0:T(8,128)S(1)} %pad_maximum_fusion.4), channel_id=1, source_target_pairs={{16,0},{24,8},{32,16},{40,24},{48,32},{56,40},{0,48},{8,56},{80,64... | collective-permute-start | bytes 98312 | tf_op jit(solution)/shard_map/ppermute | solution.py:272
  98.5 1.6 %collective-permute-start.13 = (f32[4,2,16,256]{3,2,1,0:T(8,128)S(1)}, f32[4,2,16,256]{3,2,1,0:T(8,128)S(1)}, u32[]{:S(2)}, u32[]{:S(2)}) collective-permute-start(f32[4,2,16,256]{3,2,1,0:T(8,128)S(1)} %get-tuple-element.26), channel_id=1, source_target_pairs={{8,0},{0,8},{24,16},{16,24},{40,32},{32,40},{56,48},{48,56},{72,64... | collective-permute-start | bytes 393224 | tf_op jit(solution)/shard_map/ppermute | solution.py:272
  113.4 8.7 %copy-start.5 = (f32[160]{0:T(256)S(1)}, f32[160]{0:T(256)}, u32[]{:S(2)}) copy-start(f32[160]{0:T(256)} %param.15) | copy-start | bytes 1924
  113.4 9.5 %copy-start.3 = (f32[1,2,160,160]{3,2,1,0:T(8,128)S(1)}, f32[1,2,160,160]{3,2,1,0:T(8,128)}, u32[]{:S(2)}) copy-start(f32[1,2,160,160]{3,2,1,0:T(8,128)} %param.8) | copy-start | bytes 614404
  115.3 19.0 %all-to-all-start.2 = ((f32[128,4,256]{2,1,0:T(4,128)}), f32[128,4,256]{2,1,0:T(4,128)S(1)}, u32[]{:S(2)}, u32[]{:S(2)}) async-start(f32[128,4,256]{2,1,0:T(4,128)} %shard_map.88), calls=%async_computation.2 | async-start | bytes 1048576 | tf_op jit(solution)/shard_map/all_to_all | solution.py:318

commit v2 on v1

--- a/solution.py
+++ b/solution.py
@@ -54,8 +54,66 @@
     return hi, lo
 
 
-def prepare_kernel(tbl_ref, s_ref, q_ref, k_ref, ghi, glo, chi_ref):
+def convert_block(load, store):
+    for kt in range(5):
+        if kt < 4:
+            x = load(kt, slice(0, 128))
+        else:
+            x = jnp.concatenate([load(cc, slice(128, NV)) for cc in range(4)], axis=1)
+        hi, lo = split(x)
+        store(slice(kt * 128, (kt + 1) * 128), hi)
+        store(slice(640 + kt * 128, 640 + (kt + 1) * 128), lo)
+
+
+def split_kernel(group, v_hbm, o_hbm, buf, res, sem_in, sem_out):
+    def fetch(a):
+        source = v_hbm.at[a, pl.ds(group * 4, 4)]
+        return pltpu.make_async_copy(source, buf.at[a], sem_in.at[a])
+
+    def send(a):
+        target = o_hbm.at[pl.ds(a * NV, NV)]
+        return pltpu.make_async_copy(res.at[pl.ds(a * NV, NV)], target, sem_out.at[a])
+
+    for a in range(AB):
+        fetch(a).start()
+    for a in range(AB):
+        fetch(a).wait()
+
+        def store(lanes, value, a=a):
+            res[a * NV : (a + 1) * NV, lanes] = value
+
+        convert_block(lambda cc, lanes, a=a: buf[a, cc, :, lanes], store)
+        send(a).start()
+    for a in range(AB):
+        send(a).wait()
+
+
+def split_integrals(v, group):
+    hbm = pl.BlockSpec(memory_space=pltpu.HBM)
+    return pl.pallas_call(
+        functools.partial(split_kernel, group),
+        out_shape=pltpu.HBM((VROWS, 1280), jnp.bfloat16),
+        in_specs=[hbm],
+        out_specs=hbm,
+        scratch_shapes=[
+            pltpu.VMEM((AB, 4, NV, NV), jnp.float32),
+            pltpu.VMEM((VROWS, 1280), jnp.bfloat16),
+            pltpu.SemaphoreType.DMA((AB,)),
+            pltpu.SemaphoreType.DMA((AB,)),
+        ],
+        compiler_params=pltpu.CompilerParams(vmem_limit_bytes=14 << 20),
+        cost_estimate=pl.CostEstimate(flops=0, bytes_accessed=11 << 20, transcendentals=0),
+    )(v)
+
+
+def prepare_kernel(tbl_ref, s_any, q_any, k_any, ghi, glo, chi_ref, s_ref, q_ref, k_ref, sem):
+    pairs = ((s_any, s_ref), (q_any, q_ref), (k_any, k_ref))
+    copies = [pltpu.make_async_copy(x, y, sem.at[n]) for n, (x, y) in enumerate(pairs)]
+    for copy in copies:
+        copy.start()
     for rel in range(ROWS):
+        if rel % 8 == 0:
+            copies[rel // 8].wait()
         ref = s_ref if rel < 8 else q_ref
         start = pl.multiple_of(tbl_ref[rel] * NO, NO)
         for kt in range(KT):
@@ -64,6 +122,7 @@
             ghi[g, pl.ds(start, NO), place * 128 : (place + 1) * 128] = hi
             ghi[g, pl.ds(start, NO), 640 + place * 128 : 640 + (place + 1) * 128] = hi
             glo[g, pl.ds(start, NO), place * 128 : (place + 1) * 128] = lo
+    copies[2].wait()
     chi = jnp.zeros((NO * NO, NO), jnp.float32)
     for g in range(5):
         parts = [k_ref[g * 4 + cc, :, 0:128] for cc in range(4)]
@@ -88,103 +147,107 @@
             pltpu.VMEM((5, NO * NO, 640), jnp.bfloat16),
             jax.ShapeDtypeStruct((NO, NO * NO), jnp.float32),
         ),
-        in_specs=[pl.BlockSpec(memory_space=pltpu.SMEM)] + [VMEM] * 3,
+        in_specs=[pl.BlockSpec(memory_space=pltpu.SMEM)]
+        + [pl.BlockSpec(memory_space=pltpu.HBM)] * 3,
         out_specs=(VMEM, VMEM, VMEM),
-        compiler_params=pltpu.CompilerParams(vmem_limit_bytes=7 << 20),
+        scratch_shapes=[
+            pltpu.VMEM((8, KT, NO, 128), jnp.float32),
+            pltpu.VMEM((8, KT, NO, 128), jnp.float32),
+            pltpu.VMEM((CB, NO, NV), jnp.float32),
+            pltpu.SemaphoreType.DMA((3,)),
+        ],
+        compiler_params=pltpu.CompilerParams(vmem_limit_bytes=11 << 20),
         cost_estimate=pl.CostEstimate(flops=0, bytes_accessed=8 << 20, transcendentals=0),
     )(tbl, s, q, k)
 
 
-def ladder_kernel(groups, ghi, glo, v_hbm, *refs):
-    first, last = groups[0] == 0, groups[-1] == 4
+def ladder_kernel(group, fresh, last, ghi, glo, *refs):
     refs = list(refs)
-    before = None if first else refs.pop(0)
-    e_ref = refs.pop(0) if last else None
+    v_hbm = refs.pop(0) if fresh else None
+    ready = None if fresh else refs.pop(0)
+    before = None if fresh else refs.pop(0)
     out = refs.pop(0)
-    p_ref = refs.pop(0) if last else None
-    buf, hi, lo, sem = refs
-    blocks = [(g, half) for g in groups for half in range(2)]
-    copies = []
-    for n, (g, half) in enumerate(blocks):
-        source = v_hbm.at[pl.ds(half * (AB // 2), AB // 2), pl.ds(g * 4, 4)]
-        copies.append(pltpu.make_async_copy(source, buf.at[n], sem.at[n]))
-        copies[-1].start()
+    if fresh:
+        buf, parts, sem = refs
+        copies = []
+        for n in range(2):
+            source = v_hbm.at[pl.ds(n * (AB // 2), AB // 2), pl.ds(0, 4)]
+            copies.append(pltpu.make_async_copy(source, buf.at[n], sem.at[n]))
+            copies[-1].start()
+        for n in range(2):
+            copies[n].wait()
+            for a in range(AB // 2):
+
+                def store(lanes, value, n=n, a=a):
+                    parts[n, a * NV : (a + 1) * NV, lanes] = value
+
+                convert_block(lambda cc, lanes, n=n, a=a: buf[n, a, cc, :, lanes], store)
+            part = dot_nt(parts[n], ghi[0]) + dot_nt(parts[n, :, 0:640], glo[0])
+            out[n * HALF : (n + 1) * HALF, :] = part
+        return
+    total = before[...] + dot_nt(ready[...], ghi[group])
+    total = total + dot_nt(ready[:, 0:640], glo[group])
+    if not last:
+        out[...] = total
+        return
+    for a in range(AB):
+        for c in range(COLS):
+            start = a * NV + c * CB
+            out[c, a * CB : (a + 1) * CB, :] = total[start : start + CB, :]
+
+
+def ladder(ghi, glo, source, group, before=None):
+    fresh, last = before is None, group == 4
+    operands = [ghi, glo, source]
+    in_specs = [VMEM, VMEM, pl.BlockSpec(memory_space=pltpu.HBM) if fresh else VMEM]
+    if not fresh:
+        operands.append(before)
+        in_specs.append(VMEM)
+    scratch = []
+    if fresh:
+        scratch = [
+            pltpu.VMEM((2, AB // 2, 4, NV, NV), jnp.float32),
+            pltpu.VMEM((2, HALF, 1280), jnp.bfloat16),
+            pltpu.SemaphoreType.DMA((2,)),
+        ]
     if last:
-        for g in range(5):
-            block = dot_nt(e_ref[...], ghi[g, :, 0:640]) + dot_nt(e_ref[...], glo[g])
-            for a in range(AB):
-                row = a * CB + g * 4
-                p_ref[row : row + 4, :] = block[a * 4 : a * 4 + 4, :]
-
-    def convert(n):
-        copies[n].wait()
-        for a in range(AB // 2):
-            rows = slice(a * NV, (a + 1) * NV)
-            for kt in range(5):
-                if kt < 4:
-                    x = buf[n, a, kt, :, 0:128]
-                else:
-                    tails = [buf[n, a, cc, :, 128:NV] for cc in range(4)]
-                    x = jnp.concatenate(tails, axis=1)
-                xh, xl = split(x)
-                hi[n, rows, kt * 128 : (kt + 1) * 128] = xh
-                lo[n, rows, kt * 128 : (kt + 1) * 128] = xl
-
-    totals = [None, None]
-    if not first:
-        totals = [before[0:HALF, :], before[HALF:VROWS, :]]
-    for n, (g, half) in enumerate(blocks):
-        convert(n)
-        part = dot_nt(hi[n], ghi[g, :, 0:640]) + dot_nt(hi[n], glo[g])
-        part = part + dot_nt(lo[n], ghi[g, :, 0:640])
-        totals[half] = part if totals[half] is None else totals[half] + part
-    for half in range(2):
-        total = totals[half]
-        if not last:
-            out[half * HALF : (half + 1) * HALF, :] = total
-            continue
-        for a in range(AB // 2):
-            row = (half * (AB // 2) + a) * CB
-            for c in range(COLS):
-                start = a * NV + c * CB
-                out[c, row : row + CB, :] = total[start : start + CB, :]
-
-
-def ladder(ghi, glo, v, groups, before=None, onehot=None):
-    operands = [ghi, glo, v]
-    in_specs = [VMEM, VMEM, pl.BlockSpec(memory_space=pltpu.HBM)]
-    for extra in (before, onehot):
-        if extra is not None:
-            operands.append(extra)
-            in_specs.append(VMEM)
-    if onehot is not None:
-        out_shape = (
-            jax.ShapeDtypeStruct((COLS, AB * CB, NO * NO), jnp.float32),
-            jax.ShapeDtypeStruct((AB * CB, NO * NO), jnp.float32),
-        )
-        out_specs = (VMEM, VMEM)
+        out_shape = pltpu.HBM((COLS, AB * CB, NO * NO), jnp.float32)
+        out_specs = pl.BlockSpec((COLS, AB * CB, NO * NO), lambda: (0, 0, 0))
     else:
         out_shape = pltpu.VMEM((VROWS, NO * NO), jnp.float32)
         out_specs = VMEM
-    count = 2 * len(groups)
-    return pl.pallas_call(
-        functools.partial(ladder_kernel, groups),
+    return pl.pallas_call(
+        functools.partial(ladder_kernel, group, fresh, last),
         out_shape=out_shape,
         in_specs=in_specs,
         out_specs=out_specs,
-        scratch_shapes=[
-            pltpu.VMEM((count, AB // 2, 4, NV, NV), jnp.float32),
-            pltpu.VMEM((count, HALF, 640), jnp.bfloat16),
-            pltpu.VMEM((count, HALF, 640), jnp.bfloat16),
-            pltpu.SemaphoreType.DMA((count,)),
-        ],
-        compiler_params=pltpu.CompilerParams(vmem_limit_bytes=(6 + 13 * len(groups)) << 20),
+        scratch_shapes=scratch,
+        compiler_params=pltpu.CompilerParams(vmem_limit_bytes=(14 if fresh else 11) << 20),
         cost_estimate=pl.CostEstimate(
-            flops=len(groups) * 3 * 2 * 1600 * 640 * 256,
-            bytes_accessed=len(groups) * (8 << 20),
+            flops=3 * 2 * 1600 * 640 * 256,
+            bytes_accessed=8 << 20,
             transcendentals=0,
         ),
     )(*operands)
+
+
+def block_kernel(ghi, glo, e_ref, p_ref):
+    for g in range(5):
+        block = dot_nt(e_ref[...], ghi[g, :, 0:640]) + dot_nt(e_ref[...], glo[g])
+        for a in range(AB):
+            row = a * CB + g * 4
+            p_ref[row : row + 4, :] = block[a * 4 : a * 4 + 4, :]
+
+
+def own_block(ghi, glo, onehot):
+    return pl.pallas_call(
+        block_kernel,
+        out_shape=jax.ShapeDtypeStruct((AB * CB, NO * NO), jnp.float32),
+        in_specs=[VMEM] * 3,
+        out_specs=VMEM,
+        compiler_params=pltpu.CompilerParams(vmem_limit_bytes=4 << 20),
+        cost_estimate=pl.CostEstimate(flops=1 << 31, bytes_accessed=6 << 20, transcendentals=0),
+    )(ghi, glo, onehot)
 
 
 def post_kernel(tbl_ref, x_ref, chi_ref, w_ref, f_ref, p_ref, o_ref, c0, c1, r0, r1, m1):
@@ -273,15 +336,16 @@
 
     v4 = pltpu.with_memory_space_constraint(vvvv.transpose(0, 2, 1, 3), pltpu.HBM)
     k4 = exchange_ints[0].transpose(1, 0, 2)
-    bare = hole_ints.reshape(NO * NO, NO * NO)
-    fock = jnp.tile(fock_occ, (1, NO))
     pair = jnp.stack([x, hop(x, 1, 0, 0)])
-    pair, bare, fock = lax.optimization_barrier((pair, bare, fock))
+    pair, opening = lax.optimization_barrier((pair, split_integrals(v4, 1)))
     ahead = hop(pair, 0, 1, 0)
     behind = hop(pair, 0, 3, 0)
+    second, third = split_integrals(v4, 2), split_integrals(v4, 3)
+    ahead, behind, second, third = lax.optimization_barrier((ahead, behind, second, third))
     far = jnp.stack([hop(ahead[0], 0, 1, 0), hop(behind[1], 0, 3, 0)])
     own = jnp.stack([pair, ahead, far, behind])
     other = hop(own, 0, 0, 1)
+    fourth = split_integrals(v4, 4)
     own = own.reshape(8, KT, NO, 128)
     other = other.reshape(8, KT, NO, 128)
 
@@ -296,24 +360,29 @@
     place = jnp.where(want < 128, cc * 128 + want, 512 + cc * 32 + want - 128)
     onehot = (e_col == place).astype(jnp.bfloat16)
 
-    ghi, glo, chi = prepare(table, own, other, k4)
+    hbm = lambda value: pltpu.with_memory_space_constraint(value, pltpu.HBM)
+    ghi, glo, chi = prepare(table, hbm(own), hbm(other), hbm(k4))
 
     def fold(value, flip):
         return value + lax.ppermute(value, "col", [(c, c ^ flip) for c in range(COLS)])
 
     chi = fold(chi, 1)
-    lad = ladder(ghi, glo, v4, (0, 1))
+    lad = ladder(ghi, glo, v4, 0)
     chi = fold(chi, 2)
-    lad = ladder(ghi, glo, v4, (2,), before=lad)
+    lad = ladder(ghi, glo, opening, 1, before=lad)
+    lad = ladder(ghi, glo, second, 2, before=lad)
     chi = fold(chi, 4)
-    lad = ladder(ghi, glo, v4, (3,), before=lad)
+    lad = ladder(ghi, glo, third, 3, before=lad)
     chi = jnp.stack([chi, hop(chi, 1, 0, 0)])
-    lad, block = ladder(ghi, glo, v4, (4,), before=lad, onehot=onehot)
-    lad, chi = lax.optimization_barrier((lad, chi))
+    lad = ladder(ghi, glo, fourth, 4, before=lad)
+    lad, chi, holes = lax.optimization_barrier((lad, chi, hole_ints))
     scattered = lax.all_to_all(lad, "col", split_axis=0, concat_axis=0, tiled=True)
 
     chi = jnp.stack([chi] + [hop(chi, 0, dz, 0) for dz in (1, 2, 3)])
     chi = jnp.stack([chi, hop(chi, 0, 0, 1)]).reshape(ROWS, NO, NO * NO)
+    block = own_block(ghi, glo, onehot)
+    bare = holes.reshape(NO * NO, NO * NO)
+    fock = jnp.tile(fock_occ, (1, NO))
     sending = post(table, scattered, chi, bare, fock, block)
     back = lax.all_to_all(sending, ("row", "col"), split_axis=0, concat_axis=0, tiled=True)
     back = back.reshape(ROWS, COLS, 2, 2, 256).transpose(2, 3, 1, 0, 4)

time: 139 us -> 134 us (0.964)
  waiting for transfers between devices: 42 us -> 29.3 us
  Pallas kernels: 40.1 us -> 47.8 us
  starting transfers between devices: 32.8 us -> 26.6 us
  local copies, waits for them, and re-layouts: 7.81 us -> 12 us
  other arithmetic: 1.64 us -> 3.95 us
    ppermute x11, waiting for transfers between devices: 18.9 us -> 9.89 us  [hop(): return lax.ppermute(value, 'row', row_perm(dy, dz, dc))]
    all_to_all x1, waiting for transfers between devices: 13.2 us -> 5.91 us  [on_device(): lax.all_to_all(lad, 'col', split_axis=0, concat_axis=0, tiled=True)]
    pallas_call x4 -> x10, Pallas kernels: 30.7 us -> 35.9 us  [the longest x4 20.2 us: split_integrals(): pl.pallas_call(functools.partial(split_kernel, group), out_shape=pltpu.HB...]
    ppermute x11, starting transfers between devices: 19.5 us -> 14.9 us  [hop(): return lax.ppermute(value, 'row', row_perm(dy, dz, dc))]
    ppermute x3, waiting for transfers between devices: 0.01 us -> 3.49 us  [fold(): lax.ppermute(value, 'col', [(c, c ^ flip) for c in range(COLS)])]
    unnamed x14 -> x32, local copies, waits for them, and re-layouts: 1 us -> 4.23 us
    another operation x2, other arithmetic: 0.04 us -> 2.45 us  [on_device(): chi = jnp.stack([chi, hop(chi, 0, 0, 1)]).reshape(ROWS, NO, NO * NO)]
    ppermute x3, starting transfers between devices: 4.18 us -> 2.58 us  [fold(): lax.ppermute(value, 'col', [(c, c ^ flip) for c in range(COLS)])]
  transfers between devices with their start and end apart: 16 -> 16, of which waited for: 9 -> 9; matrix products, arithmetic and copies ran while one was open for 5% -> 8% of each run, Pallas kernels for 22% -> 27%
where the time goes in v2:
time: 134 us; the launch traced here: 133 us
  Pallas kernels  47.8 us (36%)
  waiting for transfers between devices  29.3 us (22%)
  starting transfers between devices  26.6 us (20%)
  local copies, waits for them, and re-layouts  12 us (9%)
  blocking collectives  11.9 us (9%)
  other arithmetic  3.95 us (3%)
  matrix products  1.6 us (1%)
    pallas_call x4, Pallas kernels, split_integrals(): pl.pallas_call(functools.partial(split_kernel, group), out_shape=pltpu.HB...  20.2 us
    ppermute x11, starting transfers between devices, hop(): return lax.ppermute(value, 'row', row_perm(dy, dz, dc))  14.9 us
    pallas_call x5, Pallas kernels, ladder(): pl.pallas_call(functools.partial(ladder_kernel, group, fresh, last), out_...  14.6 us
    all_to_all x1, blocking collectives, on_device(): lax.all_to_all(packed, 'col', split_axis=0, concat_axis=0, tiled=True)  11.9 us
    all_to_all x1, waiting for transfers between devices, on_device(): lax.all_to_all(sending, ('row', 'col'), split_axis=0, concat_axis=0, tile...  9.97 us
    ppermute x11, waiting for transfers between devices, hop(): return lax.ppermute(value, 'row', row_perm(dy, dz, dc))  9.89 us
    all_to_all x1, waiting for transfers between devices, on_device(): lax.all_to_all(lad, 'col', split_axis=0, concat_axis=0, tiled=True)  5.91 us
    all_to_all x1, starting transfers between devices, on_device(): lax.all_to_all(sending, ('row', 'col'), split_axis=0, concat_axis=0, tile...  4.61 us
  transfers between devices with their start and end apart: 16, of which 9 were waited for; matrix products, arithmetic and copies ran while one was open for 8% of the time, Pallas kernels for 27%

profile of v2, /device:TPU:0, one launch (start us, length us, event | category | flops | bytes accessed | tf_op | source)
XLA Modules:
  0.0 133.5 jit_solution(2860398275393303230)
XLA Ops:
  0.0 1.8 %shard_map.82 = f32[8,2,25,128]{3,2,1,0:T(8,128)} custom-call(f32[2,160,160]{2,1,0:T(8,128)} %bitcast.64), custom_call_target="tpu_custom_call" | custom-call | bytes 600000 | tf_op jit(solution)/shard_map/pallas_call | solution.py:43
  1.8 1.1 copy.24
  3.0 11.9 %all_to_all.15 = f32[8,2,25,128]{3,1,2,0:T(2,128)S(1)} all-to-all(f32[8,2,25,128]{3,1,2,0:T(2,128)S(1)} %copy.24), channel_id=1, replica_groups=mesh['row'=16,'col'=8] {'col'}, dimensions={0} | all-to-all | bytes 409600 | tf_op jit(solution)/shard_map/all_to_all | solution.py:331
  14.9 3.0 %collective-permute-start = (f32[25,16,128]{2,1,0:T(8,128)S(1)}, f32[25,16,128]{2,1,0:T(8,128)S(1)}, u32[]{:S(2)}, u32[]{:S(2)}) collective-permute-start(f32[25,16,128]{2,1,0:T(8,128)S(1)} %bitcast.71), channel_id=1, source_target_pairs={{64,0},{72,8},{80,16},{88,24},{96,32},{104,40},{112,48},{120,56},{... | collective-permute-start | bytes 614408 | tf_op jit(solution)/shard_map/ppermute | solution.py:335
  17.9 4.9 %shard_map.83.refs_0_ = bf16[1600,1280]{1,0:T(8,128)(2,1)} custom-call(f32[10,20,160,160]{3,2,1,0:T(8,128)} %bitcast.58), custom_call_target="tpu_custom_call" | custom-call | bytes 11534336 | tf_op jit(solution)/shard_map/pallas_call | solution.py:93
  22.9 4.1 %collective-permute-start.1 = (f32[2,25,16,128]{3,2,1,0:T(8,128)S(1)}, f32[2,25,16,128]{3,2,1,0:T(8,128)S(1)}, u32[]{:S(2)}, u32[]{:S(2)}) collective-permute-start(f32[2,25,16,128]{3,2,1,0:T(8,128)S(1)} %pad_maximum_fusion.1), channel_id=1, source_target_pairs={{16,0},{24,8},{32,16},{40,24},{48,32},{56,40},{0,48},{8,56},{80,64... | collective-permute-start | bytes 1228808 | tf_op jit(solution)/shard_map/ppermute | solution.py:335
  27.0 4.9 %shard_map.84.refs_0_ = bf16[1600,1280]{1,0:T(8,128)(2,1)} custom-call(f32[10,20,160,160]{3,2,1,0:T(8,128)} %bitcast.59), custom_call_target="tpu_custom_call" | custom-call | bytes 11534336 | tf_op jit(solution)/shard_map/pallas_call | solution.py:93
  31.9 4.9 %shard_map.85.refs_0_ = bf16[1600,1280]{1,0:T(8,128)(2,1)} custom-call(f32[10,20,160,160]{3,2,1,0:T(8,128)} %bitcast.60), custom_call_target="tpu_custom_call" | custom-call | bytes 11534336 | tf_op jit(solution)/shard_map/pallas_call | solution.py:93
  37.5 2.7 %collective-permute-start.3 = (f32[25,16,128]{2,1,0:T(8,128)S(1)}, f32[25,16,128]{2,1,0:T(8,128)S(1)}, u32[]{:S(2)}, u32[]{:S(2)}) collective-permute-start(f32[25,16,128]{2,1,0:T(8,128)S(1)} %slice_bitcast_fusion.1), channel_id=1, source_target_pairs={{16,0},{24,8},{32,16},{40,24},{48,32},{56,40},{0,48},{8,56},{80,64... | collective-permute-start | bytes 614408 | tf_op jit(solution)/shard_map/ppermute | solution.py:335
  40.3 3.2 %collective-permute-done.3 = f32[25,16,128]{2,1,0:T(8,128)S(1)} collective-permute-done((f32[25,16,128]{2,1,0:T(8,128)S(1)}, f32[25,16,128]{2,1,0:T(8,128)S(1)}, u32[]{:S(2)}, u32[]{:S(2)}) %collective-permute-start.3) | collective-permute-done | bytes 204832 | tf_op jit(solution)/shard_map/ppermute | solution.py:335
  43.5 3.8 %collective-permute-done.4 = f32[25,16,128]{2,1,0:T(8,128)S(1)} collective-permute-done((f32[25,16,128]{2,1,0:T(8,128)S(1)}, f32[25,16,128]{2,1,0:T(8,128)S(1)}, u32[]{:S(2)}, u32[]{:S(2)}) %collective-permute-start.4) | collective-permute-done | bytes 204832 | tf_op jit(solution)/shard_map/ppermute | solution.py:335
  47.5 5.4 %shard_map.87.refs_0_ = bf16[1600,1280]{1,0:T(8,128)(2,1)} custom-call(f32[10,20,160,160]{3,2,1,0:T(8,128)} %bitcast.61), custom_call_target="tpu_custom_call" | custom-call | bytes 11534336 | tf_op jit(solution)/shard_map/pallas_call | solution.py:93
  53.0 1.1 copy-done.11
  54.2 4.3 %shard_map.86 = (bf16[5,256,1280]{2,1,0:T(8,128)(2,1)S(1)}, bf16[5,256,640]{2,1,0:T(8,128)(2,1)S(1)}, f32[16,256]{1,0:T(8,128)S(1)}) custom-call(s32[16]{0:T(128)S(1)} %fusion.6.tbl_ref, f32[8,25,16,128]{3,2,1,0:T(8,128)} %bitcast.63, f32[8,25,16,128]{3,2,1,0:T(8,128)} %bitcast.68, f32[20,16,160]{2,1,0:T(8,128)} %bitcast.73), custom_call_target="tpu_custom_call" | custom-call | bytes 8388608 | tf_op jit(solution)/shard_map/pallas_call | solution.py:143
  58.5 0.8 collective-permute-start.6
  59.3 5.9 %shard_map.88.refs_1_ = f32[1600,256]{1,0:T(8,128)S(1)} custom-call(bf16[5,256,1280]{2,1,0:T(8,128)(2,1)S(1)} %get-tuple-element.20.ghi, bf16[5,256,640]{2,1,0:T(8,128)(2,1)S(1)} %get-tuple-element.21.glo, f32[10,20,160,160]{3,2,1,0:T(8,128)} %bitcast.62), custom_call_target="tpu_custom_call" | custom-call | flops 1572864000 | bytes 8388608 | tf_op jit(solution)/shard_map/pallas_call | solution.py:219
  65.2 1.9 %shard_map.89.refs_1_ = f32[1600,256]{1,0:T(8,128)S(1)} custom-call(bf16[5,256,1280]{2,1,0:T(8,128)(2,1)S(1)} %get-tuple-element.20.ghi, bf16[5,256,640]{2,1,0:T(8,128)(2,1)S(1)} %get-tuple-element.21.glo, bf16[1600,1280]{1,0:T(8,128)(2,1)S(1)} %copy-done.4, f32[1600,256]{1,0:T(8,128)S(1)} %shard_map.88.refs_1_), custom_call_target="tpu_custom_call" | custom-call | flops 1572864000 | bytes 8388608 | tf_op jit(solution)/shard_map/pallas_call | solution.py:219
  67.2 0.6 collective-permute-start.7
  67.8 1.9 %shard_map.90.refs_1_ = f32[1600,256]{1,0:T(8,128)S(1)} custom-call(bf16[5,256,1280]{2,1,0:T(8,128)(2,1)S(1)} %get-tuple-element.20.ghi, bf16[5,256,640]{2,1,0:T(8,128)(2,1)S(1)} %get-tuple-element.21.glo, bf16[1600,1280]{1,0:T(8,128)(2,1)S(1)} %copy-done.5, f32[1600,256]{1,0:T(8,128)S(1)} %shard_map.89.refs_1_), custom_call_target="tpu_custom_call" | custom-call | flops 1572864000 | bytes 8388608 | tf_op jit(solution)/shard_map/pallas_call | solution.py:219
  69.7 1.3 collective-permute-done.7
  71.0 1.1 collective-permute-start.8
  72.1 1.9 %shard_map.91.refs_1_ = f32[1600,256]{1,0:T(8,128)S(1)} custom-call(bf16[5,256,1280]{2,1,0:T(8,128)(2,1)S(1)} %get-tuple-element.20.ghi, bf16[5,256,640]{2,1,0:T(8,128)(2,1)S(1)} %get-tuple-element.21.glo, bf16[1600,1280]{1,0:T(8,128)(2,1)S(1)} %copy-done.3, f32[1600,256]{1,0:T(8,128)S(1)} %shard_map.90.refs_1_), custom_call_target="tpu_custom_call" | custom-call | flops 1572864000 | bytes 8388608 | tf_op jit(solution)/shard_map/pallas_call | solution.py:219
  74.0 2.2 %collective-permute-done.8 = f32[16,256]{1,0:T(8,128)S(1)} collective-permute-done((f32[16,256]{1,0:T(8,128)S(1)}, f32[16,256]{1,0:T(8,128)S(1)}, u32[]{:S(2)}, u32[]{:S(2)}) %collective-permute-start.8) | collective-permute-done | bytes 16416 | tf_op jit(solution)/shard_map/ppermute | solution.py:367
  76.2 2.9 %collective-permute-start.9 = (f32[16,256]{1,0:T(8,128)S(1)}, f32[16,256]{1,0:T(8,128)S(1)}, u32[]{:S(2)}, u32[]{:S(2)}) collective-permute-start(f32[16,256]{1,0:T(8,128)S(1)} %add.153), channel_id=1, source_target_pairs={{64,0},{72,8},{80,16},{88,24},{96,32},{104,40},{112,48},{120,56},{... | collective-permute-start | bytes 49160 | tf_op jit(solution)/shard_map/ppermute | solution.py:335
  79.1 3.1 %shard_map.92 = f32[8,200,256]{2,1,0:T(8,128)} custom-call(bf16[5,256,1280]{2,1,0:T(8,128)(2,1)S(1)} %get-tuple-element.20.ghi, bf16[5,256,640]{2,1,0:T(8,128)(2,1)S(1)} %get-tuple-element.21.glo, bf16[1600,1280]{1,0:T(8,128)(2,1)S(1)} %copy-done.6, f32[1600,256]{1,0:T(8,128)S(1)} %shard_map.91.refs_1_), custom_call_target="tpu_custom_call" | custom-call | flops 1572864000 | bytes 8388608 | tf_op jit(solution)/shard_map/pallas_call | solution.py:219
  82.2 4.4 %all-to-all-start.1 = ((f32[8,200,256]{2,1,0:T(8,128)}), f32[8,200,256]{2,1,0:T(8,128)}, u32[]{:S(2)}, u32[]{:S(2)}) async-start(f32[8,200,256]{2,1,0:T(8,128)} %shard_map.92), calls=%async_computation.1 | async-start | bytes 3276800 | tf_op jit(solution)/shard_map/all_to_all | solution.py:379
  86.8 0.8 collective-permute-start.11
  87.6 1.2 collective-permute-start.12
  88.9 0.7 tile.4
  89.6 1.0 tile.10.f_ref
  91.2 1.2 collective-permute-done.11
  92.4 1.1 collective-permute-done.12
  93.5 1.5 %fusion.18 = (f32[1,4,2,16,256]{4,3,2,1,0:T(8,128)}, f32[4,2,16,256]{3,2,1,0:T(8,128)}) fusion(f32[1,2,16,256]{3,2,1,0:T(8,128)} %bitcast.25, f32[1,2,16,256]{3,2,1,0:T(8,128)} %bitcast.24, f32[1,2,16,256]{3,2,1,0:T(8,128)} %bitcast.23, f32[1,2,16,256]{3,2,1,0:T(8,128)S(1)} %bitcast.77), kind=kLoop, calls=%fused_computation.52 | loop fusion | flops 98304 | bytes 393216 | tf_op jit(solution)/shard_map/stack | solution.py:382
  95.0 1.4 %copy-done.2 = bf16[5,256,640]{2,1,0:T(8,128)(2,1)S(1)} copy-done((bf16[5,256,640]{2,1,0:T(8,128)(2,1)S(1)}, bf16[5,256,640]{2,1,0:T(8,128)(2,1)}, u32[]{:S(2)}) %copy-start.2) | copy-done | bytes 1638424
  96.4 1.1 shard_map.93.p_ref
  97.6 0.7 copy-done.7
  98.2 2.5 %reshape.101.w_ref = f32[256,256]{1,0:T(8,128)S(1)} reshape(f32[16,16,16,16]{3,2,1,0:T(8,128)} %param.10) | data formatting | bytes 524288 | tf_op jit(solution)/shard_map/reshape | solution.py:384
  100.7 0.9 pad_maximum_fusion.2
  101.7 5.9 %all-to-all-done.1.x_ref = f32[8,200,256]{2,1,0:T(8,128)} async-done(((f32[8,200,256]{2,1,0:T(8,128)}), f32[8,200,256]{2,1,0:T(8,128)}, u32[]{:S(2)}, u32[]{:S(2)}) %all-to-all-start.1) | async-done | bytes 1638432 | tf_op jit(solution)/shard_map/all_to_all | solution.py:379
  107.6 0.9 copy-done.8
  108.5 2.9 %shard_map.94 = f32[128,4,256]{2,1,0:T(4,128)} custom-call(s32[16]{0:T(128)S(1)} %fusion.6.tbl_ref, f32[8,200,256]{2,1,0:T(8,128)} %all-to-all-done.1.x_ref, f32[16,16,256]{2,1,0:T(8,128)S(1)} %bitcast.57, f32[256,256]{1,0:T(8,128)S(1)} %reshape.101.w_ref, f32[16,256]{1,0:T(8,128)S(1)} %tile.10.f_ref, f32[200,256]{1,0:T(8,128)S(1)} %copy-done.8), custom_call_target="tpu_custom_call" | custom-call | flops 157286400 | bytes 3145728 | tf_op jit(solution)/shard_map/pallas_call | solution.py:282
  111.4 4.6 %all-to-all-start.2 = ((f32[128,4,256]{2,1,0:T(4,128)}), f32[128,4,256]{2,1,0:T(4,128)S(1)}, u32[]{:S(2)}, u32[]{:S(2)}) async-start(f32[128,4,256]{2,1,0:T(4,128)} %shard_map.94), calls=%async_computation.2 | async-start | bytes 1048576 | tf_op jit(solution)/shard_map/all_to_all | solution.py:387
  116.1 1.2 dynamic-slice_add_fusion.e_ref
  117.2 0.8 copy.30.vcol_ref
  118.4 1.2 fusion.tf_ref
  119.6 10.0 %all-to-all-done.2 = f32[128,4,256]{2,1,0:T(4,128)S(1)} async-done(((f32[128,4,256]{2,1,0:T(4,128)}), f32[128,4,256]{2,1,0:T(4,128)S(1)}, u32[]{:S(2)}, u32[]{:S(2)}) %all-to-all-start.2) | async-done | bytes 524320 | tf_op jit(solution)/shard_map/all_to_all | solution.py:387
  129.7 0.9 copy.34
  130.6 2.9 %shard_map.95 = f32[2,160,160]{2,1,0:T(8,128)} custom-call(f32[2]{0:T(128)} %dynamic-slice_add_fusion.e_ref, f32[2,2,8,16,256]{4,3,2,1,0:T(8,128)} %bitcast.66, f32[2,160,160]{2,1,0:T(8,128)} %fusion.tf_ref, f32[1,160]{1,0:T(1,128)} %bitcast.80, f32[160,1]{1,0:T(8,128)} %copy.30.vcol_ref), custom_call_target="tpu_custom_call" | custom-call | bytes 2097152 | tf_op jit(solution)/shard_map/pallas_call | solution.py:314
  (57 shorter events, 2.5 us)
Async XLA Ops:
  0.0 118.0 %copy-start = (f32[160,160]{1,0:T(8,128)S(1)}, f32[160,160]{1,0:T(8,128)}, u32[]{:S(2)}) copy-start(f32[160,160]{1,0:T(8,128)} %param.13) | copy-start | bytes 307204
  14.9 7.9 %collective-permute-start = (f32[25,16,128]{2,1,0:T(8,128)S(1)}, f32[25,16,128]{2,1,0:T(8,128)S(1)}, u32[]{:S(2)}, u32[]{:S(2)}) collective-permute-start(f32[25,16,128]{2,1,0:T(8,128)S(1)} %bitcast.71), channel_id=1, source_target_pairs={{64,0},{72,8},{80,16},{88,24},{96,32},{104,40},{112,48},{120,56},{... | collective-permute-start | bytes 614408 | tf_op jit(solution)/shard_map/ppermute | solution.py:335
  22.9 14.0 %collective-permute-start.1 = (f32[2,25,16,128]{3,2,1,0:T(8,128)S(1)}, f32[2,25,16,128]{3,2,1,0:T(8,128)S(1)}, u32[]{:S(2)}, u32[]{:S(2)}) collective-permute-start(f32[2,25,16,128]{3,2,1,0:T(8,128)S(1)} %pad_maximum_fusion.1), channel_id=1, source_target_pairs={{16,0},{24,8},{32,16},{40,24},{48,32},{56,40},{0,48},{8,56},{80,64... | collective-permute-start | bytes 1228808 | tf_op jit(solution)/shard_map/ppermute | solution.py:335
  27.0 10.5 %collective-permute-start.2 = (f32[2,25,16,128]{3,2,1,0:T(8,128)S(1)}, f32[2,25,16,128]{3,2,1,0:T(8,128)S(1)}, u32[]{:S(2)}, u32[]{:S(2)}) collective-permute-start(f32[2,25,16,128]{3,2,1,0:T(8,128)S(1)} %pad_maximum_fusion.1), channel_id=1, source_target_pairs={{48,0},{56,8},{0,16},{8,24},{16,32},{24,40},{32,48},{40,56},{112,6... | collective-permute-start | bytes 1228808 | tf_op jit(solution)/shard_map/ppermute | solution.py:335
  37.5 6.0 %collective-permute-start.3 = (f32[25,16,128]{2,1,0:T(8,128)S(1)}, f32[25,16,128]{2,1,0:T(8,128)S(1)}, u32[]{:S(2)}, u32[]{:S(2)}) collective-permute-start(f32[25,16,128]{2,1,0:T(8,128)S(1)} %slice_bitcast_fusion.1), channel_id=1, source_target_pairs={{16,0},{24,8},{32,16},{40,24},{48,32},{56,40},{0,48},{8,56},{80,64... | collective-permute-start | bytes 614408 | tf_op jit(solution)/shard_map/ppermute | solution.py:335
  40.2 7.0 %collective-permute-start.4 = (f32[25,16,128]{2,1,0:T(8,128)S(1)}, f32[25,16,128]{2,1,0:T(8,128)S(1)}, u32[]{:S(2)}, u32[]{:S(2)}) collective-permute-start(f32[25,16,128]{2,1,0:T(8,128)S(1)} %slice_bitcast_fusion), channel_id=1, source_target_pairs={{48,0},{56,8},{0,16},{8,24},{16,32},{24,40},{32,48},{40,56},{112,6... | collective-permute-start | bytes 614408 | tf_op jit(solution)/shard_map/ppermute | solution.py:335
  47.4 5.5 %copy-start.9 = (f32[4,2,25,16,128]{4,3,2,1,0:T(8,128)}, f32[4,2,25,16,128]{4,3,2,1,0:T(8,128)S(1)}, u32[]{:S(2)}) copy-start(f32[4,2,25,16,128]{4,3,2,1,0:T(8,128)S(1)} %pad_maximum_fusion) | copy-start | bytes 4915204
  47.4 5.6 %collective-permute-start.5 = (f32[4,2,25,16,128]{4,3,2,1,0:T(8,128)S(1)}, f32[4,2,25,16,128]{4,3,2,1,0:T(8,128)S(1)}, u32[]{:S(2)}, u32[]{:S(2)}) collective-permute-start(f32[4,2,25,16,128]{4,3,2,1,0:T(8,128)S(1)} %pad_maximum_fusion), channel_id=1, source_target_pairs={{8,0},{0,8},{24,16},{16,24},{40,32},{32,40},{56,48},{48,56},{72,64... | collective-permute-start | bytes 4915208 | tf_op jit(solution)/shard_map/ppermute | solution.py:335
  53.0 1.2 copy-start.11
  58.5 20.6 %copy-start.1 = (bf16[5,256,640]{2,1,0:T(8,128)(2,1)}, bf16[5,256,640]{2,1,0:T(8,128)(2,1)S(1)}, u32[]{:S(2)}) copy-start(bf16[5,256,640]{2,1,0:T(8,128)(2,1)S(1)} %get-tuple-element.21.glo) | copy-start | bytes 4915204
  58.5 8.6 %collective-permute-start.6 = (f32[16,256]{1,0:T(8,128)S(1)}, f32[16,256]{1,0:T(8,128)S(1)}, u32[]{:S(2)}, u32[]{:S(2)}) collective-permute-start(f32[16,256]{1,0:T(8,128)S(1)} %get-tuple-element.25), channel_id=1, source_target_pairs={{0,1},{1,0},{2,3},{3,2},{4,5},{5,4},{6,7},{7,6},{8,9},{9,8},{10,11... | collective-permute-start | bytes 49160 | tf_op jit(solution)/shard_map/ppermute | solution.py:367
  59.3 5.9 %copy-start.4 = (bf16[1600,1280]{1,0:T(8,128)(2,1)S(1)}, bf16[1600,1280]{1,0:T(8,128)(2,1)}, u32[]{:S(2)}) copy-start(bf16[1600,1280]{1,0:T(8,128)(2,1)} %shard_map.83.refs_0_) | copy-start | bytes 12288004
  65.2 2.6 %copy-start.5 = (bf16[1600,1280]{1,0:T(8,128)(2,1)S(1)}, bf16[1600,1280]{1,0:T(8,128)(2,1)}, u32[]{:S(2)}) copy-start(bf16[1600,1280]{1,0:T(8,128)(2,1)} %shard_map.84.refs_0_) | copy-start | bytes 12288004
  67.2 3.8 %collective-permute-start.7 = (f32[16,256]{1,0:T(8,128)S(1)}, f32[16,256]{1,0:T(8,128)S(1)}, u32[]{:S(2)}, u32[]{:S(2)}) collective-permute-start(f32[16,256]{1,0:T(8,128)S(1)} %add.151), channel_id=1, source_target_pairs={{0,2},{1,3},{2,0},{3,1},{4,6},{5,7},{6,4},{7,5},{8,10},{9,11},{10,... | collective-permute-start | bytes 49160 | tf_op jit(solution)/shard_map/ppermute | solution.py:367
  67.8 4.3 %copy-start.3 = (bf16[1600,1280]{1,0:T(8,128)(2,1)S(1)}, bf16[1600,1280]{1,0:T(8,128)(2,1)}, u32[]{:S(2)}) copy-start(bf16[1600,1280]{1,0:T(8,128)(2,1)} %shard_map.85.refs_0_) | copy-start | bytes 12288004
  71.0 5.2 %collective-permute-start.8 = (f32[16,256]{1,0:T(8,128)S(1)}, f32[16,256]{1,0:T(8,128)S(1)}, u32[]{:S(2)}, u32[]{:S(2)}) collective-permute-start(f32[16,256]{1,0:T(8,128)S(1)} %add.152), channel_id=1, source_target_pairs={{0,4},{1,5},{2,6},{3,7},{4,0},{5,1},{6,2},{7,3},{8,12},{9,13},{10,... | collective-permute-start | bytes 49160 | tf_op jit(solution)/shard_map/ppermute | solution.py:367
  72.1 7.0 %copy-start.6 = (bf16[1600,1280]{1,0:T(8,128)(2,1)S(1)}, bf16[1600,1280]{1,0:T(8,128)(2,1)}, u32[]{:S(2)}) copy-start(bf16[1600,1280]{1,0:T(8,128)(2,1)} %shard_map.87.refs_0_) | copy-start | bytes 12288004
  76.2 6.0 %collective-permute-start.9 = (f32[16,256]{1,0:T(8,128)S(1)}, f32[16,256]{1,0:T(8,128)S(1)}, u32[]{:S(2)}, u32[]{:S(2)}) collective-permute-start(f32[16,256]{1,0:T(8,128)S(1)} %add.153), channel_id=1, source_target_pairs={{64,0},{72,8},{80,16},{88,24},{96,32},{104,40},{112,48},{120,56},{... | collective-permute-start | bytes 49160 | tf_op jit(solution)/shard_map/ppermute | solution.py:335
  82.2 6.7 %copy-start.13 = (f32[16,16]{1,0:T(8,128)S(1)}, f32[16,16]{1,0:T(8,128)}, u32[]{:S(2)}) copy-start(f32[16,16]{1,0:T(8,128)} %param.12) | copy-start | bytes 3076
  82.2 8.3 %copy-start.15 = (f32[16]{0:T(128)S(1)}, f32[16]{0:T(128)}, u32[]{:S(2)}) copy-start(f32[16]{0:T(128)} %param.14) | copy-start | bytes 196
  82.2 25.3 %all-to-all-start.1 = ((f32[8,200,256]{2,1,0:T(8,128)}), f32[8,200,256]{2,1,0:T(8,128)}, u32[]{:S(2)}, u32[]{:S(2)}) async-start(f32[8,200,256]{2,1,0:T(8,128)} %shard_map.92), calls=%async_computation.1 | async-start | bytes 3276800 | tf_op jit(solution)/shard_map/all_to_all | solution.py:379
  86.7 4.5 %collective-permute-start.10 = (f32[2,16,256]{2,1,0:T(8,128)S(1)}, f32[2,16,256]{2,1,0:T(8,128)}, u32[]{:S(2)}, u32[]{:S(2)}) collective-permute-start(f32[2,16,256]{2,1,0:T(8,128)S(1)} %pad_maximum_fusion.4), channel_id=1, source_target_pairs={{16,0},{24,8},{32,16},{40,24},{48,32},{56,40},{0,48},{8,56},{80,64... | collective-permute-start | bytes 98312 | tf_op jit(solution)/shard_map/ppermute | solution.py:335
  86.8 5.6 %collective-permute-start.11 = (f32[2,16,256]{2,1,0:T(8,128)S(1)}, f32[2,16,256]{2,1,0:T(8,128)}, u32[]{:S(2)}, u32[]{:S(2)}) collective-permute-start(f32[2,16,256]{2,1,0:T(8,128)S(1)} %pad_maximum_fusion.4), channel_id=1, source_target_pairs={{32,0},{40,8},{48,16},{56,24},{0,32},{8,40},{16,48},{24,56},{96,64... | collective-permute-start | bytes 98312 | tf_op jit(solution)/shard_map/ppermute | solution.py:335
  87.6 5.8 %collective-permute-start.12 = (f32[2,16,256]{2,1,0:T(8,128)S(1)}, f32[2,16,256]{2,1,0:T(8,128)}, u32[]{:S(2)}, u32[]{:S(2)}) collective-permute-start(f32[2,16,256]{2,1,0:T(8,128)S(1)} %pad_maximum_fusion.4), channel_id=1, source_target_pairs={{48,0},{56,8},{0,16},{8,24},{16,32},{24,40},{32,48},{40,56},{112,6... | collective-permute-start | bytes 98312 | tf_op jit(solution)/shard_map/ppermute | solution.py:335
  95.0 5.7 %collective-permute-start.13 = (f32[4,2,16,256]{3,2,1,0:T(8,128)}, f32[4,2,16,256]{3,2,1,0:T(8,128)}, u32[]{:S(2)}, u32[]{:S(2)}) collective-permute-start(f32[4,2,16,256]{3,2,1,0:T(8,128)} %get-tuple-element.30), channel_id=1, source_target_pairs={{8,0},{0,8},{24,16},{16,24},{40,32},{32,40},{56,48},{48,56},{72,64... | collective-permute-start | bytes 393224 | tf_op jit(solution)/shard_map/ppermute | solution.py:335
  95.0 1.4 %copy-start.2 = (bf16[5,256,640]{2,1,0:T(8,128)(2,1)S(1)}, bf16[5,256,640]{2,1,0:T(8,128)(2,1)}, u32[]{:S(2)}) copy-start(bf16[5,256,640]{2,1,0:T(8,128)(2,1)} %copy-done.1) | copy-start | bytes 4915204
  97.6 0.7 copy-start.7
  98.2 2.5 %copy-start.12 = (f32[1,4,2,16,256]{4,3,2,1,0:T(8,128)S(1)}, f32[1,4,2,16,256]{4,3,2,1,0:T(8,128)}, u32[]{:S(2)}) copy-start(f32[1,4,2,16,256]{4,3,2,1,0:T(8,128)} %get-tuple-element.29) | copy-start | bytes 393220
  107.6 0.9 copy-start.8
  108.5 8.7 %copy-start.14 = (f32[160]{0:T(256)S(1)}, f32[160]{0:T(256)}, u32[]{:S(2)}) copy-start(f32[160]{0:T(256)} %param.15) | copy-start | bytes 1924
  108.5 9.5 %copy-start.10 = (f32[1,2,160,160]{3,2,1,0:T(8,128)S(1)}, f32[1,2,160,160]{3,2,1,0:T(8,128)}, u32[]{:S(2)}) copy-start(f32[1,2,160,160]{3,2,1,0:T(8,128)} %param.8) | copy-start | bytes 614404
  111.4 18.1 %all-to-all-start.2 = ((f32[128,4,256]{2,1,0:T(4,128)}), f32[128,4,256]{2,1,0:T(4,128)S(1)}, u32[]{:S(2)}, u32[]{:S(2)}) async-start(f32[128,4,256]{2,1,0:T(4,128)} %shard_map.94), calls=%async_computation.2 | async-start | bytes 1048576 | tf_op jit(solution)/shard_map/all_to_all | solution.py:387

commit v3 on v2

--- a/solution.py
+++ b/solution.py
@@ -340,9 +340,10 @@
     pair, opening = lax.optimization_barrier((pair, split_integrals(v4, 1)))
     ahead = hop(pair, 0, 1, 0)
     behind = hop(pair, 0, 3, 0)
-    second, third = split_integrals(v4, 2), split_integrals(v4, 3)
-    ahead, behind, second, third = lax.optimization_barrier((ahead, behind, second, third))
-    far = jnp.stack([hop(ahead[0], 0, 1, 0), hop(behind[1], 0, 3, 0)])
+    ahead, behind, second = lax.optimization_barrier((ahead, behind, split_integrals(v4, 2)))
+    far = [hop(ahead[0], 0, 1, 0), hop(behind[1], 0, 3, 0)]
+    far, third = lax.optimization_barrier((far, split_integrals(v4, 3)))
+    far = jnp.stack(far)
     own = jnp.stack([pair, ahead, far, behind])
     other = hop(own, 0, 0, 1)
     fourth = split_integrals(v4, 4)

time: 134 us -> 131 us (0.978)
  waiting for transfers between devices: 29.3 us -> 26.4 us
  transfers between devices with their start and end apart: 16 -> 16, of which waited for: 9 -> 10; matrix products, arithmetic and copies ran while one was open for 8% -> 8% of each run, Pallas kernels for 27% -> 28%
where the time goes in v3:
time: 131 us; the launch traced here: 130 us
  Pallas kernels  47.8 us (36%)
  waiting for transfers between devices  26.4 us (20%)
  starting transfers between devices  26.2 us (20%)
  local copies, waits for them, and re-layouts  12 us (9%)
  blocking collectives  11.9 us (9%)
  other arithmetic  3.95 us (3%)
  matrix products  1.6 us (1%)
    pallas_call x4, Pallas kernels, split_integrals(): pl.pallas_call(functools.partial(split_kernel, group), out_shape=pltpu.HB...  20.2 us
    pallas_call x5, Pallas kernels, ladder(): pl.pallas_call(functools.partial(ladder_kernel, group, fresh, last), out_...  14.6 us
    ppermute x11, starting transfers between devices, hop(): return lax.ppermute(value, 'row', row_perm(dy, dz, dc))  14.1 us
    all_to_all x1, blocking collectives, on_device(): lax.all_to_all(packed, 'col', split_axis=0, concat_axis=0, tiled=True)  11.9 us
    all_to_all x1, waiting for transfers between devices, on_device(): lax.all_to_all(sending, ('row', 'col'), split_axis=0, concat_axis=0, tile...  9.96 us
    ppermute x11, waiting for transfers between devices, hop(): return lax.ppermute(value, 'row', row_perm(dy, dz, dc))  8.8 us
    all_to_all x1, waiting for transfers between devices, on_device(): lax.all_to_all(lad, 'col', split_axis=0, concat_axis=0, tiled=True)  4.73 us
    all_to_all x1, starting transfers between devices, on_device(): lax.all_to_all(sending, ('row', 'col'), split_axis=0, concat_axis=0, tile...  4.61 us
  transfers between devices with their start and end apart: 16, of which 10 were waited for; matrix products, arithmetic and copies ran while one was open for 8% of the time, Pallas kernels for 28%

profile of v3, /device:TPU:0, one launch (start us, length us, event | category | flops | bytes accessed | tf_op | source)
XLA Modules:
  0.0 130.2 jit_solution(2113579470667668570)
XLA Ops:
  0.0 1.8 %shard_map.82 = f32[8,2,25,128]{3,2,1,0:T(8,128)} custom-call(f32[2,160,160]{2,1,0:T(8,128)} %bitcast.64), custom_call_target="tpu_custom_call" | custom-call | bytes 600000 | tf_op jit(solution)/shard_map/pallas_call | solution.py:43
  1.8 1.1 copy.24
  3.0 11.9 %all_to_all.15 = f32[8,2,25,128]{3,1,2,0:T(2,128)S(1)} all-to-all(f32[8,2,25,128]{3,1,2,0:T(2,128)S(1)} %copy.24), channel_id=1, replica_groups=mesh['row'=16,'col'=8] {'col'}, dimensions={0} | all-to-all | bytes 409600 | tf_op jit(solution)/shard_map/all_to_all | solution.py:331
  14.9 3.0 %collective-permute-start = (f32[25,16,128]{2,1,0:T(8,128)S(1)}, f32[25,16,128]{2,1,0:T(8,128)S(1)}, u32[]{:S(2)}, u32[]{:S(2)}) collective-permute-start(f32[25,16,128]{2,1,0:T(8,128)S(1)} %bitcast.71), channel_id=1, source_target_pairs={{64,0},{72,8},{80,16},{88,24},{96,32},{104,40},{112,48},{120,56},{... | collective-permute-start | bytes 614408 | tf_op jit(solution)/shard_map/ppermute | solution.py:335
  17.9 4.9 %shard_map.83.refs_0_ = bf16[1600,1280]{1,0:T(8,128)(2,1)} custom-call(f32[10,20,160,160]{3,2,1,0:T(8,128)} %bitcast.58), custom_call_target="tpu_custom_call" | custom-call | bytes 11534336 | tf_op jit(solution)/shard_map/pallas_call | solution.py:93
  22.9 4.1 %collective-permute-start.1 = (f32[2,25,16,128]{3,2,1,0:T(8,128)S(1)}, f32[2,25,16,128]{3,2,1,0:T(8,128)S(1)}, u32[]{:S(2)}, u32[]{:S(2)}) collective-permute-start(f32[2,25,16,128]{3,2,1,0:T(8,128)S(1)} %pad_maximum_fusion.1), channel_id=1, source_target_pairs={{16,0},{24,8},{32,16},{40,24},{48,32},{56,40},{0,48},{8,56},{80,64... | collective-permute-start | bytes 1228808 | tf_op jit(solution)/shard_map/ppermute | solution.py:335
  27.0 4.9 %shard_map.84.refs_0_ = bf16[1600,1280]{1,0:T(8,128)(2,1)} custom-call(f32[10,20,160,160]{3,2,1,0:T(8,128)} %bitcast.59), custom_call_target="tpu_custom_call" | custom-call | bytes 11534336 | tf_op jit(solution)/shard_map/pallas_call | solution.py:93
  31.9 2.1 %collective-permute-done.1 = f32[2,25,16,128]{3,2,1,0:T(8,128)S(1)} collective-permute-done((f32[2,25,16,128]{3,2,1,0:T(8,128)S(1)}, f32[2,25,16,128]{3,2,1,0:T(8,128)S(1)}, u32[]{:S(2)}, u32[]{:S(2)}) %collective-permute-start.1) | collective-permute-done | bytes 409632 | tf_op jit(solution)/shard_map/ppermute | solution.py:335
  34.1 3.4 %collective-permute-done.2 = f32[2,25,16,128]{3,2,1,0:T(8,128)S(1)} collective-permute-done((f32[2,25,16,128]{3,2,1,0:T(8,128)S(1)}, f32[2,25,16,128]{3,2,1,0:T(8,128)S(1)}, u32[]{:S(2)}, u32[]{:S(2)}) %collective-permute-start.2) | collective-permute-done | bytes 409632 | tf_op jit(solution)/shard_map/ppermute | solution.py:335
  37.9 1.8 %collective-permute-start.4 = (f32[25,16,128]{2,1,0:T(8,128)S(1)}, f32[25,16,128]{2,1,0:T(8,128)S(1)}, u32[]{:S(2)}, u32[]{:S(2)}) collective-permute-start(f32[25,16,128]{2,1,0:T(8,128)S(1)} %slice_bitcast_fusion), channel_id=1, source_target_pairs={{48,0},{56,8},{0,16},{8,24},{16,32},{24,40},{32,48},{40,56},{112,6... | collective-permute-start | bytes 614408 | tf_op jit(solution)/shard_map/ppermute | solution.py:335
  39.7 4.9 %shard_map.85.refs_0_ = bf16[1600,1280]{1,0:T(8,128)(2,1)} custom-call(f32[10,20,160,160]{3,2,1,0:T(8,128)} %bitcast.60), custom_call_target="tpu_custom_call" | custom-call | bytes 11534336 | tf_op jit(solution)/shard_map/pallas_call | solution.py:93
  45.2 5.4 %shard_map.87.refs_0_ = bf16[1600,1280]{1,0:T(8,128)(2,1)} custom-call(f32[10,20,160,160]{3,2,1,0:T(8,128)} %bitcast.61), custom_call_target="tpu_custom_call" | custom-call | bytes 11534336 | tf_op jit(solution)/shard_map/pallas_call | solution.py:93
  50.7 1.1 copy-done.11
  51.8 4.3 %shard_map.86 = (bf16[5,256,1280]{2,1,0:T(8,128)(2,1)S(1)}, bf16[5,256,640]{2,1,0:T(8,128)(2,1)S(1)}, f32[16,256]{1,0:T(8,128)S(1)}) custom-call(s32[16]{0:T(128)S(1)} %fusion.6.tbl_ref, f32[8,25,16,128]{3,2,1,0:T(8,128)} %bitcast.63, f32[8,25,16,128]{3,2,1,0:T(8,128)} %bitcast.68, f32[20,16,160]{2,1,0:T(8,128)} %bitcast.73), custom_call_target="tpu_custom_call" | custom-call | bytes 8388608 | tf_op jit(solution)/shard_map/pallas_call | solution.py:143
  56.2 0.7 collective-permute-start.6
  56.9 5.9 %shard_map.88.refs_1_ = f32[1600,256]{1,0:T(8,128)S(1)} custom-call(bf16[5,256,1280]{2,1,0:T(8,128)(2,1)S(1)} %get-tuple-element.24.ghi, bf16[5,256,640]{2,1,0:T(8,128)(2,1)S(1)} %get-tuple-element.25.glo, f32[10,20,160,160]{3,2,1,0:T(8,128)} %bitcast.62), custom_call_target="tpu_custom_call" | custom-call | flops 1572864000 | bytes 8388608 | tf_op jit(solution)/shard_map/pallas_call | solution.py:219
  62.8 1.9 %shard_map.89.refs_1_ = f32[1600,256]{1,0:T(8,128)S(1)} custom-call(bf16[5,256,1280]{2,1,0:T(8,128)(2,1)S(1)} %get-tuple-element.24.ghi, bf16[5,256,640]{2,1,0:T(8,128)(2,1)S(1)} %get-tuple-element.25.glo, bf16[1600,1280]{1,0:T(8,128)(2,1)S(1)} %copy-done.3, f32[1600,256]{1,0:T(8,128)S(1)} %shard_map.88.refs_1_), custom_call_target="tpu_custom_call" | custom-call | flops 1572864000 | bytes 8388608 | tf_op jit(solution)/shard_map/pallas_call | solution.py:219
  64.7 0.9 collective-permute-start.7
  65.7 1.9 %shard_map.90.refs_1_ = f32[1600,256]{1,0:T(8,128)S(1)} custom-call(bf16[5,256,1280]{2,1,0:T(8,128)(2,1)S(1)} %get-tuple-element.24.ghi, bf16[5,256,640]{2,1,0:T(8,128)(2,1)S(1)} %get-tuple-element.25.glo, bf16[1600,1280]{1,0:T(8,128)(2,1)S(1)} %copy-done.4, f32[1600,256]{1,0:T(8,128)S(1)} %shard_map.89.refs_1_), custom_call_target="tpu_custom_call" | custom-call | flops 1572864000 | bytes 8388608 | tf_op jit(solution)/shard_map/pallas_call | solution.py:219
  67.6 1.0 collective-permute-done.7
  68.5 1.4 %collective-permute-start.8 = (f32[16,256]{1,0:T(8,128)S(1)}, f32[16,256]{1,0:T(8,128)S(1)}, u32[]{:S(2)}, u32[]{:S(2)}) collective-permute-start(f32[16,256]{1,0:T(8,128)S(1)} %add.152), channel_id=1, source_target_pairs={{0,4},{1,5},{2,6},{3,7},{4,0},{5,1},{6,2},{7,3},{8,12},{9,13},{10,... | collective-permute-start | bytes 49160 | tf_op jit(solution)/shard_map/ppermute | solution.py:368
  70.0 1.9 %shard_map.91.refs_1_ = f32[1600,256]{1,0:T(8,128)S(1)} custom-call(bf16[5,256,1280]{2,1,0:T(8,128)(2,1)S(1)} %get-tuple-element.24.ghi, bf16[5,256,640]{2,1,0:T(8,128)(2,1)S(1)} %get-tuple-element.25.glo, bf16[1600,1280]{1,0:T(8,128)(2,1)S(1)} %copy-done.5, f32[1600,256]{1,0:T(8,128)S(1)} %shard_map.90.refs_1_), custom_call_target="tpu_custom_call" | custom-call | flops 1572864000 | bytes 8388608 | tf_op jit(solution)/shard_map/pallas_call | solution.py:219
  71.9 1.9 %collective-permute-done.8 = f32[16,256]{1,0:T(8,128)S(1)} collective-permute-done((f32[16,256]{1,0:T(8,128)S(1)}, f32[16,256]{1,0:T(8,128)S(1)}, u32[]{:S(2)}, u32[]{:S(2)}) %collective-permute-start.8) | collective-permute-done | bytes 16416 | tf_op jit(solution)/shard_map/ppermute | solution.py:368
  73.8 2.1 %collective-permute-start.9 = (f32[16,256]{1,0:T(8,128)S(1)}, f32[16,256]{1,0:T(8,128)S(1)}, u32[]{:S(2)}, u32[]{:S(2)}) collective-permute-start(f32[16,256]{1,0:T(8,128)S(1)} %add.153), channel_id=1, source_target_pairs={{64,0},{72,8},{80,16},{88,24},{96,32},{104,40},{112,48},{120,56},{... | collective-permute-start | bytes 49160 | tf_op jit(solution)/shard_map/ppermute | solution.py:335
  75.9 3.1 %shard_map.92 = f32[8,200,256]{2,1,0:T(8,128)} custom-call(bf16[5,256,1280]{2,1,0:T(8,128)(2,1)S(1)} %get-tuple-element.24.ghi, bf16[5,256,640]{2,1,0:T(8,128)(2,1)S(1)} %get-tuple-element.25.glo, bf16[1600,1280]{1,0:T(8,128)(2,1)S(1)} %copy-done.6, f32[1600,256]{1,0:T(8,128)S(1)} %shard_map.91.refs_1_), custom_call_target="tpu_custom_call" | custom-call | flops 1572864000 | bytes 8388608 | tf_op jit(solution)/shard_map/pallas_call | solution.py:219
  79.0 4.4 %all-to-all-start.1 = ((f32[8,200,256]{2,1,0:T(8,128)}), f32[8,200,256]{2,1,0:T(8,128)}, u32[]{:S(2)}, u32[]{:S(2)}) async-start(f32[8,200,256]{2,1,0:T(8,128)} %shard_map.92), calls=%async_computation.1 | async-start | bytes 3276800 | tf_op jit(solution)/shard_map/all_to_all | solution.py:380
  83.5 1.3 collective-permute-start.10
  84.8 1.4 %collective-permute-start.11 = (f32[2,16,256]{2,1,0:T(8,128)S(1)}, f32[2,16,256]{2,1,0:T(8,128)}, u32[]{:S(2)}, u32[]{:S(2)}) collective-permute-start(f32[2,16,256]{2,1,0:T(8,128)S(1)} %pad_maximum_fusion.4), channel_id=1, source_target_pairs={{32,0},{40,8},{48,16},{56,24},{0,32},{8,40},{16,48},{24,56},{96,64... | collective-permute-start | bytes 98312 | tf_op jit(solution)/shard_map/ppermute | solution.py:335
  86.3 0.7 tile.4
  86.9 1.0 tile.10.f_ref
  88.5 1.8 %collective-permute-done.11 = f32[2,16,256]{2,1,0:T(8,128)} collective-permute-done((f32[2,16,256]{2,1,0:T(8,128)S(1)}, f32[2,16,256]{2,1,0:T(8,128)}, u32[]{:S(2)}, u32[]{:S(2)}) %collective-permute-start.11) | collective-permute-done | bytes 32800 | tf_op jit(solution)/shard_map/ppermute | solution.py:335
  90.3 1.1 collective-permute-done.12
  91.4 1.5 %fusion.18 = (f32[1,4,2,16,256]{4,3,2,1,0:T(8,128)}, f32[4,2,16,256]{3,2,1,0:T(8,128)}) fusion(f32[1,2,16,256]{3,2,1,0:T(8,128)} %bitcast.25, f32[1,2,16,256]{3,2,1,0:T(8,128)} %bitcast.24, f32[1,2,16,256]{3,2,1,0:T(8,128)} %bitcast.23, f32[1,2,16,256]{3,2,1,0:T(8,128)S(1)} %bitcast.77), kind=kLoop, calls=%fused_computation.52 | loop fusion | flops 98304 | bytes 393216 | tf_op jit(solution)/shard_map/stack | solution.py:383
  92.9 1.4 %copy-done.2 = bf16[5,256,640]{2,1,0:T(8,128)(2,1)S(1)} copy-done((bf16[5,256,640]{2,1,0:T(8,128)(2,1)S(1)}, bf16[5,256,640]{2,1,0:T(8,128)(2,1)}, u32[]{:S(2)}) %copy-start.2) | copy-done | bytes 1638424
  94.4 1.1 shard_map.93.p_ref
  95.5 0.7 copy-done.7
  96.2 2.5 %reshape.101.w_ref = f32[256,256]{1,0:T(8,128)S(1)} reshape(f32[16,16,16,16]{3,2,1,0:T(8,128)} %param.10) | data formatting | bytes 524288 | tf_op jit(solution)/shard_map/reshape | solution.py:385
  98.7 0.9 pad_maximum_fusion.2
  99.6 4.7 %all-to-all-done.1.x_ref = f32[8,200,256]{2,1,0:T(8,128)} async-done(((f32[8,200,256]{2,1,0:T(8,128)}), f32[8,200,256]{2,1,0:T(8,128)}, u32[]{:S(2)}, u32[]{:S(2)}) %all-to-all-start.1) | async-done | bytes 1638432 | tf_op jit(solution)/shard_map/all_to_all | solution.py:380
  104.3 0.9 copy-done.8
  105.3 2.9 %shard_map.94 = f32[128,4,256]{2,1,0:T(4,128)} custom-call(s32[16]{0:T(128)S(1)} %fusion.6.tbl_ref, f32[8,200,256]{2,1,0:T(8,128)} %all-to-all-done.1.x_ref, f32[16,16,256]{2,1,0:T(8,128)S(1)} %bitcast.57, f32[256,256]{1,0:T(8,128)S(1)} %reshape.101.w_ref, f32[16,256]{1,0:T(8,128)S(1)} %tile.10.f_ref, f32[200,256]{1,0:T(8,128)S(1)} %copy-done.8), custom_call_target="tpu_custom_call" | custom-call | flops 157286400 | bytes 3145728 | tf_op jit(solution)/shard_map/pallas_call | solution.py:282
  108.2 4.6 %all-to-all-start.2 = ((f32[128,4,256]{2,1,0:T(4,128)}), f32[128,4,256]{2,1,0:T(4,128)S(1)}, u32[]{:S(2)}, u32[]{:S(2)}) async-start(f32[128,4,256]{2,1,0:T(4,128)} %shard_map.94), calls=%async_computation.2 | async-start | bytes 1048576 | tf_op jit(solution)/shard_map/all_to_all | solution.py:388
  112.8 1.2 dynamic-slice_add_fusion.e_ref
  114.0 0.8 copy.30.vcol_ref
  115.2 1.2 fusion.tf_ref
  116.3 10.0 %all-to-all-done.2 = f32[128,4,256]{2,1,0:T(4,128)S(1)} async-done(((f32[128,4,256]{2,1,0:T(4,128)}), f32[128,4,256]{2,1,0:T(4,128)S(1)}, u32[]{:S(2)}, u32[]{:S(2)}) %all-to-all-start.2) | async-done | bytes 524320 | tf_op jit(solution)/shard_map/all_to_all | solution.py:388
  126.4 0.9 copy.34
  127.4 2.9 %shard_map.95 = f32[2,160,160]{2,1,0:T(8,128)} custom-call(f32[2]{0:T(128)} %dynamic-slice_add_fusion.e_ref, f32[2,2,8,16,256]{4,3,2,1,0:T(8,128)} %bitcast.66, f32[2,160,160]{2,1,0:T(8,128)} %fusion.tf_ref, f32[1,160]{1,0:T(1,128)} %bitcast.80, f32[160,1]{1,0:T(8,128)} %copy.30.vcol_ref), custom_call_target="tpu_custom_call" | custom-call | bytes 2097152 | tf_op jit(solution)/shard_map/pallas_call | solution.py:314
  (57 shorter events, 2.4 us)
Async XLA Ops:
  0.0 114.7 %copy-start = (f32[160,160]{1,0:T(8,128)S(1)}, f32[160,160]{1,0:T(8,128)}, u32[]{:S(2)}) copy-start(f32[160,160]{1,0:T(8,128)} %param.13) | copy-start | bytes 307204
  14.9 7.9 %collective-permute-start = (f32[25,16,128]{2,1,0:T(8,128)S(1)}, f32[25,16,128]{2,1,0:T(8,128)S(1)}, u32[]{:S(2)}, u32[]{:S(2)}) collective-permute-start(f32[25,16,128]{2,1,0:T(8,128)S(1)} %bitcast.71), channel_id=1, source_target_pairs={{64,0},{72,8},{80,16},{88,24},{96,32},{104,40},{112,48},{120,56},{... | collective-permute-start | bytes 614408 | tf_op jit(solution)/shard_map/ppermute | solution.py:335
  22.9 11.2 %collective-permute-start.1 = (f32[2,25,16,128]{3,2,1,0:T(8,128)S(1)}, f32[2,25,16,128]{3,2,1,0:T(8,128)S(1)}, u32[]{:S(2)}, u32[]{:S(2)}) collective-permute-start(f32[2,25,16,128]{3,2,1,0:T(8,128)S(1)} %pad_maximum_fusion.1), channel_id=1, source_target_pairs={{16,0},{24,8},{32,16},{40,24},{48,32},{56,40},{0,48},{8,56},{80,64... | collective-permute-start | bytes 1228808 | tf_op jit(solution)/shard_map/ppermute | solution.py:335
  27.0 10.5 %collective-permute-start.2 = (f32[2,25,16,128]{3,2,1,0:T(8,128)S(1)}, f32[2,25,16,128]{3,2,1,0:T(8,128)S(1)}, u32[]{:S(2)}, u32[]{:S(2)}) collective-permute-start(f32[2,25,16,128]{3,2,1,0:T(8,128)S(1)} %pad_maximum_fusion.1), channel_id=1, source_target_pairs={{48,0},{56,8},{0,16},{8,24},{16,32},{24,40},{32,48},{40,56},{112,6... | collective-permute-start | bytes 1228808 | tf_op jit(solution)/shard_map/ppermute | solution.py:335
  37.5 7.1 %collective-permute-start.3 = (f32[25,16,128]{2,1,0:T(8,128)S(1)}, f32[25,16,128]{2,1,0:T(8,128)S(1)}, u32[]{:S(2)}, u32[]{:S(2)}) collective-permute-start(f32[25,16,128]{2,1,0:T(8,128)S(1)} %slice_bitcast_fusion.1), channel_id=1, source_target_pairs={{16,0},{24,8},{32,16},{40,24},{48,32},{56,40},{0,48},{8,56},{80,64... | collective-permute-start | bytes 614408 | tf_op jit(solution)/shard_map/ppermute | solution.py:335
  37.9 7.0 %collective-permute-start.4 = (f32[25,16,128]{2,1,0:T(8,128)S(1)}, f32[25,16,128]{2,1,0:T(8,128)S(1)}, u32[]{:S(2)}, u32[]{:S(2)}) collective-permute-start(f32[25,16,128]{2,1,0:T(8,128)S(1)} %slice_bitcast_fusion), channel_id=1, source_target_pairs={{48,0},{56,8},{0,16},{8,24},{16,32},{24,40},{32,48},{40,56},{112,6... | collective-permute-start | bytes 614408 | tf_op jit(solution)/shard_map/ppermute | solution.py:335
  45.1 5.5 %copy-start.9 = (f32[4,2,25,16,128]{4,3,2,1,0:T(8,128)}, f32[4,2,25,16,128]{4,3,2,1,0:T(8,128)S(1)}, u32[]{:S(2)}) copy-start(f32[4,2,25,16,128]{4,3,2,1,0:T(8,128)S(1)} %pad_maximum_fusion) | copy-start | bytes 4915204
  45.1 5.6 %collective-permute-start.5 = (f32[4,2,25,16,128]{4,3,2,1,0:T(8,128)S(1)}, f32[4,2,25,16,128]{4,3,2,1,0:T(8,128)S(1)}, u32[]{:S(2)}, u32[]{:S(2)}) collective-permute-start(f32[4,2,25,16,128]{4,3,2,1,0:T(8,128)S(1)} %pad_maximum_fusion), channel_id=1, source_target_pairs={{8,0},{0,8},{24,16},{16,24},{40,32},{32,40},{56,48},{48,56},{72,64... | collective-permute-start | bytes 4915208 | tf_op jit(solution)/shard_map/ppermute | solution.py:335
  50.7 1.2 copy-start.11
  56.2 19.7 %copy-start.1 = (bf16[5,256,640]{2,1,0:T(8,128)(2,1)}, bf16[5,256,640]{2,1,0:T(8,128)(2,1)S(1)}, u32[]{:S(2)}) copy-start(bf16[5,256,640]{2,1,0:T(8,128)(2,1)S(1)} %get-tuple-element.25.glo) | copy-start | bytes 4915204
  56.2 8.5 %collective-permute-start.6 = (f32[16,256]{1,0:T(8,128)S(1)}, f32[16,256]{1,0:T(8,128)S(1)}, u32[]{:S(2)}, u32[]{:S(2)}) collective-permute-start(f32[16,256]{1,0:T(8,128)S(1)} %get-tuple-element.29), channel_id=1, source_target_pairs={{0,1},{1,0},{2,3},{3,2},{4,5},{5,4},{6,7},{7,6},{8,9},{9,8},{10,11... | collective-permute-start | bytes 49160 | tf_op jit(solution)/shard_map/ppermute | solution.py:368
  56.9 5.9 %copy-start.3 = (bf16[1600,1280]{1,0:T(8,128)(2,1)S(1)}, bf16[1600,1280]{1,0:T(8,128)(2,1)}, u32[]{:S(2)}) copy-start(bf16[1600,1280]{1,0:T(8,128)(2,1)} %shard_map.83.refs_0_) | copy-start | bytes 12288004
  62.8 2.9 %copy-start.4 = (bf16[1600,1280]{1,0:T(8,128)(2,1)S(1)}, bf16[1600,1280]{1,0:T(8,128)(2,1)}, u32[]{:S(2)}) copy-start(bf16[1600,1280]{1,0:T(8,128)(2,1)} %shard_map.84.refs_0_) | copy-start | bytes 12288004
  64.7 3.8 %collective-permute-start.7 = (f32[16,256]{1,0:T(8,128)S(1)}, f32[16,256]{1,0:T(8,128)S(1)}, u32[]{:S(2)}, u32[]{:S(2)}) collective-permute-start(f32[16,256]{1,0:T(8,128)S(1)} %add.151), channel_id=1, source_target_pairs={{0,2},{1,3},{2,0},{3,1},{4,6},{5,7},{6,4},{7,5},{8,10},{9,11},{10,... | collective-permute-start | bytes 49160 | tf_op jit(solution)/shard_map/ppermute | solution.py:368
  65.6 4.3 %copy-start.5 = (bf16[1600,1280]{1,0:T(8,128)(2,1)S(1)}, bf16[1600,1280]{1,0:T(8,128)(2,1)}, u32[]{:S(2)}) copy-start(bf16[1600,1280]{1,0:T(8,128)(2,1)} %shard_map.85.refs_0_) | copy-start | bytes 12288004
  68.5 5.2 %collective-permute-start.8 = (f32[16,256]{1,0:T(8,128)S(1)}, f32[16,256]{1,0:T(8,128)S(1)}, u32[]{:S(2)}, u32[]{:S(2)}) collective-permute-start(f32[16,256]{1,0:T(8,128)S(1)} %add.152), channel_id=1, source_target_pairs={{0,4},{1,5},{2,6},{3,7},{4,0},{5,1},{6,2},{7,3},{8,12},{9,13},{10,... | collective-permute-start | bytes 49160 | tf_op jit(solution)/shard_map/ppermute | solution.py:368
  70.0 5.9 %copy-start.6 = (bf16[1600,1280]{1,0:T(8,128)(2,1)S(1)}, bf16[1600,1280]{1,0:T(8,128)(2,1)}, u32[]{:S(2)}) copy-start(bf16[1600,1280]{1,0:T(8,128)(2,1)} %shard_map.87.refs_0_) | copy-start | bytes 12288004
  73.8 5.2 %collective-permute-start.9 = (f32[16,256]{1,0:T(8,128)S(1)}, f32[16,256]{1,0:T(8,128)S(1)}, u32[]{:S(2)}, u32[]{:S(2)}) collective-permute-start(f32[16,256]{1,0:T(8,128)S(1)} %add.153), channel_id=1, source_target_pairs={{64,0},{72,8},{80,16},{88,24},{96,32},{104,40},{112,48},{120,56},{... | collective-permute-start | bytes 49160 | tf_op jit(solution)/shard_map/ppermute | solution.py:335
  79.0 7.2 %copy-start.13 = (f32[16,16]{1,0:T(8,128)S(1)}, f32[16,16]{1,0:T(8,128)}, u32[]{:S(2)}) copy-start(f32[16,16]{1,0:T(8,128)} %param.12) | copy-start | bytes 3076
  79.0 8.9 %copy-start.15 = (f32[16]{0:T(128)S(1)}, f32[16]{0:T(128)}, u32[]{:S(2)}) copy-start(f32[16]{0:T(128)} %param.14) | copy-start | bytes 196
  79.0 25.3 %all-to-all-start.1 = ((f32[8,200,256]{2,1,0:T(8,128)}), f32[8,200,256]{2,1,0:T(8,128)}, u32[]{:S(2)}, u32[]{:S(2)}) async-start(f32[8,200,256]{2,1,0:T(8,128)} %shard_map.92), calls=%async_computation.1 | async-start | bytes 3276800 | tf_op jit(solution)/shard_map/all_to_all | solution.py:380
  83.5 5.0 %collective-permute-start.10 = (f32[2,16,256]{2,1,0:T(8,128)S(1)}, f32[2,16,256]{2,1,0:T(8,128)}, u32[]{:S(2)}, u32[]{:S(2)}) collective-permute-start(f32[2,16,256]{2,1,0:T(8,128)S(1)} %pad_maximum_fusion.4), channel_id=1, source_target_pairs={{16,0},{24,8},{32,16},{40,24},{48,32},{56,40},{0,48},{8,56},{80,64... | collective-permute-start | bytes 98312 | tf_op jit(solution)/shard_map/ppermute | solution.py:335
  84.8 5.5 %collective-permute-start.11 = (f32[2,16,256]{2,1,0:T(8,128)S(1)}, f32[2,16,256]{2,1,0:T(8,128)}, u32[]{:S(2)}, u32[]{:S(2)}) collective-permute-start(f32[2,16,256]{2,1,0:T(8,128)S(1)} %pad_maximum_fusion.4), channel_id=1, source_target_pairs={{32,0},{40,8},{48,16},{56,24},{0,32},{8,40},{16,48},{24,56},{96,64... | collective-permute-start | bytes 98312 | tf_op jit(solution)/shard_map/ppermute | solution.py:335
  86.2 5.2 %collective-permute-start.12 = (f32[2,16,256]{2,1,0:T(8,128)S(1)}, f32[2,16,256]{2,1,0:T(8,128)}, u32[]{:S(2)}, u32[]{:S(2)}) collective-permute-start(f32[2,16,256]{2,1,0:T(8,128)S(1)} %pad_maximum_fusion.4), channel_id=1, source_target_pairs={{48,0},{56,8},{0,16},{8,24},{16,32},{24,40},{32,48},{40,56},{112,6... | collective-permute-start | bytes 98312 | tf_op jit(solution)/shard_map/ppermute | solution.py:335
  92.9 5.7 %collective-permute-start.13 = (f32[4,2,16,256]{3,2,1,0:T(8,128)}, f32[4,2,16,256]{3,2,1,0:T(8,128)}, u32[]{:S(2)}, u32[]{:S(2)}) collective-permute-start(f32[4,2,16,256]{3,2,1,0:T(8,128)} %get-tuple-element.34), channel_id=1, source_target_pairs={{8,0},{0,8},{24,16},{16,24},{40,32},{32,40},{56,48},{48,56},{72,64... | collective-permute-start | bytes 393224 | tf_op jit(solution)/shard_map/ppermute | solution.py:335
  92.9 1.4 %copy-start.2 = (bf16[5,256,640]{2,1,0:T(8,128)(2,1)S(1)}, bf16[5,256,640]{2,1,0:T(8,128)(2,1)}, u32[]{:S(2)}) copy-start(bf16[5,256,640]{2,1,0:T(8,128)(2,1)} %copy-done.1) | copy-start | bytes 4915204
  95.5 0.7 copy-start.7
  96.2 2.5 %copy-start.12 = (f32[1,4,2,16,256]{4,3,2,1,0:T(8,128)S(1)}, f32[1,4,2,16,256]{4,3,2,1,0:T(8,128)}, u32[]{:S(2)}) copy-start(f32[1,4,2,16,256]{4,3,2,1,0:T(8,128)} %get-tuple-element.33) | copy-start | bytes 393220
  104.3 0.9 copy-start.8
  105.2 8.7 %copy-start.14 = (f32[160]{0:T(256)S(1)}, f32[160]{0:T(256)}, u32[]{:S(2)}) copy-start(f32[160]{0:T(256)} %param.15) | copy-start | bytes 1924
  105.3 9.5 %copy-start.10 = (f32[1,2,160,160]{3,2,1,0:T(8,128)S(1)}, f32[1,2,160,160]{3,2,1,0:T(8,128)}, u32[]{:S(2)}) copy-start(f32[1,2,160,160]{3,2,1,0:T(8,128)} %param.8) | copy-start | bytes 614404
  108.2 18.1 %all-to-all-start.2 = ((f32[128,4,256]{2,1,0:T(4,128)}), f32[128,4,256]{2,1,0:T(4,128)S(1)}, u32[]{:S(2)}, u32[]{:S(2)}) async-start(f32[128,4,256]{2,1,0:T(4,128)} %shard_map.94), calls=%async_computation.2 | async-start | bytes 1048576 | tf_op jit(solution)/shard_map/all_to_all | solution.py:388

commit v4 on v3

--- a/solution.py
+++ b/solution.py
@@ -161,33 +161,12 @@
     )(tbl, s, q, k)
 
 
-def ladder_kernel(group, fresh, last, ghi, glo, *refs):
-    refs = list(refs)
-    v_hbm = refs.pop(0) if fresh else None
-    ready = None if fresh else refs.pop(0)
-    before = None if fresh else refs.pop(0)
-    out = refs.pop(0)
-    if fresh:
-        buf, parts, sem = refs
-        copies = []
-        for n in range(2):
-            source = v_hbm.at[pl.ds(n * (AB // 2), AB // 2), pl.ds(0, 4)]
-            copies.append(pltpu.make_async_copy(source, buf.at[n], sem.at[n]))
-            copies[-1].start()
-        for n in range(2):
-            copies[n].wait()
-            for a in range(AB // 2):
-
-                def store(lanes, value, n=n, a=a):
-                    parts[n, a * NV : (a + 1) * NV, lanes] = value
-
-                convert_block(lambda cc, lanes, n=n, a=a: buf[n, a, cc, :, lanes], store)
-            part = dot_nt(parts[n], ghi[0]) + dot_nt(parts[n, :, 0:640], glo[0])
-            out[n * HALF : (n + 1) * HALF, :] = part
-        return
-    total = before[...] + dot_nt(ready[...], ghi[group])
-    total = total + dot_nt(ready[:, 0:640], glo[group])
-    if not last:
+def ladder_kernel(group, ghi, glo, ready, *refs):
+    out = refs[-1]
+    total = dot_nt(ready[...], ghi[group]) + dot_nt(ready[:, 0:640], glo[group])
+    if group > 0:
+        total = total + refs[0][...]
+    if group < 4:
         out[...] = total
         return
     for a in range(AB):
@@ -197,36 +176,24 @@
 
 
 def ladder(ghi, glo, source, group, before=None):
-    fresh, last = before is None, group == 4
     operands = [ghi, glo, source]
-    in_specs = [VMEM, VMEM, pl.BlockSpec(memory_space=pltpu.HBM) if fresh else VMEM]
-    if not fresh:
+    if group > 0:
         operands.append(before)
-        in_specs.append(VMEM)
-    scratch = []
-    if fresh:
-        scratch = [
-            pltpu.VMEM((2, AB // 2, 4, NV, NV), jnp.float32),
-            pltpu.VMEM((2, HALF, 1280), jnp.bfloat16),
-            pltpu.SemaphoreType.DMA((2,)),
-        ]
-    if last:
-        out_shape = pltpu.HBM((COLS, AB * CB, NO * NO), jnp.float32)
-        out_specs = pl.BlockSpec((COLS, AB * CB, NO * NO), lambda: (0, 0, 0))
+    if group == 4:
+        shape = (COLS, AB * CB, NO * NO)
+        out_shape = pltpu.HBM(shape, jnp.float32)
+        out_specs = pl.BlockSpec(shape, lambda: (0, 0, 0))
     else:
         out_shape = pltpu.VMEM((VROWS, NO * NO), jnp.float32)
         out_specs = VMEM
     return pl.pallas_call(
-        functools.partial(ladder_kernel, group, fresh, last),
+        functools.partial(ladder_kernel, group),
         out_shape=out_shape,
-        in_specs=in_specs,
+        in_specs=[VMEM] * len(operands),
         out_specs=out_specs,
-        scratch_shapes=scratch,
-        compiler_params=pltpu.CompilerParams(vmem_limit_bytes=(14 if fresh else 11) << 20),
+        compiler_params=pltpu.CompilerParams(vmem_limit_bytes=11 << 20),
         cost_estimate=pl.CostEstimate(
-            flops=3 * 2 * 1600 * 640 * 256,
-            bytes_accessed=8 << 20,
-            transcendentals=0,
+            flops=3 * 2 * 1600 * 640 * 256, bytes_accessed=8 << 20, transcendentals=0
         ),
     )(*operands)
 
@@ -329,12 +296,13 @@
     t = amplitudes[0]
     packed = pack(t)
     arrived = lax.all_to_all(packed, "col", split_axis=0, concat_axis=0, tiled=True)
+    v4 = pltpu.with_memory_space_constraint(vvvv.transpose(0, 2, 1, 3), pltpu.HBM)
+    arrived, zero = lax.optimization_barrier((arrived, split_integrals(v4, 0)))
     x = arrived.reshape(NO, KT, 128).transpose(1, 0, 2)
 
     def hop(value, dy, dz, dc):
         return lax.ppermute(value, "row", row_perm(dy, dz, dc))
 
-    v4 = pltpu.with_memory_space_constraint(vvvv.transpose(0, 2, 1, 3), pltpu.HBM)
     k4 = exchange_ints[0].transpose(1, 0, 2)
     pair = jnp.stack([x, hop(x, 1, 0, 0)])
     pair, opening = lax.optimization_barrier((pair, split_integrals(v4, 1)))
@@ -368,7 +336,7 @@
         return value + lax.ppermute(value, "col", [(c, c ^ flip) for c in range(COLS)])
 
     chi = fold(chi, 1)
-    lad = ladder(ghi, glo, v4, 0)
+    lad = ladder(ghi, glo, zero, 0)
     chi = fold(chi, 2)
     lad = ladder(ghi, glo, opening, 1, before=lad)
     lad = ladder(ghi, glo, second, 2, before=lad)

time: 131 us -> 132 us (level)
  blocking collectives: 11.9 us -> 0 us
  starting transfers between devices: 26.2 us -> 34.3 us
  local copies, waits for them, and re-layouts: 12 us -> 15.1 us
    all_to_all x1 -> x0, blocking collectives: 11.9 us -> none  [on_device(): lax.all_to_all(packed, 'col', split_axis=0, concat_axis=0, tiled=True)]
    all_to_all x0 -> x1, starting transfers between devices: none -> 5.4 us  [on_device(): lax.all_to_all(packed, 'col', split_axis=0, concat_axis=0, tiled=True)]
    pallas_call x4 -> x5, Pallas kernels: 20.2 us -> 25.1 us  [split_integrals(): pl.pallas_call(functools.partial(split_kernel, group), out_shape=pltpu.HB...]
    pallas_call x5, Pallas kernels: 14.6 us -> 10.6 us  [ladder(): pl.pallas_call(functools.partial(ladder_kernel, group), out_shape=out_sha...]
    unnamed x32 -> x34, local copies, waits for them, and re-layouts: 4.23 us -> 6.69 us
    ppermute x3, starting transfers between devices: 3.1 us -> 5.19 us  [fold(): lax.ppermute(value, 'col', [(c, c ^ flip) for c in range(COLS)])]
    ppermute x3, waiting for transfers between devices: 2.86 us -> 0.79 us  [fold(): lax.ppermute(value, 'col', [(c, c ^ flip) for c in range(COLS)])]
    all_to_all x0 -> x1, waiting for transfers between devices: none -> 1.8 us  [on_device(): lax.all_to_all(packed, 'col', split_axis=0, concat_axis=0, tiled=True)]
  transfers between devices with their start and end apart: 16 -> 17, of which waited for: 10 -> 10; matrix products, arithmetic and copies ran while one was open for 8% -> 8% of each run, Pallas kernels for 28% -> 28%
where the time goes in v4:
time: 132 us; the launch traced here: 131 us
  Pallas kernels  48.7 us (37%)
  starting transfers between devices  34.3 us (26%)
  waiting for transfers between devices  26.9 us (20%)
  local copies, waits for them, and re-layouts  15.1 us (11%)
  other arithmetic  4.03 us (3%)
  matrix products  1.62 us (1%)
    pallas_call x5, Pallas kernels, split_integrals(): pl.pallas_call(functools.partial(split_kernel, group), out_shape=pltpu.HB...  25.1 us
    ppermute x11, starting transfers between devices, hop(): return lax.ppermute(value, 'row', row_perm(dy, dz, dc))  14.5 us
    pallas_call x5, Pallas kernels, ladder(): pl.pallas_call(functools.partial(ladder_kernel, group), out_shape=out_sha...  10.6 us
    all_to_all x1, waiting for transfers between devices, on_device(): lax.all_to_all(sending, ('row', 'col'), split_axis=0, concat_axis=0, tile...  9.9 us
    ppermute x11, waiting for transfers between devices, hop(): return lax.ppermute(value, 'row', row_perm(dy, dz, dc))  8.67 us
    unnamed x34, local copies, waits for them, and re-layouts  6.69 us
    all_to_all x1, waiting for transfers between devices, on_device(): lax.all_to_all(lad, 'col', split_axis=0, concat_axis=0, tiled=True)  5.79 us
    all_to_all x1, starting transfers between devices, on_device(): lax.all_to_all(packed, 'col', split_axis=0, concat_axis=0, tiled=True)  5.4 us
  transfers between devices with their start and end apart: 17, of which 10 were waited for; matrix products, arithmetic and copies ran while one was open for 8% of the time, Pallas kernels for 28%

profile of v4, /device:TPU:0, one launch (start us, length us, event | category | flops | bytes accessed | tf_op | source)
XLA Modules:
  0.0 131.2 jit_solution(7659694485272574809)
XLA Ops:
  0.0 1.8 %shard_map.82 = f32[8,2,25,128]{3,2,1,0:T(8,128)} custom-call(f32[2,160,160]{2,1,0:T(8,128)} %bitcast.64), custom_call_target="tpu_custom_call" | custom-call | bytes 600000 | tf_op jit(solution)/shard_map/pallas_call | solution.py:43
  1.8 1.8 %copy.24 = f32[8,2,25,128]{3,1,2,0:T(2,128)} copy(f32[8,2,25,128]{3,2,1,0:T(8,128)} %shard_map.82) | data formatting | bytes 409600 | tf_op jit(solution)/shard_map/pallas_call | solution.py:43
  3.6 5.4 %all-to-all-start = ((f32[8,2,25,128]{3,1,2,0:T(2,128)}), f32[8,2,25,128]{3,1,2,0:T(2,128)S(1)}, u32[]{:S(2)}, u32[]{:S(2)}) async-start(f32[8,2,25,128]{3,1,2,0:T(2,128)} %copy.24), calls=%async_computation | async-start | bytes 409600 | tf_op jit(solution)/shard_map/all_to_all | solution.py:298
  9.0 4.9 %shard_map.83.ready = bf16[1600,1280]{1,0:T(8,128)(2,1)} custom-call(f32[10,20,160,160]{3,2,1,0:T(8,128)} %bitcast.58), custom_call_target="tpu_custom_call" | custom-call | bytes 11534336 | tf_op jit(solution)/shard_map/pallas_call | solution.py:93
  13.9 1.8 %all-to-all-done = f32[8,2,25,128]{3,1,2,0:T(2,128)S(1)} async-done(((f32[8,2,25,128]{3,1,2,0:T(2,128)}), f32[8,2,25,128]{3,1,2,0:T(2,128)S(1)}, u32[]{:S(2)}, u32[]{:S(2)}) %all-to-all-start) | async-done | bytes 204832 | tf_op jit(solution)/shard_map/all_to_all | solution.py:298
  15.8 3.0 %collective-permute-start = (f32[25,16,128]{2,1,0:T(8,128)S(1)}, f32[25,16,128]{2,1,0:T(8,128)S(1)}, u32[]{:S(2)}, u32[]{:S(2)}) collective-permute-start(f32[25,16,128]{2,1,0:T(8,128)S(1)} %bitcast.71), channel_id=1, source_target_pairs={{64,0},{72,8},{80,16},{88,24},{96,32},{104,40},{112,48},{120,56},{... | collective-permute-start | bytes 614408 | tf_op jit(solution)/shard_map/ppermute | solution.py:304
  18.8 4.9 %shard_map.84.ready = bf16[1600,1280]{1,0:T(8,128)(2,1)} custom-call(f32[10,20,160,160]{3,2,1,0:T(8,128)} %bitcast.59), custom_call_target="tpu_custom_call" | custom-call | bytes 11534336 | tf_op jit(solution)/shard_map/pallas_call | solution.py:93
  23.8 4.1 %collective-permute-start.1 = (f32[2,25,16,128]{3,2,1,0:T(8,128)S(1)}, f32[2,25,16,128]{3,2,1,0:T(8,128)S(1)}, u32[]{:S(2)}, u32[]{:S(2)}) collective-permute-start(f32[2,25,16,128]{3,2,1,0:T(8,128)S(1)} %pad_maximum_fusion.1), channel_id=1, source_target_pairs={{16,0},{24,8},{32,16},{40,24},{48,32},{56,40},{0,48},{8,56},{80,64... | collective-permute-start | bytes 1228808 | tf_op jit(solution)/shard_map/ppermute | solution.py:304
  27.9 4.9 %shard_map.85.ready = bf16[1600,1280]{1,0:T(8,128)(2,1)} custom-call(f32[10,20,160,160]{3,2,1,0:T(8,128)} %bitcast.60), custom_call_target="tpu_custom_call" | custom-call | bytes 11534336 | tf_op jit(solution)/shard_map/pallas_call | solution.py:93
  32.8 2.2 %collective-permute-done.1 = f32[2,25,16,128]{3,2,1,0:T(8,128)S(1)} collective-permute-done((f32[2,25,16,128]{3,2,1,0:T(8,128)S(1)}, f32[2,25,16,128]{3,2,1,0:T(8,128)S(1)}, u32[]{:S(2)}, u32[]{:S(2)}) %collective-permute-start.1) | collective-permute-done | bytes 409632 | tf_op jit(solution)/shard_map/ppermute | solution.py:304
  35.0 3.4 %collective-permute-done.2 = f32[2,25,16,128]{3,2,1,0:T(8,128)S(1)} collective-permute-done((f32[2,25,16,128]{3,2,1,0:T(8,128)S(1)}, f32[2,25,16,128]{3,2,1,0:T(8,128)S(1)}, u32[]{:S(2)}, u32[]{:S(2)}) %collective-permute-start.2) | collective-permute-done | bytes 409632 | tf_op jit(solution)/shard_map/ppermute | solution.py:304
  38.8 1.8 %collective-permute-start.4 = (f32[25,16,128]{2,1,0:T(8,128)S(1)}, f32[25,16,128]{2,1,0:T(8,128)S(1)}, u32[]{:S(2)}, u32[]{:S(2)}) collective-permute-start(f32[25,16,128]{2,1,0:T(8,128)S(1)} %slice_bitcast_fusion), channel_id=1, source_target_pairs={{48,0},{56,8},{0,16},{8,24},{16,32},{24,40},{32,48},{40,56},{112,6... | collective-permute-start | bytes 614408 | tf_op jit(solution)/shard_map/ppermute | solution.py:304
  40.6 5.0 %shard_map.86.ready = bf16[1600,1280]{1,0:T(8,128)(2,1)} custom-call(f32[10,20,160,160]{3,2,1,0:T(8,128)} %bitcast.61), custom_call_target="tpu_custom_call" | custom-call | bytes 11534336 | tf_op jit(solution)/shard_map/pallas_call | solution.py:93
  46.1 5.4 %shard_map.88.ready = bf16[1600,1280]{1,0:T(8,128)(2,1)} custom-call(f32[10,20,160,160]{3,2,1,0:T(8,128)} %bitcast.62), custom_call_target="tpu_custom_call" | custom-call | bytes 11534336 | tf_op jit(solution)/shard_map/pallas_call | solution.py:93
  51.6 1.2 copy-done.12
  52.7 4.3 %shard_map.87 = (bf16[5,256,1280]{2,1,0:T(8,128)(2,1)S(1)}, bf16[5,256,640]{2,1,0:T(8,128)(2,1)S(1)}, f32[16,256]{1,0:T(8,128)S(1)}) custom-call(s32[16]{0:T(128)S(1)} %fusion.6.tbl_ref, f32[8,25,16,128]{3,2,1,0:T(8,128)} %bitcast.63, f32[8,25,16,128]{3,2,1,0:T(8,128)} %bitcast.68, f32[20,16,160]{2,1,0:T(8,128)} %bitcast.73), custom_call_target="tpu_custom_call" | custom-call | bytes 8388608 | tf_op jit(solution)/shard_map/pallas_call | solution.py:143
  57.1 0.7 collective-permute-start.6
  57.8 2.2 %copy-done.7 = bf16[1600,1280]{1,0:T(8,128)(2,1)S(1)} copy-done((bf16[1600,1280]{1,0:T(8,128)(2,1)S(1)}, bf16[1600,1280]{1,0:T(8,128)(2,1)}, u32[]{:S(2)}) %copy-start.7) | copy-done | bytes 4096024
  59.9 1.9 %shard_map.89.refs_0_ = f32[1600,256]{1,0:T(8,128)S(1)} custom-call(bf16[5,256,1280]{2,1,0:T(8,128)(2,1)S(1)} %get-tuple-element.27.ghi, bf16[5,256,640]{2,1,0:T(8,128)(2,1)S(1)} %get-tuple-element.28.glo, bf16[1600,1280]{1,0:T(8,128)(2,1)S(1)} %copy-done.7), custom_call_target="tpu_custom_call" | custom-call | flops 1572864000 | bytes 8388608 | tf_op jit(solution)/shard_map/pallas_call | solution.py:189
  62.1 1.9 %shard_map.90.refs_0_ = f32[1600,256]{1,0:T(8,128)S(1)} custom-call(bf16[5,256,1280]{2,1,0:T(8,128)(2,1)S(1)} %get-tuple-element.27.ghi, bf16[5,256,640]{2,1,0:T(8,128)(2,1)S(1)} %get-tuple-element.28.glo, bf16[1600,1280]{1,0:T(8,128)(2,1)S(1)} %copy-done.3, f32[1600,256]{1,0:T(8,128)S(1)} %shard_map.89.refs_0_), custom_call_target="tpu_custom_call" | custom-call | flops 1572864000 | bytes 8388608 | tf_op jit(solution)/shard_map/pallas_call | solution.py:189
  64.0 1.5 %collective-permute-start.7 = (f32[16,256]{1,0:T(8,128)S(1)}, f32[16,256]{1,0:T(8,128)S(1)}, u32[]{:S(2)}, u32[]{:S(2)}) collective-permute-start(f32[16,256]{1,0:T(8,128)S(1)} %add.151), channel_id=1, source_target_pairs={{0,2},{1,3},{2,0},{3,1},{4,6},{5,7},{6,4},{7,5},{8,10},{9,11},{10,... | collective-permute-start | bytes 49160 | tf_op jit(solution)/shard_map/ppermute | solution.py:336
  65.5 1.9 %shard_map.91.refs_0_ = f32[1600,256]{1,0:T(8,128)S(1)} custom-call(bf16[5,256,1280]{2,1,0:T(8,128)(2,1)S(1)} %get-tuple-element.27.ghi, bf16[5,256,640]{2,1,0:T(8,128)(2,1)S(1)} %get-tuple-element.28.glo, bf16[1600,1280]{1,0:T(8,128)(2,1)S(1)} %copy-done.4, f32[1600,256]{1,0:T(8,128)S(1)} %shard_map.90.refs_0_), custom_call_target="tpu_custom_call" | custom-call | flops 1572864000 | bytes 8388608 | tf_op jit(solution)/shard_map/pallas_call | solution.py:189
  67.8 3.0 %collective-permute-start.8 = (f32[16,256]{1,0:T(8,128)S(1)}, f32[16,256]{1,0:T(8,128)S(1)}, u32[]{:S(2)}, u32[]{:S(2)}) collective-permute-start(f32[16,256]{1,0:T(8,128)S(1)} %add.152), channel_id=1, source_target_pairs={{0,4},{1,5},{2,6},{3,7},{4,0},{5,1},{6,2},{7,3},{8,12},{9,13},{10,... | collective-permute-start | bytes 49160 | tf_op jit(solution)/shard_map/ppermute | solution.py:336
  70.8 1.9 %shard_map.92.refs_0_ = f32[1600,256]{1,0:T(8,128)S(1)} custom-call(bf16[5,256,1280]{2,1,0:T(8,128)(2,1)S(1)} %get-tuple-element.27.ghi, bf16[5,256,640]{2,1,0:T(8,128)(2,1)S(1)} %get-tuple-element.28.glo, bf16[1600,1280]{1,0:T(8,128)(2,1)S(1)} %copy-done.5, f32[1600,256]{1,0:T(8,128)S(1)} %shard_map.91.refs_0_), custom_call_target="tpu_custom_call" | custom-call | flops 1572864000 | bytes 8388608 | tf_op jit(solution)/shard_map/pallas_call | solution.py:189
  73.1 2.5 %collective-permute-start.9 = (f32[16,256]{1,0:T(8,128)S(1)}, f32[16,256]{1,0:T(8,128)S(1)}, u32[]{:S(2)}, u32[]{:S(2)}) collective-permute-start(f32[16,256]{1,0:T(8,128)S(1)} %add.153), channel_id=1, source_target_pairs={{64,0},{72,8},{80,16},{88,24},{96,32},{104,40},{112,48},{120,56},{... | collective-permute-start | bytes 49160 | tf_op jit(solution)/shard_map/ppermute | solution.py:304
  75.6 3.1 %shard_map.93 = f32[8,200,256]{2,1,0:T(8,128)} custom-call(bf16[5,256,1280]{2,1,0:T(8,128)(2,1)S(1)} %get-tuple-element.27.ghi, bf16[5,256,640]{2,1,0:T(8,128)(2,1)S(1)} %get-tuple-element.28.glo, bf16[1600,1280]{1,0:T(8,128)(2,1)S(1)} %copy-done.6, f32[1600,256]{1,0:T(8,128)S(1)} %shard_map.92.refs_0_), custom_call_target="tpu_custom_call" | custom-call | flops 1572864000 | bytes 8388608 | tf_op jit(solution)/shard_map/pallas_call | solution.py:189
  78.7 4.7 %all-to-all-start.1 = ((f32[8,200,256]{2,1,0:T(8,128)}), f32[8,200,256]{2,1,0:T(8,128)}, u32[]{:S(2)}, u32[]{:S(2)}) async-start(f32[8,200,256]{2,1,0:T(8,128)} %shard_map.93), calls=%async_computation.1 | async-start | bytes 3276800 | tf_op jit(solution)/shard_map/all_to_all | solution.py:348
  83.3 1.3 %collective-permute-start.10 = (f32[2,16,256]{2,1,0:T(8,128)S(1)}, f32[2,16,256]{2,1,0:T(8,128)}, u32[]{:S(2)}, u32[]{:S(2)}) collective-permute-start(f32[2,16,256]{2,1,0:T(8,128)S(1)} %pad_maximum_fusion.4), channel_id=1, source_target_pairs={{16,0},{24,8},{32,16},{40,24},{48,32},{56,40},{0,48},{8,56},{80,64... | collective-permute-start | bytes 98312 | tf_op jit(solution)/shard_map/ppermute | solution.py:304
  84.7 1.3 %collective-permute-start.11 = (f32[2,16,256]{2,1,0:T(8,128)S(1)}, f32[2,16,256]{2,1,0:T(8,128)}, u32[]{:S(2)}, u32[]{:S(2)}) collective-permute-start(f32[2,16,256]{2,1,0:T(8,128)S(1)} %pad_maximum_fusion.4), channel_id=1, source_target_pairs={{32,0},{40,8},{48,16},{56,24},{0,32},{8,40},{16,48},{24,56},{96,64... | collective-permute-start | bytes 98312 | tf_op jit(solution)/shard_map/ppermute | solution.py:304
  86.8 1.0 tile.10.f_ref
  88.4 1.8 %collective-permute-done.11 = f32[2,16,256]{2,1,0:T(8,128)} collective-permute-done((f32[2,16,256]{2,1,0:T(8,128)S(1)}, f32[2,16,256]{2,1,0:T(8,128)}, u32[]{:S(2)}, u32[]{:S(2)}) %collective-permute-start.11) | collective-permute-done | bytes 32800 | tf_op jit(solution)/shard_map/ppermute | solution.py:304
  90.2 1.0 collective-permute-done.12
  91.2 1.5 %fusion.18 = (f32[1,4,2,16,256]{4,3,2,1,0:T(8,128)}, f32[4,2,16,256]{3,2,1,0:T(8,128)}) fusion(f32[1,2,16,256]{3,2,1,0:T(8,128)} %bitcast.25, f32[1,2,16,256]{3,2,1,0:T(8,128)} %bitcast.24, f32[1,2,16,256]{3,2,1,0:T(8,128)} %bitcast.23, f32[1,2,16,256]{3,2,1,0:T(8,128)S(1)} %bitcast.77), kind=kLoop, calls=%fused_computation.52 | loop fusion | flops 98304 | bytes 393216 | tf_op jit(solution)/shard_map/stack | solution.py:351
  92.8 1.4 %copy-done.2 = bf16[5,256,640]{2,1,0:T(8,128)(2,1)S(1)} copy-done((bf16[5,256,640]{2,1,0:T(8,128)(2,1)S(1)}, bf16[5,256,640]{2,1,0:T(8,128)(2,1)}, u32[]{:S(2)}) %copy-start.2) | copy-done | bytes 1638424
  94.2 1.1 shard_map.94.p_ref
  95.4 0.7 copy-done.8
  96.0 2.5 %reshape.101.w_ref = f32[256,256]{1,0:T(8,128)S(1)} reshape(f32[16,16,16,16]{3,2,1,0:T(8,128)} %param.10) | data formatting | bytes 524288 | tf_op jit(solution)/shard_map/reshape | solution.py:353
  98.5 0.9 pad_maximum_fusion.2
  99.5 5.8 %all-to-all-done.1.x_ref = f32[8,200,256]{2,1,0:T(8,128)} async-done(((f32[8,200,256]{2,1,0:T(8,128)}), f32[8,200,256]{2,1,0:T(8,128)}, u32[]{:S(2)}, u32[]{:S(2)}) %all-to-all-start.1) | async-done | bytes 1638432 | tf_op jit(solution)/shard_map/all_to_all | solution.py:348
  105.2 0.9 copy-done.9
  106.2 2.9 %shard_map.95 = f32[128,4,256]{2,1,0:T(4,128)} custom-call(s32[16]{0:T(128)S(1)} %fusion.6.tbl_ref, f32[8,200,256]{2,1,0:T(8,128)} %all-to-all-done.1.x_ref, f32[16,16,256]{2,1,0:T(8,128)S(1)} %bitcast.57, f32[256,256]{1,0:T(8,128)S(1)} %reshape.101.w_ref, f32[16,256]{1,0:T(8,128)S(1)} %tile.10.f_ref, f32[200,256]{1,0:T(8,128)S(1)} %copy-done.9), custom_call_target="tpu_custom_call" | custom-call | flops 157286400 | bytes 3145728 | tf_op jit(solution)/shard_map/pallas_call | solution.py:249
  109.1 4.6 %all-to-all-start.2 = ((f32[128,4,256]{2,1,0:T(4,128)}), f32[128,4,256]{2,1,0:T(4,128)S(1)}, u32[]{:S(2)}, u32[]{:S(2)}) async-start(f32[128,4,256]{2,1,0:T(4,128)} %shard_map.95), calls=%async_computation.2 | async-start | bytes 1048576 | tf_op jit(solution)/shard_map/all_to_all | solution.py:356
  113.7 1.2 dynamic-slice_add_fusion.e_ref
  115.0 0.8 copy.30.vcol_ref
  116.1 1.2 fusion.tf_ref
  117.3 9.9 %all-to-all-done.2 = f32[128,4,256]{2,1,0:T(4,128)S(1)} async-done(((f32[128,4,256]{2,1,0:T(4,128)}), f32[128,4,256]{2,1,0:T(4,128)S(1)}, u32[]{:S(2)}, u32[]{:S(2)}) %all-to-all-start.2) | async-done | bytes 524320 | tf_op jit(solution)/shard_map/all_to_all | solution.py:356
  127.3 1.0 copy.34
  128.3 2.9 %shard_map.96 = f32[2,160,160]{2,1,0:T(8,128)} custom-call(f32[2]{0:T(128)} %dynamic-slice_add_fusion.e_ref, f32[2,2,8,16,256]{4,3,2,1,0:T(8,128)} %bitcast.66, f32[2,160,160]{2,1,0:T(8,128)} %fusion.tf_ref, f32[1,160]{1,0:T(1,128)} %bitcast.80, f32[160,1]{1,0:T(8,128)} %copy.30.vcol_ref), custom_call_target="tpu_custom_call" | custom-call | bytes 2097152 | tf_op jit(solution)/shard_map/pallas_call | solution.py:281
  (61 shorter events, 4.0 us)
Async XLA Ops:
  0.0 115.7 %copy-start = (f32[160,160]{1,0:T(8,128)S(1)}, f32[160,160]{1,0:T(8,128)}, u32[]{:S(2)}) copy-start(f32[160,160]{1,0:T(8,128)} %param.13) | copy-start | bytes 307204
  3.6 12.1 %all-to-all-start = ((f32[8,2,25,128]{3,1,2,0:T(2,128)}), f32[8,2,25,128]{3,1,2,0:T(2,128)S(1)}, u32[]{:S(2)}, u32[]{:S(2)}) async-start(f32[8,2,25,128]{3,1,2,0:T(2,128)} %copy.24), calls=%async_computation | async-start | bytes 409600 | tf_op jit(solution)/shard_map/all_to_all | solution.py:298
  15.8 7.9 %collective-permute-start = (f32[25,16,128]{2,1,0:T(8,128)S(1)}, f32[25,16,128]{2,1,0:T(8,128)S(1)}, u32[]{:S(2)}, u32[]{:S(2)}) collective-permute-start(f32[25,16,128]{2,1,0:T(8,128)S(1)} %bitcast.71), channel_id=1, source_target_pairs={{64,0},{72,8},{80,16},{88,24},{96,32},{104,40},{112,48},{120,56},{... | collective-permute-start | bytes 614408 | tf_op jit(solution)/shard_map/ppermute | solution.py:304
  23.8 11.2 %collective-permute-start.1 = (f32[2,25,16,128]{3,2,1,0:T(8,128)S(1)}, f32[2,25,16,128]{3,2,1,0:T(8,128)S(1)}, u32[]{:S(2)}, u32[]{:S(2)}) collective-permute-start(f32[2,25,16,128]{3,2,1,0:T(8,128)S(1)} %pad_maximum_fusion.1), channel_id=1, source_target_pairs={{16,0},{24,8},{32,16},{40,24},{48,32},{56,40},{0,48},{8,56},{80,64... | collective-permute-start | bytes 1228808 | tf_op jit(solution)/shard_map/ppermute | solution.py:304
  27.9 10.5 %collective-permute-start.2 = (f32[2,25,16,128]{3,2,1,0:T(8,128)S(1)}, f32[2,25,16,128]{3,2,1,0:T(8,128)S(1)}, u32[]{:S(2)}, u32[]{:S(2)}) collective-permute-start(f32[2,25,16,128]{3,2,1,0:T(8,128)S(1)} %pad_maximum_fusion.1), channel_id=1, source_target_pairs={{48,0},{56,8},{0,16},{8,24},{16,32},{24,40},{32,48},{40,56},{112,6... | collective-permute-start | bytes 1228808 | tf_op jit(solution)/shard_map/ppermute | solution.py:304
  38.4 7.2 %collective-permute-start.3 = (f32[25,16,128]{2,1,0:T(8,128)S(1)}, f32[25,16,128]{2,1,0:T(8,128)S(1)}, u32[]{:S(2)}, u32[]{:S(2)}) collective-permute-start(f32[25,16,128]{2,1,0:T(8,128)S(1)} %slice_bitcast_fusion.1), channel_id=1, source_target_pairs={{16,0},{24,8},{32,16},{40,24},{48,32},{56,40},{0,48},{8,56},{80,64... | collective-permute-start | bytes 614408 | tf_op jit(solution)/shard_map/ppermute | solution.py:304
  38.8 7.0 %collective-permute-start.4 = (f32[25,16,128]{2,1,0:T(8,128)S(1)}, f32[25,16,128]{2,1,0:T(8,128)S(1)}, u32[]{:S(2)}, u32[]{:S(2)}) collective-permute-start(f32[25,16,128]{2,1,0:T(8,128)S(1)} %slice_bitcast_fusion), channel_id=1, source_target_pairs={{48,0},{56,8},{0,16},{8,24},{16,32},{24,40},{32,48},{40,56},{112,6... | collective-permute-start | bytes 614408 | tf_op jit(solution)/shard_map/ppermute | solution.py:304
  46.0 5.5 %copy-start.10 = (f32[4,2,25,16,128]{4,3,2,1,0:T(8,128)}, f32[4,2,25,16,128]{4,3,2,1,0:T(8,128)S(1)}, u32[]{:S(2)}) copy-start(f32[4,2,25,16,128]{4,3,2,1,0:T(8,128)S(1)} %pad_maximum_fusion) | copy-start | bytes 4915204
  46.0 5.6 %collective-permute-start.5 = (f32[4,2,25,16,128]{4,3,2,1,0:T(8,128)S(1)}, f32[4,2,25,16,128]{4,3,2,1,0:T(8,128)S(1)}, u32[]{:S(2)}, u32[]{:S(2)}) collective-permute-start(f32[4,2,25,16,128]{4,3,2,1,0:T(8,128)S(1)} %pad_maximum_fusion), channel_id=1, source_target_pairs={{8,0},{0,8},{24,16},{16,24},{40,32},{32,40},{56,48},{48,56},{72,64... | collective-permute-start | bytes 4915208 | tf_op jit(solution)/shard_map/ppermute | solution.py:304
  51.6 1.2 copy-start.12
  57.1 18.5 %copy-start.1 = (bf16[5,256,640]{2,1,0:T(8,128)(2,1)}, bf16[5,256,640]{2,1,0:T(8,128)(2,1)S(1)}, u32[]{:S(2)}) copy-start(bf16[5,256,640]{2,1,0:T(8,128)(2,1)S(1)} %get-tuple-element.28.glo) | copy-start | bytes 4915204
  57.1 6.9 %collective-permute-start.6 = (f32[16,256]{1,0:T(8,128)S(1)}, f32[16,256]{1,0:T(8,128)S(1)}, u32[]{:S(2)}, u32[]{:S(2)}) collective-permute-start(f32[16,256]{1,0:T(8,128)S(1)} %get-tuple-element.33), channel_id=1, source_target_pairs={{0,1},{1,0},{2,3},{3,2},{4,5},{5,4},{6,7},{7,6},{8,9},{9,8},{10,11... | collective-permute-start | bytes 49160 | tf_op jit(solution)/shard_map/ppermute | solution.py:336
  57.8 2.2 %copy-start.7 = (bf16[1600,1280]{1,0:T(8,128)(2,1)S(1)}, bf16[1600,1280]{1,0:T(8,128)(2,1)}, u32[]{:S(2)}) copy-start(bf16[1600,1280]{1,0:T(8,128)(2,1)} %shard_map.83.ready) | copy-start | bytes 12288004
  59.9 2.2 %copy-start.3 = (bf16[1600,1280]{1,0:T(8,128)(2,1)S(1)}, bf16[1600,1280]{1,0:T(8,128)(2,1)}, u32[]{:S(2)}) copy-start(bf16[1600,1280]{1,0:T(8,128)(2,1)} %shard_map.84.ready) | copy-start | bytes 12288004
  62.1 3.4 %copy-start.4 = (bf16[1600,1280]{1,0:T(8,128)(2,1)S(1)}, bf16[1600,1280]{1,0:T(8,128)(2,1)}, u32[]{:S(2)}) copy-start(bf16[1600,1280]{1,0:T(8,128)(2,1)} %shard_map.85.ready) | copy-start | bytes 12288004
  64.0 3.8 %collective-permute-start.7 = (f32[16,256]{1,0:T(8,128)S(1)}, f32[16,256]{1,0:T(8,128)S(1)}, u32[]{:S(2)}, u32[]{:S(2)}) collective-permute-start(f32[16,256]{1,0:T(8,128)S(1)} %add.151), channel_id=1, source_target_pairs={{0,2},{1,3},{2,0},{3,1},{4,6},{5,7},{6,4},{7,5},{8,10},{9,11},{10,... | collective-permute-start | bytes 49160 | tf_op jit(solution)/shard_map/ppermute | solution.py:336
  65.5 5.2 %copy-start.5 = (bf16[1600,1280]{1,0:T(8,128)(2,1)S(1)}, bf16[1600,1280]{1,0:T(8,128)(2,1)}, u32[]{:S(2)}) copy-start(bf16[1600,1280]{1,0:T(8,128)(2,1)} %shard_map.86.ready) | copy-start | bytes 12288004
  67.8 5.2 %collective-permute-start.8 = (f32[16,256]{1,0:T(8,128)S(1)}, f32[16,256]{1,0:T(8,128)S(1)}, u32[]{:S(2)}, u32[]{:S(2)}) collective-permute-start(f32[16,256]{1,0:T(8,128)S(1)} %add.152), channel_id=1, source_target_pairs={{0,4},{1,5},{2,6},{3,7},{4,0},{5,1},{6,2},{7,3},{8,12},{9,13},{10,... | collective-permute-start | bytes 49160 | tf_op jit(solution)/shard_map/ppermute | solution.py:336
  70.8 4.8 %copy-start.6 = (bf16[1600,1280]{1,0:T(8,128)(2,1)S(1)}, bf16[1600,1280]{1,0:T(8,128)(2,1)}, u32[]{:S(2)}) copy-start(bf16[1600,1280]{1,0:T(8,128)(2,1)} %shard_map.88.ready) | copy-start | bytes 12288004
  73.1 5.6 %collective-permute-start.9 = (f32[16,256]{1,0:T(8,128)S(1)}, f32[16,256]{1,0:T(8,128)S(1)}, u32[]{:S(2)}, u32[]{:S(2)}) collective-permute-start(f32[16,256]{1,0:T(8,128)S(1)} %add.153), channel_id=1, source_target_pairs={{64,0},{72,8},{80,16},{88,24},{96,32},{104,40},{112,48},{120,56},{... | collective-permute-start | bytes 49160 | tf_op jit(solution)/shard_map/ppermute | solution.py:304
  78.6 7.5 %copy-start.14 = (f32[16,16]{1,0:T(8,128)S(1)}, f32[16,16]{1,0:T(8,128)}, u32[]{:S(2)}) copy-start(f32[16,16]{1,0:T(8,128)} %param.12) | copy-start | bytes 3076
  78.7 9.1 %copy-start.16 = (f32[16]{0:T(128)S(1)}, f32[16]{0:T(128)}, u32[]{:S(2)}) copy-start(f32[16]{0:T(128)} %param.14) | copy-start | bytes 196
  78.7 26.6 %all-to-all-start.1 = ((f32[8,200,256]{2,1,0:T(8,128)}), f32[8,200,256]{2,1,0:T(8,128)}, u32[]{:S(2)}, u32[]{:S(2)}) async-start(f32[8,200,256]{2,1,0:T(8,128)} %shard_map.93), calls=%async_computation.1 | async-start | bytes 3276800 | tf_op jit(solution)/shard_map/all_to_all | solution.py:348
  83.3 5.1 %collective-permute-start.10 = (f32[2,16,256]{2,1,0:T(8,128)S(1)}, f32[2,16,256]{2,1,0:T(8,128)}, u32[]{:S(2)}, u32[]{:S(2)}) collective-permute-start(f32[2,16,256]{2,1,0:T(8,128)S(1)} %pad_maximum_fusion.4), channel_id=1, source_target_pairs={{16,0},{24,8},{32,16},{40,24},{48,32},{56,40},{0,48},{8,56},{80,64... | collective-permute-start | bytes 98312 | tf_op jit(solution)/shard_map/ppermute | solution.py:304
  84.7 5.5 %collective-permute-start.11 = (f32[2,16,256]{2,1,0:T(8,128)S(1)}, f32[2,16,256]{2,1,0:T(8,128)}, u32[]{:S(2)}, u32[]{:S(2)}) collective-permute-start(f32[2,16,256]{2,1,0:T(8,128)S(1)} %pad_maximum_fusion.4), channel_id=1, source_target_pairs={{32,0},{40,8},{48,16},{56,24},{0,32},{8,40},{16,48},{24,56},{96,64... | collective-permute-start | bytes 98312 | tf_op jit(solution)/shard_map/ppermute | solution.py:304
  86.0 5.2 %collective-permute-start.12 = (f32[2,16,256]{2,1,0:T(8,128)S(1)}, f32[2,16,256]{2,1,0:T(8,128)}, u32[]{:S(2)}, u32[]{:S(2)}) collective-permute-start(f32[2,16,256]{2,1,0:T(8,128)S(1)} %pad_maximum_fusion.4), channel_id=1, source_target_pairs={{48,0},{56,8},{0,16},{8,24},{16,32},{24,40},{32,48},{40,56},{112,6... | collective-permute-start | bytes 98312 | tf_op jit(solution)/shard_map/ppermute | solution.py:304
  92.8 5.7 %collective-permute-start.13 = (f32[4,2,16,256]{3,2,1,0:T(8,128)}, f32[4,2,16,256]{3,2,1,0:T(8,128)}, u32[]{:S(2)}, u32[]{:S(2)}) collective-permute-start(f32[4,2,16,256]{3,2,1,0:T(8,128)} %get-tuple-element.38), channel_id=1, source_target_pairs={{8,0},{0,8},{24,16},{16,24},{40,32},{32,40},{56,48},{48,56},{72,64... | collective-permute-start | bytes 393224 | tf_op jit(solution)/shard_map/ppermute | solution.py:304
  92.8 1.4 %copy-start.2 = (bf16[5,256,640]{2,1,0:T(8,128)(2,1)S(1)}, bf16[5,256,640]{2,1,0:T(8,128)(2,1)}, u32[]{:S(2)}) copy-start(bf16[5,256,640]{2,1,0:T(8,128)(2,1)} %copy-done.1) | copy-start | bytes 4915204
  95.3 0.7 copy-start.8
  96.0 2.5 %copy-start.13 = (f32[1,4,2,16,256]{4,3,2,1,0:T(8,128)S(1)}, f32[1,4,2,16,256]{4,3,2,1,0:T(8,128)}, u32[]{:S(2)}) copy-start(f32[1,4,2,16,256]{4,3,2,1,0:T(8,128)} %get-tuple-element.37) | copy-start | bytes 393220
  105.2 0.9 copy-start.9
  106.2 8.8 %copy-start.15 = (f32[160]{0:T(256)S(1)}, f32[160]{0:T(256)}, u32[]{:S(2)}) copy-start(f32[160]{0:T(256)} %param.15) | copy-start | bytes 1924
  106.2 9.5 %copy-start.11 = (f32[1,2,160,160]{3,2,1,0:T(8,128)S(1)}, f32[1,2,160,160]{3,2,1,0:T(8,128)}, u32[]{:S(2)}) copy-start(f32[1,2,160,160]{3,2,1,0:T(8,128)} %param.8) | copy-start | bytes 614404
  109.1 18.1 %all-to-all-start.2 = ((f32[128,4,256]{2,1,0:T(4,128)}), f32[128,4,256]{2,1,0:T(4,128)S(1)}, u32[]{:S(2)}, u32[]{:S(2)}) async-start(f32[128,4,256]{2,1,0:T(4,128)} %shard_map.95), calls=%async_computation.2 | async-start | bytes 1048576 | tf_op jit(solution)/shard_map/all_to_all | solution.py:356
